TPU v7x, 32 devices: a whole 2x2x4 slice. The times are simulated.
32 devices in a mesh: tm: 8 (over y, x, core), space: 4 (over z).
Axes of the slice: x: 2, y: 2, z: 4, core: 2. Of those that a mesh axis runs over, the one named last changes fastest.
Arguments:
- initial_starts: float32 [8, 1024, 512], P('tm', None, 'space'), may hold values from -6 to 6
- source: float32 [8, 1024, 512], P('tm', None, 'space'), may hold values from -12 to 12
- region: int32 [1024, 512], P(None, 'space'), may hold values from 0 to 7
- base_reluctivity: float32 [8], replicated, may hold values from 0.4 to 1
- saturation: float32 [8], replicated, may hold values from 0.2 to 1
- mobility: float32 [8], replicated, may hold values from 0.01 to 0.12
Outputs:
- final_starts: float32 [8, 1024, 512], P('tm', None, 'space')
- fine_ends: float32 [8, 1024, 512], P('tm', None, 'space')
All inputs are finite; a program needn't handle non-finite values.
Results may differ from a plain program's by a relative error of at most 0.00002.
Values sent between devices are 32-bit elements; how exact they have to be, the bound alone decides.
No kernel may reach another device: no remote copies, remote signals or barrier semaphores. Data moves between devices by JAX's collectives and lax.ppermute only.
A program may use at most 64 MiB of HBM per device.

v0:
```python
import jax
import jax.numpy as jnp
from jax import lax
from jax.sharding import PartitionSpec as P

STEPS = 3
ITERS = 2


def with_halo(cells, sides, width):
    for axis, dim in sides:
        count = lax.axis_size(axis)
        head = lax.slice_in_dim(cells, 0, width, axis=dim)
        tail = lax.slice_in_dim(cells, cells.shape[dim] - width, cells.shape[dim], axis=dim)
        cells = jnp.concatenate(
            [
                lax.ppermute(tail, axis, [(i, (i + 1) % count) for i in range(count)]),
                cells,
                lax.ppermute(head, axis, [((i + 1) % count, i) for i in range(count)]),
            ],
            axis=dim,
        )
    return cells


def shifted(value, axis, steps):
    count = lax.axis_size(axis)
    pairs = [(source, (source + steps) % count) for source in range(count)]
    return lax.ppermute(value, axis, pairs)


def shifted_2(value, axis, steps):
    count = lax.axis_size(axis)
    leading, last = (max(0, -steps), min(count, count - steps))
    return lax.ppermute(value, axis, [(source, source + steps) for source in range(leading, last)])


def lookup(region, region_table):
    region_ids = jnp.arange(region_table.shape[0], dtype=jnp.int32)
    picked = jnp.where(
        region[None] == region_ids[:, None, None], region_table[:, None, None], jnp.float32(0.0)
    )
    return jnp.sum(picked, axis=0)


def advance(potential, base_nu, satur_rate, mobile, driver):
    padded = jnp.pad(potential, ((1, 1), (0, 0)))
    radial_b = (padded[2:, 1:-1] - padded[:-2, 1:-1]) * 0.5
    angle_b = (potential[:, 2:] - potential[:, :-2]) * 0.5
    flux_sq = radial_b * radial_b + angle_b * angle_b
    reluct = base_nu * (1.0 + satur_rate * flux_sq / (1.0 + flux_sq))
    reluct_pad = jnp.pad(reluct, ((1, 1), (0, 0)), mode="edge")
    reluct_mid = reluct[:, 1:-1]
    centre = potential[:, 2:-2]
    east_flux = 0.5 * (reluct_mid + reluct[:, 2:]) * (potential[:, 3:-1] - centre)
    west_flux = 0.5 * (reluct_mid + reluct[:, :-2]) * (potential[:, 1:-3] - centre)
    north_flux = 0.5 * (reluct_mid + reluct_pad[2:, 1:-1]) * (padded[2:, 2:-2] - centre)
    south_flux = 0.5 * (reluct_mid + reluct_pad[:-2, 1:-1]) * (padded[:-2, 2:-2] - centre)
    return centre + mobile * (east_flux + west_flux + north_flux + south_flux + driver)


def local(initial_starts, source, region, base_reluctivity, saturation, mobility):
    potential = initial_starts[0]
    driver = source[0]
    base_nu = lookup(region, base_reluctivity)
    satur_rate = lookup(region, saturation)
    mobile = lookup(region, mobility)
    coarse_gain = 1.0 / (1.0 + 12.0 * mobile * base_nu)
    slot_index = lax.axis_index("tm")
    loop_size = lax.axis_size("tm")
    is_first = slot_index == 0
    is_last = slot_index == loop_size - 1
    slopes = jnp.where(is_first, jnp.float32(0.0), coarse_gain)
    margin_coefs = with_halo(
        jnp.stack([base_nu, satur_rate, mobile, driver]), (("space", 2),), 2 * STEPS - 1
    )
    full_width = margin_coefs.shape[2]
    fine_ends = potential
    for iteration in range(ITERS):
        extended = with_halo(potential, (("space", 1),), 2 * STEPS)
        for segment in range(STEPS):
            reach_now = 2 * STEPS - 2 * segment
            outer_cut = 2 * STEPS - reach_now
            inner_cut = outer_cut + 1
            extended = advance(
                extended,
                margin_coefs[0][:, outer_cut : full_width - outer_cut],
                margin_coefs[1][:, outer_cut : full_width - outer_cut],
                margin_coefs[2][:, inner_cut : full_width - inner_cut],
                margin_coefs[3][:, inner_cut : full_width - inner_cut],
            )
        fine_ends = extended
        corrected = jnp.where(is_last, fine_ends, fine_ends - coarse_gain * potential)
        carried = shifted(corrected, "tm", 1)

        def relay_step(turn_no, chained):
            return slopes * shifted_2(chained, "tm", 1) + carried

        potential = lax.fori_loop(0, loop_size - 1, relay_step, carried)
    return (potential[None], fine_ends[None])


def solution(mesh):
    placed = (P("tm", None, "space"), P("tm", None, "space"), P(None, "space"), P(), P(), P())
    return jax.shard_map(
        local,
        mesh=mesh,
        in_specs=placed,
        out_specs=(P("tm", None, "space"), P("tm", None, "space")),
        check_vma=False,
    )
```

profile of v0, /device:TPU:12, one launch (start us, length us, event | category | flops | bytes accessed | tf_op | source)
XLA Modules:
  0.0 285.2 jit_solution(1569271085826305372)
XLA Ops:
  15.9 12.0 %collective-permute-done.2 = f32[1024,6]{1,0:T(8,128)S(1)} collective-permute-done((f32[1024,6]{1,0:T(8,128)}, f32[1024,6]{1,0:T(8,128)S(1)}, u32[]{:S(2)}, u32[]{:S(2)}) %collective-permute-start.2) | collective-permute-done | bytes 24608 | tf_op jit(solution)/shard_map/ppermute | solution.py:17
  35.8 5.0 %pad_maximum_fusion = f32[4,1024,138]{2,1,0:T(8,128)S(1)} fusion(f32[4,1024,5]{2,1,0:T(8,128)} %copy.29, f32[1,1024,128]{2,1,0:T(8,128)S(1)} %copy-done.16, f32[1,1024,128]{2,1,0:T(8,128)S(1)} %bitcast.26, f32[1,1024,128]{2,1,0:T(8,128)S(1)} %bitcast.30, f32[1,1024,128]{2,1,0:T(8,128)S(1)} %bitcast.24, f32[4,1024,5]{2,1,0:T(8,128)} %copy.28), kind=kLoop, calls=%fused_computation.2 | loop fusion | flops 2826240 | bytes 4521984 | tf_op jit(solution)/shard_map/concatenate | solution.py:15
  43.8 3.1 %fusion.69 = f32[1024,136]{1,0:T(8,128)S(1)} fusion(f32[1024,138]{1,0:T(8,128)S(1)} %add_multiply_fusion.5, f32[1,138]{1,0:T(1,128)S(1)} %get-tuple-element.98, f32[1,138]{1,0:T(1,128)S(1)} %get-tuple-element.97, f32[1024,140]{1,0:T(8,128)S(1)} %pad_maximum_fusion.10, f32[1024,138]{1,0:T(8,128)S(1)} %get-tuple-element.80, f32[1024,138]{1,0:T(8,128)S(1)} %get-tuple-element.82), kind=kLoop, calls=%fused_computation.102 | loop fusion | flops 3342336 | bytes 11044864 | tf_op jit(solution)/shard_map/add | solution.py:59
  55.2 9.7 %collective-permute-done.6 = f32[1024,128]{1,0:T(8,128)S(1)} collective-permute-done((f32[1024,128]{1,0:T(8,128)}, f32[1024,128]{1,0:T(8,128)S(1)}, u32[]{:S(2)}, u32[]{:S(2)}) %collective-permute-start.6) | collective-permute-done | bytes 524320 | tf_op jit(solution)/shard_map/ppermute | solution.py:29
  65.7 95.2 %while.20 = (s32[]{:T(128)}, f32[1024,128]{1,0:T(8,128)}, f32[1024,128]{1,0:T(8,128)S(1)}, f32[1024,128]{1,0:T(8,128)S(1)}, s32[]{:T(128)}) while((s32[]{:T(128)}, f32[1024,128]{1,0:T(8,128)}, f32[1024,128]{1,0:T(8,128)S(1)}, f32[1024,128]{1,0:T(8,128)S(1)}, s32[]{:T(128)}) %tuple.54), condition=%wide.region_4.5_spmd, body=%wide.region_3.4_spmd.sunk | while | flops 262146 | bytes 4194405 | solution.py:99
  67.6 9.8 %collective-permute-done = f32[1024,128]{1,0:T(8,128)} collective-permute-done((f32[1024,128]{1,0:T(8,128)}, f32[1024,128]{1,0:T(8,128)}, u32[]{:S(2)}, u32[]{:S(2)}) %collective-permute-start) | collective-permute-done | bytes 524320 | tf_op jit(solution)/shard_map/while/body/eval_jaxpr/ppermute | solution.py:35
  81.3 9.8 %collective-permute-done = f32[1024,128]{1,0:T(8,128)} collective-permute-done((f32[1024,128]{1,0:T(8,128)}, f32[1024,128]{1,0:T(8,128)}, u32[]{:S(2)}, u32[]{:S(2)}) %collective-permute-start) | collective-permute-done | bytes 524320 | tf_op jit(solution)/shard_map/while/body/eval_jaxpr/ppermute | solution.py:35
  94.9 9.8 %collective-permute-done = f32[1024,128]{1,0:T(8,128)} collective-permute-done((f32[1024,128]{1,0:T(8,128)}, f32[1024,128]{1,0:T(8,128)}, u32[]{:S(2)}, u32[]{:S(2)}) %collective-permute-start) | collective-permute-done | bytes 524320 | tf_op jit(solution)/shard_map/while/body/eval_jaxpr/ppermute | solution.py:35
  108.5 9.8 %collective-permute-done = f32[1024,128]{1,0:T(8,128)} collective-permute-done((f32[1024,128]{1,0:T(8,128)}, f32[1024,128]{1,0:T(8,128)}, u32[]{:S(2)}, u32[]{:S(2)}) %collective-permute-start) | collective-permute-done | bytes 524320 | tf_op jit(solution)/shard_map/while/body/eval_jaxpr/ppermute | solution.py:35
  122.1 9.8 %collective-permute-done = f32[1024,128]{1,0:T(8,128)} collective-permute-done((f32[1024,128]{1,0:T(8,128)}, f32[1024,128]{1,0:T(8,128)}, u32[]{:S(2)}, u32[]{:S(2)}) %collective-permute-start) | collective-permute-done | bytes 524320 | tf_op jit(solution)/shard_map/while/body/eval_jaxpr/ppermute | solution.py:35
  135.7 9.8 %collective-permute-done = f32[1024,128]{1,0:T(8,128)} collective-permute-done((f32[1024,128]{1,0:T(8,128)}, f32[1024,128]{1,0:T(8,128)}, u32[]{:S(2)}, u32[]{:S(2)}) %collective-permute-start) | collective-permute-done | bytes 524320 | tf_op jit(solution)/shard_map/while/body/eval_jaxpr/ppermute | solution.py:35
  149.3 9.8 %collective-permute-done = f32[1024,128]{1,0:T(8,128)} collective-permute-done((f32[1024,128]{1,0:T(8,128)}, f32[1024,128]{1,0:T(8,128)}, u32[]{:S(2)}, u32[]{:S(2)}) %collective-permute-start) | collective-permute-done | bytes 524320 | tf_op jit(solution)/shard_map/while/body/eval_jaxpr/ppermute | solution.py:35
  164.6 9.9 %collective-permute-done.7 = f32[1024,6]{1,0:T(8,128)S(1)} collective-permute-done((f32[1024,6]{1,0:T(8,128)S(1)}, f32[1024,6]{1,0:T(8,128)S(1)}, u32[]{:S(2)}, u32[]{:S(2)}) %collective-permute-start.7) | collective-permute-done | bytes 24608 | tf_op jit(solution)/shard_map/ppermute | solution.py:17
  174.5 6.9 %collective-permute-done.8 = f32[1024,6]{1,0:T(8,128)S(1)} collective-permute-done((f32[1024,6]{1,0:T(8,128)S(1)}, f32[1024,6]{1,0:T(8,128)S(1)}, u32[]{:S(2)}, u32[]{:S(2)}) %collective-permute-start.8) | collective-permute-done | bytes 24608 | tf_op jit(solution)/shard_map/ppermute | solution.py:19
  182.9 3.1 %fusion.28 = f32[1024,136]{1,0:T(8,128)S(1)} fusion(f32[1024,138]{1,0:T(8,128)S(1)} %add_multiply_fusion.2, f32[1,138]{1,0:T(1,128)S(1)} %get-tuple-element.90, f32[1,138]{1,0:T(1,128)S(1)} %get-tuple-element.89, f32[1024,140]{1,0:T(8,128)S(1)} %pad_maximum_fusion.11, f32[1024,138]{1,0:T(8,128)S(1)} %get-tuple-element.80, f32[1024,138]{1,0:T(8,128)S(1)} %get-tuple-element.82), kind=kLoop, calls=%fused_computation.45 | loop fusion | flops 3342336 | bytes 11044864 | tf_op jit(solution)/shard_map/add | solution.py:59
  194.3 9.5 %collective-permute-done.9 = f32[1024,128]{1,0:T(8,128)S(1)} collective-permute-done((f32[1024,128]{1,0:T(8,128)S(1)}, f32[1024,128]{1,0:T(8,128)S(1)}, u32[]{:S(2)}, u32[]{:S(2)}) %collective-permute-start.9) | collective-permute-done | bytes 524320 | tf_op jit(solution)/shard_map/ppermute | solution.py:29
  203.9 80.5 %while.21 = (s32[]{:T(128)}, f32[1024,128]{1,0:T(8,128)S(1)}, f32[1024,128]{1,0:T(8,128)S(1)}, f32[1024,128]{1,0:T(8,128)S(1)}, s32[]{:T(128)}) while((s32[]{:T(128)}, f32[1024,128]{1,0:T(8,128)S(1)}, f32[1024,128]{1,0:T(8,128)S(1)}, f32[1024,128]{1,0:T(8,128)S(1)}, s32[]{:T(128)}) %tuple.60), condition=%wide.region_6.7_spmd, body=%wide.region_5.6_spmd.sunk | while | flops 262146 | bytes 4194405 | solution.py:99
  205.8 9.5 %collective-permute-done.1 = f32[1024,128]{1,0:T(8,128)S(1)} collective-permute-done((f32[1024,128]{1,0:T(8,128)S(1)}, f32[1024,128]{1,0:T(8,128)S(1)}, u32[]{:S(2)}, u32[]{:S(2)}) %collective-permute-start.1) | collective-permute-done | bytes 524320 | tf_op jit(solution)/shard_map/while/body/eval_jaxpr/ppermute | solution.py:35
  217.3 9.5 %collective-permute-done.1 = f32[1024,128]{1,0:T(8,128)S(1)} collective-permute-done((f32[1024,128]{1,0:T(8,128)S(1)}, f32[1024,128]{1,0:T(8,128)S(1)}, u32[]{:S(2)}, u32[]{:S(2)}) %collective-permute-start.1) | collective-permute-done | bytes 524320 | tf_op jit(solution)/shard_map/while/body/eval_jaxpr/ppermute | solution.py:35
  228.8 9.5 %collective-permute-done.1 = f32[1024,128]{1,0:T(8,128)S(1)} collective-permute-done((f32[1024,128]{1,0:T(8,128)S(1)}, f32[1024,128]{1,0:T(8,128)S(1)}, u32[]{:S(2)}, u32[]{:S(2)}) %collective-permute-start.1) | collective-permute-done | bytes 524320 | tf_op jit(solution)/shard_map/while/body/eval_jaxpr/ppermute | solution.py:35
  240.3 9.5 %collective-permute-done.1 = f32[1024,128]{1,0:T(8,128)S(1)} collective-permute-done((f32[1024,128]{1,0:T(8,128)S(1)}, f32[1024,128]{1,0:T(8,128)S(1)}, u32[]{:S(2)}, u32[]{:S(2)}) %collective-permute-start.1) | collective-permute-done | bytes 524320 | tf_op jit(solution)/shard_map/while/body/eval_jaxpr/ppermute | solution.py:35
  251.8 9.5 %collective-permute-done.1 = f32[1024,128]{1,0:T(8,128)S(1)} collective-permute-done((f32[1024,128]{1,0:T(8,128)S(1)}, f32[1024,128]{1,0:T(8,128)S(1)}, u32[]{:S(2)}, u32[]{:S(2)}) %collective-permute-start.1) | collective-permute-done | bytes 524320 | tf_op jit(solution)/shard_map/while/body/eval_jaxpr/ppermute | solution.py:35
  263.3 9.5 %collective-permute-done.1 = f32[1024,128]{1,0:T(8,128)S(1)} collective-permute-done((f32[1024,128]{1,0:T(8,128)S(1)}, f32[1024,128]{1,0:T(8,128)S(1)}, u32[]{:S(2)}, u32[]{:S(2)}) %collective-permute-start.1) | collective-permute-done | bytes 524320 | tf_op jit(solution)/shard_map/while/body/eval_jaxpr/ppermute | solution.py:35
  274.8 9.5 %collective-permute-done.1 = f32[1024,128]{1,0:T(8,128)S(1)} collective-permute-done((f32[1024,128]{1,0:T(8,128)S(1)}, f32[1024,128]{1,0:T(8,128)S(1)}, u32[]{:S(2)}, u32[]{:S(2)}) %collective-permute-start.1) | collective-permute-done | bytes 524320 | tf_op jit(solution)/shard_map/while/body/eval_jaxpr/ppermute | solution.py:35
  (115 shorter events, 89.8 us)
Async XLA Ops:
  3.1 24.9 %collective-permute-start.2 = (f32[1024,6]{1,0:T(8,128)}, f32[1024,6]{1,0:T(8,128)S(1)}, u32[]{:S(2)}, u32[]{:S(2)}) collective-permute-start(f32[1024,6]{1,0:T(8,128)} %get-tuple-element.101), channel_id=1, source_target_pairs={{0,1},{1,2},{2,3},{3,0},{4,5},{5,6},{6,7},{7,4},{8,9},{9,10},{10,1... | collective-permute-start | bytes 73736 | tf_op jit(solution)/shard_map/ppermute | solution.py:17
  4.7 25.5 %collective-permute-start.3 = (f32[1024,6]{1,0:T(8,128)}, f32[1024,6]{1,0:T(8,128)}, u32[]{:S(2)}, u32[]{:S(2)}) collective-permute-start(f32[1024,6]{1,0:T(8,128)} %get-tuple-element.102), channel_id=1, source_target_pairs={{1,0},{2,1},{3,2},{0,3},{5,4},{6,5},{7,6},{4,7},{9,8},{10,9},{11,1... | collective-permute-start | bytes 73736 | tf_op jit(solution)/shard_map/ppermute | solution.py:19
  6.2 29.6 %copy-start.7 = (f32[1024,128]{1,0:T(8,128)}, f32[1024,128]{1,0:T(8,128)S(1)}, u32[]{:S(2)}) copy-start(f32[1024,128]{1,0:T(8,128)S(1)} %get-tuple-element.58) | copy-start | bytes 1572868
  6.2 29.6 %copy-start.10 = (f32[1024,128]{1,0:T(8,128)}, f32[1024,128]{1,0:T(8,128)S(1)}, u32[]{:S(2)}) copy-start(f32[1024,128]{1,0:T(8,128)S(1)} %get-tuple-element.59) | copy-start | bytes 1572868
  11.3 20.5 %collective-permute-start.4 = (f32[4,1024,5]{1,0,2:T(4,128)S(1)}, f32[4,1024,5]{1,0,2:T(4,128)S(1)}, u32[]{:S(2)}, u32[]{:S(2)}) collective-permute-start(f32[4,1024,5]{1,0,2:T(4,128)S(1)} %copy.26), channel_id=1, source_target_pairs={{0,1},{1,2},{2,3},{3,0},{4,5},{5,6},{6,7},{7,4},{8,9},{9,10},{10,1... | collective-permute-start | bytes 245768 | tf_op jit(solution)/shard_map/ppermute | solution.py:17
  15.2 18.6 %collective-permute-start.5 = (f32[4,1024,5]{1,0,2:T(4,128)S(1)}, f32[4,1024,5]{1,0,2:T(4,128)S(1)}, u32[]{:S(2)}, u32[]{:S(2)}) collective-permute-start(f32[4,1024,5]{1,0,2:T(4,128)S(1)} %copy.27), channel_id=1, source_target_pairs={{1,0},{2,1},{3,2},{0,3},{5,4},{6,5},{7,6},{4,7},{9,8},{10,9},{11,1... | collective-permute-start | bytes 245768 | tf_op jit(solution)/shard_map/ppermute | solution.py:19
  55.2 9.7 %collective-permute-start.6 = (f32[1024,128]{1,0:T(8,128)}, f32[1024,128]{1,0:T(8,128)S(1)}, u32[]{:S(2)}, u32[]{:S(2)}) collective-permute-start(f32[1024,128]{1,0:T(8,128)} %get-tuple-element.92), channel_id=1, source_target_pairs={{0,4},{4,8},{8,12},{12,16},{16,20},{20,24},{24,28},{28,0},{1,5},{5... | collective-permute-start | bytes 1572872 | tf_op jit(solution)/shard_map/ppermute | solution.py:29
  65.7 11.7 %collective-permute-start = (f32[1024,128]{1,0:T(8,128)}, f32[1024,128]{1,0:T(8,128)}, u32[]{:S(2)}, u32[]{:S(2)}) collective-permute-start(f32[1024,128]{1,0:T(8,128)} %get-tuple-element.159), channel_id=1, source_target_pairs={{0,4},{4,8},{8,12},{12,16},{16,20},{20,24},{24,28},{1,5},{5,9},{9,... | collective-permute-start | bytes 1572872 | tf_op jit(solution)/shard_map/while/body/eval_jaxpr/ppermute | solution.py:35
  79.3 11.7 %collective-permute-start = (f32[1024,128]{1,0:T(8,128)}, f32[1024,128]{1,0:T(8,128)}, u32[]{:S(2)}, u32[]{:S(2)}) collective-permute-start(f32[1024,128]{1,0:T(8,128)} %get-tuple-element.159), channel_id=1, source_target_pairs={{0,4},{4,8},{8,12},{12,16},{16,20},{20,24},{24,28},{1,5},{5,9},{9,... | collective-permute-start | bytes 1572872 | tf_op jit(solution)/shard_map/while/body/eval_jaxpr/ppermute | solution.py:35
  92.9 11.7 %collective-permute-start = (f32[1024,128]{1,0:T(8,128)}, f32[1024,128]{1,0:T(8,128)}, u32[]{:S(2)}, u32[]{:S(2)}) collective-permute-start(f32[1024,128]{1,0:T(8,128)} %get-tuple-element.159), channel_id=1, source_target_pairs={{0,4},{4,8},{8,12},{12,16},{16,20},{20,24},{24,28},{1,5},{5,9},{9,... | collective-permute-start | bytes 1572872 | tf_op jit(solution)/shard_map/while/body/eval_jaxpr/ppermute | solution.py:35
  106.5 11.7 %collective-permute-start = (f32[1024,128]{1,0:T(8,128)}, f32[1024,128]{1,0:T(8,128)}, u32[]{:S(2)}, u32[]{:S(2)}) collective-permute-start(f32[1024,128]{1,0:T(8,128)} %get-tuple-element.159), channel_id=1, source_target_pairs={{0,4},{4,8},{8,12},{12,16},{16,20},{20,24},{24,28},{1,5},{5,9},{9,... | collective-permute-start | bytes 1572872 | tf_op jit(solution)/shard_map/while/body/eval_jaxpr/ppermute | solution.py:35
  120.1 11.7 %collective-permute-start = (f32[1024,128]{1,0:T(8,128)}, f32[1024,128]{1,0:T(8,128)}, u32[]{:S(2)}, u32[]{:S(2)}) collective-permute-start(f32[1024,128]{1,0:T(8,128)} %get-tuple-element.159), channel_id=1, source_target_pairs={{0,4},{4,8},{8,12},{12,16},{16,20},{20,24},{24,28},{1,5},{5,9},{9,... | collective-permute-start | bytes 1572872 | tf_op jit(solution)/shard_map/while/body/eval_jaxpr/ppermute | solution.py:35
  133.7 11.7 %collective-permute-start = (f32[1024,128]{1,0:T(8,128)}, f32[1024,128]{1,0:T(8,128)}, u32[]{:S(2)}, u32[]{:S(2)}) collective-permute-start(f32[1024,128]{1,0:T(8,128)} %get-tuple-element.159), channel_id=1, source_target_pairs={{0,4},{4,8},{8,12},{12,16},{16,20},{20,24},{24,28},{1,5},{5,9},{9,... | collective-permute-start | bytes 1572872 | tf_op jit(solution)/shard_map/while/body/eval_jaxpr/ppermute | solution.py:35
  147.3 11.7 %collective-permute-start = (f32[1024,128]{1,0:T(8,128)}, f32[1024,128]{1,0:T(8,128)}, u32[]{:S(2)}, u32[]{:S(2)}) collective-permute-start(f32[1024,128]{1,0:T(8,128)} %get-tuple-element.159), channel_id=1, source_target_pairs={{0,4},{4,8},{8,12},{12,16},{16,20},{20,24},{24,28},{1,5},{5,9},{9,... | collective-permute-start | bytes 1572872 | tf_op jit(solution)/shard_map/while/body/eval_jaxpr/ppermute | solution.py:35
  162.5 12.0 %collective-permute-start.7 = (f32[1024,6]{1,0:T(8,128)S(1)}, f32[1024,6]{1,0:T(8,128)S(1)}, u32[]{:S(2)}, u32[]{:S(2)}) collective-permute-start(f32[1024,6]{1,0:T(8,128)S(1)} %get-tuple-element.99), channel_id=1, source_target_pairs={{0,1},{1,2},{2,3},{3,0},{4,5},{5,6},{6,7},{7,4},{8,9},{9,10},{10,1... | collective-permute-start | bytes 73736 | tf_op jit(solution)/shard_map/ppermute | solution.py:17
  164.2 17.2 %collective-permute-start.8 = (f32[1024,6]{1,0:T(8,128)S(1)}, f32[1024,6]{1,0:T(8,128)S(1)}, u32[]{:S(2)}, u32[]{:S(2)}) collective-permute-start(f32[1024,6]{1,0:T(8,128)S(1)} %get-tuple-element.100), channel_id=1, source_target_pairs={{1,0},{2,1},{3,2},{0,3},{5,4},{6,5},{7,6},{4,7},{9,8},{10,9},{11,1... | collective-permute-start | bytes 73736 | tf_op jit(solution)/shard_map/ppermute | solution.py:19
  194.3 9.5 %collective-permute-start.9 = (f32[1024,128]{1,0:T(8,128)S(1)}, f32[1024,128]{1,0:T(8,128)S(1)}, u32[]{:S(2)}, u32[]{:S(2)}) collective-permute-start(f32[1024,128]{1,0:T(8,128)S(1)} %get-tuple-element.77), channel_id=1, source_target_pairs={{0,4},{4,8},{8,12},{12,16},{16,20},{20,24},{24,28},{28,0},{1,5},{5... | collective-permute-start | bytes 1572872 | tf_op jit(solution)/shard_map/ppermute | solution.py:29
  203.9 11.4 %collective-permute-start.1 = (f32[1024,128]{1,0:T(8,128)S(1)}, f32[1024,128]{1,0:T(8,128)S(1)}, u32[]{:S(2)}, u32[]{:S(2)}) collective-permute-start(f32[1024,128]{1,0:T(8,128)S(1)} %get-tuple-element.174), channel_id=1, source_target_pairs={{0,4},{4,8},{8,12},{12,16},{16,20},{20,24},{24,28},{1,5},{5,9},{9,... | collective-permute-start | bytes 1572872 | tf_op jit(solution)/shard_map/while/body/eval_jaxpr/ppermute | solution.py:35
  215.4 11.4 %collective-permute-start.1 = (f32[1024,128]{1,0:T(8,128)S(1)}, f32[1024,128]{1,0:T(8,128)S(1)}, u32[]{:S(2)}, u32[]{:S(2)}) collective-permute-start(f32[1024,128]{1,0:T(8,128)S(1)} %get-tuple-element.174), channel_id=1, source_target_pairs={{0,4},{4,8},{8,12},{12,16},{16,20},{20,24},{24,28},{1,5},{5,9},{9,... | collective-permute-start | bytes 1572872 | tf_op jit(solution)/shard_map/while/body/eval_jaxpr/ppermute | solution.py:35
  226.9 11.4 %collective-permute-start.1 = (f32[1024,128]{1,0:T(8,128)S(1)}, f32[1024,128]{1,0:T(8,128)S(1)}, u32[]{:S(2)}, u32[]{:S(2)}) collective-permute-start(f32[1024,128]{1,0:T(8,128)S(1)} %get-tuple-element.174), channel_id=1, source_target_pairs={{0,4},{4,8},{8,12},{12,16},{16,20},{20,24},{24,28},{1,5},{5,9},{9,... | collective-permute-start | bytes 1572872 | tf_op jit(solution)/shard_map/while/body/eval_jaxpr/ppermute | solution.py:35
  238.4 11.4 %collective-permute-start.1 = (f32[1024,128]{1,0:T(8,128)S(1)}, f32[1024,128]{1,0:T(8,128)S(1)}, u32[]{:S(2)}, u32[]{:S(2)}) collective-permute-start(f32[1024,128]{1,0:T(8,128)S(1)} %get-tuple-element.174), channel_id=1, source_target_pairs={{0,4},{4,8},{8,12},{12,16},{16,20},{20,24},{24,28},{1,5},{5,9},{9,... | collective-permute-start | bytes 1572872 | tf_op jit(solution)/shard_map/while/body/eval_jaxpr/ppermute | solution.py:35
  249.9 11.4 %collective-permute-start.1 = (f32[1024,128]{1,0:T(8,128)S(1)}, f32[1024,128]{1,0:T(8,128)S(1)}, u32[]{:S(2)}, u32[]{:S(2)}) collective-permute-start(f32[1024,128]{1,0:T(8,128)S(1)} %get-tuple-element.174), channel_id=1, source_target_pairs={{0,4},{4,8},{8,12},{12,16},{16,20},{20,24},{24,28},{1,5},{5,9},{9,... | collective-permute-start | bytes 1572872 | tf_op jit(solution)/shard_map/while/body/eval_jaxpr/ppermute | solution.py:35
  261.4 11.4 %collective-permute-start.1 = (f32[1024,128]{1,0:T(8,128)S(1)}, f32[1024,128]{1,0:T(8,128)S(1)}, u32[]{:S(2)}, u32[]{:S(2)}) collective-permute-start(f32[1024,128]{1,0:T(8,128)S(1)} %get-tuple-element.174), channel_id=1, source_target_pairs={{0,4},{4,8},{8,12},{12,16},{16,20},{20,24},{24,28},{1,5},{5,9},{9,... | collective-permute-start | bytes 1572872 | tf_op jit(solution)/shard_map/while/body/eval_jaxpr/ppermute | solution.py:35
  272.9 11.4 %collective-permute-start.1 = (f32[1024,128]{1,0:T(8,128)S(1)}, f32[1024,128]{1,0:T(8,128)S(1)}, u32[]{:S(2)}, u32[]{:S(2)}) collective-permute-start(f32[1024,128]{1,0:T(8,128)S(1)} %get-tuple-element.174), channel_id=1, source_target_pairs={{0,4},{4,8},{8,12},{12,16},{16,20},{20,24},{24,28},{1,5},{5,9},{9,... | collective-permute-start | bytes 1572872 | tf_op jit(solution)/shard_map/while/body/eval_jaxpr/ppermute | solution.py:35
  (21 other events, 124.2 us)
where the time goes:
time: 286 us; the launch traced here: 285 us
  waiting for transfers between devices  184 us (64%)
  other arithmetic  46.7 us (16%)
  starting transfers between devices  33.3 us (12%)
  local copies, waits for them, and re-layouts  19.6 us (7%)
    ppermute x14, waiting for transfers between devices, shifted_2(): lax.ppermute(value, axis, [(source, source + steps) for source in range(l...  135 us
    ppermute x14, starting transfers between devices, shifted_2(): lax.ppermute(value, axis, [(source, source + steps) for source in range(l...  26.8 us
    ppermute x3, waiting for transfers between devices, with_halo(): lax.ppermute(tail, axis, [(i, (i + 1) % count) for i in range(count)])  21.9 us
    ppermute x2, waiting for transfers between devices, shifted(): return lax.ppermute(value, axis, pairs)  19.2 us
    add x14, other arithmetic, relay_step(): return slopes * shifted_2(chained, 'tm', 1) + carried  13.8 us
    add x4, other arithmetic, advance(): centre + mobile * (east_flux + west_flux + north_flux + south_flux + driver)  12.3 us
    slice x4, local copies, waits for them, and re-layouts, with_halo(): lax.slice_in_dim(cells, cells.shape[dim] - width, cells.shape[dim], axis=...  8.89 us
    ppermute x3, waiting for transfers between devices, with_halo(): lax.ppermute(head, axis, [((i + 1) % count, i) for i in range(count)])  8.33 us
  transfers between devices with their start and end apart: 22, of which 20 were waited for; matrix products, arithmetic and copies ran while one was open for 4% of the time, Pallas kernels for 0%

commit v1 on v0

v1 whole, which is shorter than its diff:
```python
import functools

import jax
import jax.numpy as jnp
import numpy as np
from jax import lax
from jax.experimental import pallas as pl
from jax.experimental.pallas import tpu as pltpu
from jax.sharding import PartitionSpec as P

STEPS = 3
ITERS = 2
HALO = 2 * STEPS * ITERS
REACH = 2 * STEPS
PAD = 8
CHUNK = 48
FOLD = 8
VMEM = pl.BlockSpec(memory_space=pltpu.VMEM)
SMEM = pl.BlockSpec(memory_space=pltpu.SMEM)
PARAMS = pltpu.CompilerParams(vmem_limit_bytes=24 * 1024 * 1024)


def lanes_of(rows, lanes):
    return lax.broadcasted_iota(jnp.int32, (rows, lanes), 1)


def roll(x, amount):
    return pltpu.roll(x, amount % x.shape[1], 1)


def inside(lane, *spans):
    hit = None
    for low, high in spans:
        one = (lane >= low) & (lane < high)
        hit = one if hit is None else hit | one
    return hit


def over_chunks(rows, body):
    chunk = max(n for n in range(8, CHUNK + 1, 8) if rows % n == 0)

    def step(c, carry):
        body(pl.multiple_of(c * chunk, 8), chunk)
        return carry

    lax.fori_loop(0, rows // chunk, step, 0)


def coefficients(region, nu_tab, sat_tab, mob_tab):
    base = jnp.zeros(region.shape, jnp.float32)
    satur, mobile = base, base
    for r in range(nu_tab.shape[0]):
        hit = region == r
        base = jnp.where(hit, nu_tab[r], base)
        satur = jnp.where(hit, sat_tab[r], satur)
        mobile = jnp.where(hit, mob_tab[r], mobile)
    gain = 1.0 / (1.0 + 12.0 * mobile * base)
    slope = base * satur
    return base + slope, slope, mobile * 0.5, gain


def fine_steps(units, rows):
    for bufs, nu, top, slope, mob, drive in units:
        for old, new in zip(bufs[:-1], bufs[1:]):

            def first(base, n, old=old, nu=nu, top=top, slope=slope):
                here = old[pl.ds(base + PAD, n), :]
                dr = old[pl.ds(base + PAD + 1, n), :] - old[pl.ds(base + PAD - 1, n), :]
                dt = roll(here, -1) - roll(here, 1)
                bottom = 1.0 + 0.25 * (dr * dr + dt * dt)
                nu[pl.ds(base + PAD, n), :] = top[pl.ds(base, n), :] - slope[pl.ds(base, n), :] / bottom

            over_chunks(rows, first)
            nu[PAD - 1 : PAD, :] = nu[PAD : PAD + 1, :]
            nu[PAD + rows : PAD + rows + 1, :] = nu[PAD + rows - 1 : PAD + rows, :]

            def second(base, n, old=old, new=new, nu=nu, mob=mob, drive=drive):
                here = old[pl.ds(base + PAD, n), :]
                nu0 = nu[pl.ds(base + PAD, n), :]
                east = (nu0 + roll(nu0, -1)) * (roll(here, -1) - here)
                total = east - roll(east, 1)
                north = (nu0 + nu[pl.ds(base + PAD + 1, n), :]) * (old[pl.ds(base + PAD + 1, n), :] - here)
                south = (nu0 + nu[pl.ds(base + PAD - 1, n), :]) * (old[pl.ds(base + PAD - 1, n), :] - here)
                total = total + north + south + drive[pl.ds(base, n), :]
                new[pl.ds(base + PAD, n), :] = here + mob[pl.ds(base, n), :] * total

            over_chunks(rows, second)


def clear_pads(ref, rows):
    ref[0:PAD, :] = jnp.zeros((PAD, ref.shape[1]), jnp.float32)
    ref[PAD + rows : rows + 2 * PAD, :] = jnp.zeros((PAD, ref.shape[1]), jnp.float32)


def pack_kernel(rows, start, core, own_a, own_j, got, region, a0, a1, j0, j1, to_west, to_east):
    h = core[0]
    q = a0.shape[1] // 4
    clear_pads(a0, rows)
    clear_pads(a1, rows)
    first = h * start

    def body(base, n):
        lane = lanes_of(n, a0.shape[1])
        src = pl.ds(pl.multiple_of(first + base, 8), n)
        a_own, j_own = own_a[src, :], own_j[src, :]
        a_got = got[pl.ds(base, n), :]
        j_got = got[pl.ds(pl.multiple_of(base + rows, 8), n), :]
        mine = h == 0
        a_0, a_1 = jnp.where(mine, a_own, a_got), jnp.where(mine, a_got, a_own)
        j_0, j_1 = jnp.where(mine, j_own, j_got), jnp.where(mine, j_got, j_own)
        a0[pl.ds(base + PAD, n), :] = a_0
        a1[pl.ds(base + PAD, n), :] = a_1
        j0[pl.ds(base, n), :] = j_0 * 2.0
        j1[pl.ds(base, n), :] = j_1 * 2.0
        ids = region[src, :].astype(jnp.float32)
        out = jnp.zeros((n, a0.shape[1]), jnp.float32)
        for part, (first0, second0) in enumerate(((a_0, a_1), (j_0, j_1), (ids, ids))):
            for s, x in enumerate((first0, second0)):
                at = (2 * s + 2) * q - HALO * (part + 1)
                out = jnp.where(inside(lane, (at, at + HALO)), roll(x, at), out)
        to_west[pl.ds(base, n), :] = out
        out = jnp.zeros((n, a0.shape[1]), jnp.float32)
        for part, (first0, second0) in enumerate(((a_0, a_1), (j_0, j_1), (ids, ids))):
            for s, x in enumerate((first0, second0)):
                at = 2 * s * q + HALO * part
                out = jnp.where(inside(lane, (at, at + HALO)), roll(x, at + HALO), out)
        to_east[pl.ds(base, n), :] = out

    over_chunks(rows, body)


def own_part(s0, s1, lane, rest):
    q = s0.shape[1] // 4
    out = rest
    for s, x in enumerate((s0, s1)):
        w = 2 * s * q
        out = jnp.where(inside(lane, (w + HALO, w + q)), roll(x, w + HALO), out)
        out = jnp.where(inside(lane, (w + q, w + 2 * q - HALO)), roll(x, w + 2 * q - HALO), out)
    return out


def merge_edges(main, strip, s, lane):
    lanes = main.shape[1]
    q = lanes // 4
    w = 2 * s * q
    out = jnp.where(lane < REACH, roll(strip, -(w + HALO)), main)
    return jnp.where(lane >= lanes - REACH, roll(strip, -(w + 2 * q - HALO)), out)


def main_kernel(rows, start, core, nu_tab, sat_tab, mob_tab, region, a0, a1, j0, j1, f0, f1, top, slope, mob, gain, b, c, nu):
    first = core[0] * start
    for ref in (b, c):
        clear_pads(ref, rows)

    def body(base, n):
        ids = region[pl.ds(pl.multiple_of(first + base, 8), n), :]
        here = pl.ds(base, n)
        top[here, :], slope[here, :], mob[here, :], gain[here, :] = coefficients(ids, nu_tab, sat_tab, mob_tab)

    over_chunks(rows, body)
    fine_steps(
        (((a0, b, c, f0), nu, top, slope, mob, j0), ((a1, b, c, f1), nu, top, slope, mob, j1)), rows
    )


def strip_kernel(
    rows, cut, flags, nu_tab, sat_tab, mob_tab, west, east, region, a0, a1, j0, j1, f0, f1, gain,
    top_s, slope_s, mob_s, gain_s, j_s, corr, corr_s, d_a, d_b, g_a, g_b, a_s, b_s, c_s, nu, d_s,
):
    lanes = a0.shape[1]
    q = lanes // 4
    first = flags[0] * flags[2]
    last = flags[1] == 1
    for ref in (a_s, b_s, c_s):
        clear_pads(ref, rows)

    def build(base, n):
        lane = lanes_of(n, lanes)
        here, padded = pl.ds(base, n), pl.ds(base + PAD, n)
        w, e = west[here, :], east[here, :]
        heads = inside(lane, (0, HALO), (2 * q, 2 * q + HALO))
        a_s[padded, :] = own_part(a0[padded, :], a1[padded, :], lane, jnp.where(heads, w, e))
        rest = jnp.where(heads, roll(w, -HALO), roll(e, HALO)) * 2.0
        j_s[here, :] = own_part(j0[here, :], j1[here, :], lane, rest)
        ids = region[pl.ds(pl.multiple_of(first + base, 8), n), :].astype(jnp.float32)
        rest = jnp.where(heads, roll(w, -2 * HALO), roll(e, 2 * HALO))
        ids = own_part(ids, ids, lane, rest).astype(jnp.int32)
        top_s[here, :], slope_s[here, :], mob_s[here, :], gain_s[here, :] = coefficients(
            ids, nu_tab, sat_tab, mob_tab
        )

    over_chunks(rows, build)
    fine_steps((((a_s, b_s, c_s, b_s), nu, top_s, slope_s, mob_s, j_s),), rows)

    def finish(base, n):
        lane = lanes_of(n, lanes)
        here, padded = pl.ds(base, n), pl.ds(base + PAD, n)
        strip = b_s[padded, :]
        g_s = gain_s[here, :]
        c = strip - g_s * a_s[padded, :]
        corr_s[here, :] = c
        d_s[here, :] = jnp.where(last, roll(strip, 2 * q), g_s * c + roll(c, 2 * q))
        g = gain[here, :]
        end0 = merge_edges(f0[padded, :], strip, 0, lane)
        end1 = merge_edges(f1[padded, :], strip, 1, lane)
        c0 = end0 - g * a0[padded, :]
        corr[here, :] = c0
        nu[here, :] = jnp.where(last, end1, g * c0 + end1 - g * a1[padded, :])

    over_chunks(rows, finish)
    d_a[...] = nu[0:cut, :]
    g_a[...] = gain[0:cut, :]
    d_b[0 : rows - cut, :] = nu[cut:rows, :]
    g_b[0 : rows - cut, :] = gain[cut:rows, :]
    fold(d_s, d_b, rows, rows - cut)
    fold(gain_s, g_b, rows, rows - cut)


def fold_tiles(rows):
    return -(-(rows // 8) // FOLD)


def fold(src, dst, rows, at):
    lanes = src.shape[1]
    q, width = lanes // 4, lanes // FOLD
    lane = lanes_of(8, lanes)
    tiles = fold_tiles(rows)
    for r in range(tiles):
        out = jnp.zeros((8, lanes), jnp.float32)
        for k in range(FOLD):
            t = k * tiles + r
            if 8 * t >= rows:
                continue
            x = src[8 * t : 8 * t + 8, :]
            at_w, at_e = width * k, width * k + width // 2
            out = jnp.where(inside(lane, (at_w, at_w + REACH)), roll(x, at_w - (HALO - REACH)), out)
            out = jnp.where(inside(lane, (at_e, at_e + REACH)), roll(x, at_e - (2 * q - HALO)), out)
        dst[at + 8 * r : at + 8 * r + 8, :] = out


def unfold(src, at, dst, rows):
    lanes = src.shape[1]
    q, width = lanes // 4, lanes // FOLD
    lane = lanes_of(8, lanes)
    tiles = fold_tiles(rows)
    for r in range(tiles):
        x = src[at + 8 * r : at + 8 * r + 8, :]
        for k in range(FOLD):
            t = k * tiles + r
            if 8 * t >= rows:
                continue
            at_w, at_e = width * k, width * k + width // 2
            out = jnp.where(lane < q, roll(x, HALO - REACH - at_w), roll(x, 2 * q - HALO - at_e))
            dst[8 * t : 8 * t + 8, :] = out


def second_kernel(
    rows, half, cut, flags, s_a, s_b, corr, corr_s, gain, top, slope, mob, j0, j1,
    gain_s, top_s, slope_s, mob_s, j_s,
    end_own, end_send, d_out, corr_out, gain_out, a0, a1, a_s, b0, b1, b_s, c, nu, spread,
):
    lanes = a0.shape[1]
    q = lanes // 4
    h = flags[0]
    last = flags[1] == 1
    for ref in (a0, a1, a_s, b0, b1, b_s, c):
        clear_pads(ref, rows)
    a0[PAD : PAD + cut, :] = s_a[...]
    a0[PAD + cut : PAD + rows, :] = s_b[0 : rows - cut, :]
    unfold(s_b, rows - cut, spread, rows)

    def build(base, n):
        lane = lanes_of(n, lanes)
        here, padded = pl.ds(base, n), pl.ds(base + PAD, n)
        s = a0[padded, :]
        a1[padded, :] = gain[here, :] * s + corr[here, :]
        strip = spread[here, :]
        strip = jnp.where(inside(lane, (HALO, q)), roll(s, HALO), strip)
        strip = jnp.where(inside(lane, (q, 2 * q - HALO)), roll(s, 2 * q - HALO), strip)
        other = roll(gain_s[here, :] * strip + corr_s[here, :], 2 * q)
        a_s[padded, :] = jnp.where(lane < 2 * q, strip, other)

    over_chunks(rows, build)
    fine_steps(
        (
            ((a0, b0, c, b0), nu, top, slope, mob, j0),
            ((a1, b1, c, b1), nu, top, slope, mob, j1),
            ((a_s, b_s, c, b_s), nu, top_s, slope_s, mob_s, j_s),
        ),
        rows,
    )

    def finish(base, n):
        lane = lanes_of(n, lanes)
        here = pl.ds(base, n)
        at = pl.multiple_of(base + h * (rows - half), 8)
        inner, padded = pl.ds(at, n), pl.ds(at + PAD, n)
        strip = b_s[padded, :]
        end0 = merge_edges(b0[padded, :], strip, 0, lane)
        end1 = merge_edges(b1[padded, :], strip, 1, lane)
        end_own[here, :] = jnp.where(h == 0, end0, end1)
        end_send[here, :] = jnp.where(h == 0, end1, end0)
        g = gain[inner, :]
        c0 = end0 - g * a0[padded, :]
        corr_out[here, :] = c0
        gain_out[here, :] = g
        d_out[here, :] = jnp.where(last, end1, g * c0 + end1 - g * a1[padded, :])

    over_chunks(half, finish)


def last_kernel(flags, s, corr, gain, own, send):
    h = flags[0]

    def body(base, n):
        here = pl.ds(base, n)
        new0 = s[here, :]
        new1 = gain[here, :] * new0 + corr[here, :]
        own[here, :] = jnp.where(h == 0, new0, new1)
        send[here, :] = jnp.where(h == 0, new1, new0)

    over_chunks(s.shape[0], body)


def join_kernel(half, flags, own, got, out):
    h = flags[0]
    out[pl.ds(pl.multiple_of(h * half, 8), half), :] = own[...]
    out[pl.ds(pl.multiple_of((1 - h) * half, 8), half), :] = got[...]


def call(kernel, outs, scratch=(), smem=1, cost=None):
    def run(*operands):
        return pl.pallas_call(
            kernel,
            out_shape=[jax.ShapeDtypeStruct(shape, jnp.float32) for shape in outs],
            in_specs=[SMEM] * smem + [VMEM] * (len(operands) - smem),
            out_specs=[VMEM] * len(outs),
            scratch_shapes=[pltpu.VMEM(shape, jnp.float32) for shape in scratch],
            compiler_params=PARAMS,
            cost_estimate=cost,
        )(*operands)

    return run


def scan_plan(chips):
    levels = chips.bit_length() - 1
    every = range(chips)
    end = chips - 1
    own = [end if c == end else -1 for c in every]
    rising = []
    for b in range(levels):
        size = 1 << b
        into, keep, came = [], [], []
        for c in every:
            closes = (c >> (b + 1)) == (end >> (b + 1))
            if c & size:
                into.append(c % size)
                keep.append(0)
                came.append(-1 if closes else size)
            else:
                into.append(c if closes else -1)
                keep.append(-1 if closes else size)
                came.append(0)
        rising.append((b, into, keep, came))
    if levels != 2:
        return own, (rising, rising)

    def weight(to, at):
        return max(to - (at + 1) % chips, -1)

    turned = [
        (1, [weight(c, c ^ 2) for c in every], [weight(c ^ 1, c) for c in every], [weight(c ^ 1, c ^ 2) for c in every]),
        (0, [0 for c in every], None, None),
    ]
    return own, (rising, turned)


def power(square, exponents, chip):
    most = max(exponents)
    e = jnp.asarray(np.array(exponents, np.int32))[chip]
    value, factor = jnp.ones_like(square), square
    for k in range(max(most, 0).bit_length()):
        value = jnp.where((e >> k) & 1 == 1, value * factor, value)
        factor = factor * factor
    return jnp.where(e < 0, jnp.float32(0.0), value)


def scan(parts, gains, chip, chips, count):
    own, orders = scan_plan(chips)
    squares = [g * g for g in gains]
    sums = [power(sq, own, chip) * d for sq, d in zip(squares, parts)]
    passed = list(parts)
    for stage in range(len(orders[0])):
        arrived = []
        for p, order in enumerate(orders):
            pairs = [(i, i ^ (2 << order[stage][0])) for i in range(count)]
            arrived.append(lax.ppermute(passed[p], "tm", pairs))
        for p, order in enumerate(orders):
            _, into, keep, came = order[stage]
            sums[p] = sums[p] + power(squares[p], into, chip) * arrived[p]
            if stage + 1 < len(order):
                passed[p] = (
                    power(squares[p], keep, chip) * passed[p] + power(squares[p], came, chip) * arrived[p]
                )
    return sums


def local(initial_starts, source, region, base_reluctivity, saturation, mobility):
    potential, driver = initial_starts[0], source[0]
    radial, lanes = potential.shape
    count = lax.axis_size("tm")
    chips = count // 2
    spaces = lax.axis_size("space")
    slot = lax.axis_index("tm")
    h, chip = slot % 2, slot // 2
    half = radial // 2
    margin = -(-HALO // 8) * 8
    rows, start = half + margin, half - margin
    flags = jnp.stack([h, (chip == chips - 1).astype(jnp.int32), jnp.int32(start)]).astype(jnp.int32)
    tables = (base_reluctivity, saturation, mobility)
    partner = [(i, i ^ 1) for i in range(count)]
    slab, padded = (rows, lanes), (rows + 2 * PAD, lanes)
    cost = pl.CostEstimate(flops=240 * rows * lanes, bytes_accessed=40 * rows * lanes, transcendentals=0)

    there = (1 - h) * start
    send = jnp.concatenate(
        [lax.dynamic_slice(x, (there, 0), slab) for x in (potential, driver)], axis=0
    )
    got = lax.ppermute(send, "tm", partner)
    a0, a1, j0, j1, to_west, to_east = call(
        functools.partial(pack_kernel, rows, start), (padded, padded, slab, slab, slab, slab), cost=cost
    )(flags, potential, driver, got, region)
    from_east = lax.ppermute(to_west, "space", [((i + 1) % spaces, i) for i in range(spaces)])
    from_west = lax.ppermute(to_east, "space", [(i, (i + 1) % spaces) for i in range(spaces)])
    f0, f1, top, slope, mob, gain = call(
        functools.partial(main_kernel, rows, start),
        (padded, padded, slab, slab, slab, slab), (padded, padded, padded), smem=4, cost=cost,
    )(flags, *tables, region, a0, a1, j0, j1)

    tail = 8 * fold_tiles(rows)
    cut = 8 * (-(-(rows + tail) // 16))
    part_a, part_b = (cut, lanes), (rows - cut + tail, lanes)
    top_s, slope_s, mob_s, gain_s, j_s, corr, corr_s, d_a, d_b, g_a, g_b = call(
        functools.partial(strip_kernel, rows, cut),
        (slab, slab, slab, slab, slab, slab, slab, part_a, part_b, part_a, part_b),
        (padded, padded, padded, padded, slab), smem=4, cost=cost,
    )(flags, *tables, from_west, from_east, region, a0, a1, j0, j1, f0, f1, gain)
    s_a, s_b = scan((d_a, d_b), (g_a, g_b), chip, chips, count)

    own_rows = (half, lanes)
    end_own, end_send, d_out, corr_2, gain_2 = call(
        functools.partial(second_kernel, rows, half, cut),
        (own_rows, own_rows, own_rows, own_rows, own_rows),
        (padded, padded, padded, padded, padded, padded, padded, padded, slab), cost=cost,
    )(flags, s_a, s_b, corr, corr_s, gain, top, slope, mob, j0, j1, gain_s, top_s, slope_s, mob_s, j_s)
    quarter = half // 2
    s_2 = scan(
        (d_out[:quarter], d_out[quarter:]), (gain_2[:quarter], gain_2[quarter:]), chip, chips, count
    )
    end_got = lax.ppermute(end_send, "tm", partner)
    (ends,) = call(functools.partial(join_kernel, half), ((radial, lanes),))(flags, end_own, end_got)
    new_own, new_send = call(last_kernel, (own_rows, own_rows))(
        flags, jnp.concatenate(s_2, axis=0), corr_2, gain_2
    )
    new_got = lax.ppermute(new_send, "tm", partner)
    (starts,) = call(functools.partial(join_kernel, half), ((radial, lanes),))(flags, new_own, new_got)
    return (starts[None], ends[None])


def solution(mesh):
    placed = (P("tm", None, "space"), P("tm", None, "space"), P(None, "space"), P(), P(), P())
    return jax.shard_map(
        local,
        mesh=mesh,
        in_specs=placed,
        out_specs=(P("tm", None, "space"), P("tm", None, "space")),
        check_vma=False,
    )
```

time: 286 us -> 123 us (0.43)
  the two profiles are of different devices: /device:TPU:12 before, /device:TPU:0 now
where the time goes in v1:
time: 123 us
  Pallas kernels  64.7 us (53%)
  waiting for transfers between devices  21 us (17%)
  starting transfers between devices  13.5 us (11%)
  local copies, waits for them, and re-layouts  11.6 us (9%)
  between operations  11.3 us (9%)
    pallas_call x7, Pallas kernels, run(): pl.pallas_call(kernel, out_shape=[jax.ShapeDtypeStruct(shape, jnp.float32...  64.7 us
    ppermute x8, waiting for transfers between devices, scan(): arrived.append(lax.ppermute(passed[p], 'tm', pairs))  19.4 us
    ppermute x8, starting transfers between devices, scan(): arrived.append(lax.ppermute(passed[p], 'tm', pairs))  7.76 us
    unnamed x46, local copies, waits for them, and re-layouts  6.21 us
    dynamic_slice x7, local copies, waits for them, and re-layouts, power(): e = jnp.asarray(np.array(exponents, np.int32))[chip]  4.2 us
    ppermute x1, starting transfers between devices, local(): lax.ppermute(to_east, 'space', [(i, (i + 1) % spaces) for i in range(spac...  2.99 us
  transfers between devices with their start and end apart: 13, of which 9 were waited for; matrix products, arithmetic and copies ran while one was open for 4% of the time, Pallas kernels for 16%

profile of v1, /device:TPU:0, one launch (start us, length us, event | category | flops | bytes accessed | tf_op | source)
XLA Modules:
  0.0 122.6 jit_solution(11316472214523845515)
XLA Ops:
  0.7 1.1 dynamic-slice_bitcast_fusion
  2.5 1.5 %collective-permute-done.got = f32[1056,128]{1,0:T(8,128)S(1)} collective-permute-done((f32[1056,128]{1,0:T(8,128)S(1)}, f32[1056,128]{1,0:T(8,128)S(1)}, u32[]{:S(2)}, u32[]{:S(2)}) %collective-permute-start) | collective-permute-done | bytes 540704 | tf_op jit(solution)/shard_map/ppermute | solution.py:430
  4.0 2.1 %shard_map.257 = (f32[544,128]{1,0:T(8,128)S(1)}, f32[544,128]{1,0:T(8,128)S(1)}, f32[528,128]{1,0:T(8,128)S(1)}, f32[528,128]{1,0:T(8,128)S(1)}, f32[528,128]{1,0:T(8,128)S(1)}, /*index=5*/f32[528,128]{1,0:T(8,128)S(1)}) custom-call(s32[3]{0:T(128)S(1)} %pad_add_fusion.core.flags, f32[1024,128]{1,0:T(8,128)S(1)} %bitcast.27, f32[1024,128]{1,0:T(8,128)S(1)} %bitcast.28, ...), custom_call_target="tpu_custom_call" | custom-call | flops 16220160 | bytes 2703360 | tf_op jit(solution)/shard_map/pallas_call | solution.py:333
  6.1 3.0 %collective-permute-start.1 = (f32[528,128]{1,0:T(8,128)S(1)}, f32[528,128]{1,0:T(8,128)S(1)}, u32[]{:S(2)}, u32[]{:S(2)}) collective-permute-start(f32[528,128]{1,0:T(8,128)S(1)} %get-tuple-element.32), channel_id=1, source_target_pairs={{0,1},{1,2},{2,3},{3,0},{4,5},{5,6},{6,7},{7,4},{8,9},{9,10},{10,1... | collective-permute-start | bytes 811016 | tf_op jit(solution)/shard_map/ppermute | solution.py:435
  9.1 2.1 %collective-permute-start.2 = (f32[528,128]{1,0:T(8,128)S(1)}, f32[528,128]{1,0:T(8,128)S(1)}, u32[]{:S(2)}, u32[]{:S(2)}) collective-permute-start(f32[528,128]{1,0:T(8,128)S(1)} %get-tuple-element.33), channel_id=1, source_target_pairs={{1,0},{2,1},{3,2},{0,3},{5,4},{6,5},{7,6},{4,7},{9,8},{10,9},{11,1... | collective-permute-start | bytes 811016 | tf_op jit(solution)/shard_map/ppermute | solution.py:434
  11.9 17.7 %shard_map.258 = (f32[544,128]{1,0:T(8,128)S(1)}, f32[544,128]{1,0:T(8,128)S(1)}, f32[528,128]{1,0:T(8,128)S(1)}, f32[528,128]{1,0:T(8,128)S(1)}, f32[528,128]{1,0:T(8,128)S(1)}, /*index=5*/f32[528,128]{1,0:T(8,128)S(1)}) custom-call(s32[3]{0:T(128)S(1)} %pad_add_fusion.core.flags, f32[8]{0:T(128)S(1)} %copy-done.13, f32[8]{0:T(128)S(1)} %copy-done.14, ...), custom_call_target="tpu_custom_call" | custom-call | flops 16220160 | bytes 2703360 | tf_op jit(solution)/shard_map/pallas_call | solution.py:333
  29.6 12.6 %shard_map.259 = (f32[528,128]{1,0:T(8,128)S(1)}, f32[528,128]{1,0:T(8,128)S(1)}, f32[528,128]{1,0:T(8,128)S(1)}, f32[528,128]{1,0:T(8,128)S(1)}, f32[528,128]{1...) custom-call(s32[3]{0:T(128)S(1)} %pad_add_fusion.core.flags, ...), custom_call_target="tpu_custom_call" | custom-call | flops 16220160 | bytes 2703360 | tf_op jit(solution)/shard_map/pallas_call | solution.py:333
  42.2 0.7 copy-done.3
  43.7 0.7 copy-done.7
  45.8 1.7 %collective-permute-start.5 = (f32[296,128]{1,0:T(8,128)S(1)}, f32[296,128]{1,0:T(8,128)S(1)}, u32[]{:S(2)}, u32[]{:S(2)}) collective-permute-start(f32[296,128]{1,0:T(8,128)S(1)} %get-tuple-element.44), channel_id=1, source_target_pairs={{0,16},{4,20},{8,24},{12,28},{16,0},{20,4},{24,8},{28,12},{1,17},{... | collective-permute-start | bytes 454664 | tf_op jit(solution)/shard_map/ppermute | solution.py:398
  63.1 1.6 %collective-permute-start.3 = (f32[304,128]{1,0:T(8,128)S(1)}, f32[304,128]{1,0:T(8,128)S(1)}, u32[]{:S(2)}, u32[]{:S(2)}) collective-permute-start(f32[304,128]{1,0:T(8,128)S(1)} %get-tuple-element.42), channel_id=1, source_target_pairs={{0,8},{4,12},{8,0},{12,4},{16,24},{20,28},{24,16},{28,20},{1,9},{5... | collective-permute-start | bytes 466952 | tf_op jit(solution)/shard_map/ppermute | solution.py:398
  65.4 4.7 %collective-permute-done.3 = f32[304,128]{1,0:T(8,128)S(1)} collective-permute-done((f32[304,128]{1,0:T(8,128)S(1)}, f32[304,128]{1,0:T(8,128)S(1)}, u32[]{:S(2)}, u32[]{:S(2)}) %collective-permute-start.3) | collective-permute-done | bytes 155680 | tf_op jit(solution)/shard_map/ppermute | solution.py:398
  70.6 1.3 %collective-permute-done.6 = f32[296,128]{1,0:T(8,128)S(1)} collective-permute-done((f32[296,128]{1,0:T(8,128)S(1)}, f32[296,128]{1,0:T(8,128)S(1)}, u32[]{:S(2)}, u32[]{:S(2)}) %collective-permute-start.6) | collective-permute-done | bytes 151584 | tf_op jit(solution)/shard_map/ppermute | solution.py:398
  71.9 3.5 %collective-permute-done.4 = f32[304,128]{1,0:T(8,128)S(1)} collective-permute-done((f32[304,128]{1,0:T(8,128)S(1)}, f32[304,128]{1,0:T(8,128)S(1)}, u32[]{:S(2)}, u32[]{:S(2)}) %collective-permute-start.4) | collective-permute-done | bytes 155680 | tf_op jit(solution)/shard_map/ppermute | solution.py:398
  75.6 0.8 copy-done.4
  76.5 28.9 %shard_map.260 = (f32[512,128]{1,0:T(8,128)S(1)}, f32[512,128]{1,0:T(8,128)S(1)}, f32[512,128]{1,0:T(8,128)S(1)}, f32[512,128]{1,0:T(8,128)S(1)}, f32[512,128]{1,0:T(8,128)S(1)}) custom-call(s32[3]{0:T(128)S(1)} %pad_add_fusion.core.flags, f32[304,128]{1,0:T(8,128)S(1)} %fusion.3.s_a, f32[296,128]{1,0:T(8,128)S(1)} %fusion.9.s_b, f32[528,128]{1,0:T(8,128)S(1)} %copy-done.10, ...), custom_call_target="tpu_custom_call" | custom-call | flops 16220160 | bytes 2703360 | tf_op jit(solution)/shard_map/pallas_call | solution.py:333
  105.4 1.6 %collective-permute-start.7 = (f32[256,128]{1,0:T(8,128)S(1)}, f32[256,128]{1,0:T(8,128)S(1)}, u32[]{:S(2)}, u32[]{:S(2)}) collective-permute-start(f32[256,128]{1,0:T(8,128)S(1)} %get-tuple-element.66), channel_id=1, source_target_pairs={{0,8},{4,12},{8,0},{12,4},{16,24},{20,28},{24,16},{28,20},{1,9},{5... | collective-permute-start | bytes 393224 | tf_op jit(solution)/shard_map/ppermute | solution.py:398
  107.4 3.9 %collective-permute-done.7 = f32[256,128]{1,0:T(8,128)S(1)} collective-permute-done((f32[256,128]{1,0:T(8,128)S(1)}, f32[256,128]{1,0:T(8,128)S(1)}, u32[]{:S(2)}, u32[]{:S(2)}) %collective-permute-start.7) | collective-permute-done | bytes 131104 | tf_op jit(solution)/shard_map/ppermute | solution.py:398
  111.4 1.1 collective-permute-done.9
  112.6 1.3 %collective-permute-start.10 = (f32[256,128]{1,0:T(8,128)S(1)}, f32[256,128]{1,0:T(8,128)S(1)}, u32[]{:S(2)}, u32[]{:S(2)}) collective-permute-start(f32[256,128]{1,0:T(8,128)S(1)} %get-tuple-element.65), channel_id=1, source_target_pairs={{0,8},{4,12},{8,0},{12,4},{16,24},{20,28},{24,16},{28,20},{1,9},{5... | collective-permute-start | bytes 393224 | tf_op jit(solution)/shard_map/ppermute | solution.py:398
  114.0 3.6 %collective-permute-done.10 = f32[256,128]{1,0:T(8,128)S(1)} collective-permute-done((f32[256,128]{1,0:T(8,128)S(1)}, f32[256,128]{1,0:T(8,128)S(1)}, u32[]{:S(2)}, u32[]{:S(2)}) %collective-permute-start.10) | collective-permute-done | bytes 131104 | tf_op jit(solution)/shard_map/ppermute | solution.py:398
  117.6 1.2 collective-permute-done.8
  119.8 1.4 %shard_map.263 = f32[1024,128]{1,0:T(8,128)} custom-call(s32[3]{0:T(128)S(1)} %pad_add_fusion.core.flags, f32[512,128]{1,0:T(8,128)S(1)} %get-tuple-element.60.own, f32[512,128]{1,0:T(8,128)S(1)} %collective-permute-done.12.got), custom_call_target="tpu_custom_call" | custom-call | tf_op jit(solution)/shard_map/pallas_call | solution.py:333
  121.3 1.4 %shard_map.262 = f32[1024,128]{1,0:T(8,128)} custom-call(s32[3]{0:T(128)S(1)} %pad_add_fusion.core.flags, f32[512,128]{1,0:T(8,128)S(1)} %get-tuple-element.58.own, f32[512,128]{1,0:T(8,128)S(1)} %collective-permute-done.11.got), custom_call_target="tpu_custom_call" | custom-call | tf_op jit(solution)/shard_map/pallas_call | solution.py:333
  (73 shorter events, 12.0 us)
Async XLA Ops:
  0.6 3.3 %copy-start.2 = (f32[1,1024,128]{2,1,0:T(8,128)S(1)}, f32[1,1024,128]{2,1,0:T(8,128)}, u32[]{:S(2)}) copy-start(f32[1,1024,128]{2,1,0:T(8,128)} %param.27) | copy-start | bytes 1572868
  1.8 2.2 %copy-start = (s32[1024,128]{1,0:T(8,128)S(1)}, s32[1024,128]{1,0:T(8,128)}, u32[]{:S(2)}) copy-start(s32[1024,128]{1,0:T(8,128)} %region.5) | copy-start | bytes 1572868
  1.8 2.2 %copy-start.1 = (f32[1,1024,128]{2,1,0:T(8,128)S(1)}, f32[1,1024,128]{2,1,0:T(8,128)}, u32[]{:S(2)}) copy-start(f32[1,1024,128]{2,1,0:T(8,128)} %param.26) | copy-start | bytes 1572868
  1.9 2.1 %collective-permute-start = (f32[1056,128]{1,0:T(8,128)S(1)}, f32[1056,128]{1,0:T(8,128)S(1)}, u32[]{:S(2)}, u32[]{:S(2)}) collective-permute-start(f32[1056,128]{1,0:T(8,128)S(1)} %pad_maximum_fusion), channel_id=1, source_target_pairs={{0,4},{4,0},{8,12},{12,8},{16,20},{20,16},{24,28},{28,24},{1,5},{5... | collective-permute-start | bytes 1622024 | tf_op jit(solution)/shard_map/ppermute | solution.py:430
  6.1 23.5 %collective-permute-start.1 = (f32[528,128]{1,0:T(8,128)S(1)}, f32[528,128]{1,0:T(8,128)S(1)}, u32[]{:S(2)}, u32[]{:S(2)}) collective-permute-start(f32[528,128]{1,0:T(8,128)S(1)} %get-tuple-element.32), channel_id=1, source_target_pairs={{0,1},{1,2},{2,3},{3,0},{4,5},{5,6},{6,7},{7,4},{8,9},{9,10},{10,1... | collective-permute-start | bytes 811016 | tf_op jit(solution)/shard_map/ppermute | solution.py:435
  9.1 20.5 %collective-permute-start.2 = (f32[528,128]{1,0:T(8,128)S(1)}, f32[528,128]{1,0:T(8,128)S(1)}, u32[]{:S(2)}, u32[]{:S(2)}) collective-permute-start(f32[528,128]{1,0:T(8,128)S(1)} %get-tuple-element.33), channel_id=1, source_target_pairs={{1,0},{2,1},{3,2},{0,3},{5,4},{6,5},{7,6},{4,7},{9,8},{10,9},{11,1... | collective-permute-start | bytes 811016 | tf_op jit(solution)/shard_map/ppermute | solution.py:434
  42.2 0.7 copy-start.3
  43.7 0.7 copy-start.7
  44.4 0.7 copy-start.9
  45.8 18.9 %collective-permute-start.5 = (f32[296,128]{1,0:T(8,128)S(1)}, f32[296,128]{1,0:T(8,128)S(1)}, u32[]{:S(2)}, u32[]{:S(2)}) collective-permute-start(f32[296,128]{1,0:T(8,128)S(1)} %get-tuple-element.44), channel_id=1, source_target_pairs={{0,16},{4,20},{8,24},{12,28},{16,0},{20,4},{24,8},{28,12},{1,17},{... | collective-permute-start | bytes 454664 | tf_op jit(solution)/shard_map/ppermute | solution.py:398
  63.1 7.0 %collective-permute-start.3 = (f32[304,128]{1,0:T(8,128)S(1)}, f32[304,128]{1,0:T(8,128)S(1)}, u32[]{:S(2)}, u32[]{:S(2)}) collective-permute-start(f32[304,128]{1,0:T(8,128)S(1)} %get-tuple-element.42), channel_id=1, source_target_pairs={{0,8},{4,12},{8,0},{12,4},{16,24},{20,28},{24,16},{28,20},{1,9},{5... | collective-permute-start | bytes 466952 | tf_op jit(solution)/shard_map/ppermute | solution.py:398
  64.8 7.0 %collective-permute-start.6 = (f32[296,128]{1,0:T(8,128)S(1)}, f32[296,128]{1,0:T(8,128)S(1)}, u32[]{:S(2)}, u32[]{:S(2)}) collective-permute-start(f32[296,128]{1,0:T(8,128)S(1)} %fusion.12), channel_id=1, source_target_pairs={{0,8},{4,12},{8,0},{12,4},{16,24},{20,28},{24,16},{28,20},{1,9},{5... | collective-permute-start | bytes 454664 | tf_op jit(solution)/shard_map/ppermute | solution.py:398
  70.1 5.3 %collective-permute-start.4 = (f32[304,128]{1,0:T(8,128)S(1)}, f32[304,128]{1,0:T(8,128)S(1)}, u32[]{:S(2)}, u32[]{:S(2)}) collective-permute-start(f32[304,128]{1,0:T(8,128)S(1)} %multiply_add_fusion), channel_id=1, source_target_pairs={{0,16},{4,20},{8,24},{12,28},{16,0},{20,4},{24,8},{28,12},{1,17},{... | collective-permute-start | bytes 466952 | tf_op jit(solution)/shard_map/ppermute | solution.py:398
  71.8 3.7 %copy-start.8 = (f32[528,128]{1,0:T(8,128)S(1)}, f32[528,128]{1,0:T(8,128)}, u32[]{:S(2)}) copy-start(f32[528,128]{1,0:T(8,128)} %copy-done.7) | copy-start | bytes 811012
  71.8 3.7 %copy-start.10 = (f32[528,128]{1,0:T(8,128)S(1)}, f32[528,128]{1,0:T(8,128)}, u32[]{:S(2)}) copy-start(f32[528,128]{1,0:T(8,128)} %copy-done.9) | copy-start | bytes 811012
  71.8 3.8 %copy-start.12 = (f32[528,128]{1,0:T(8,128)S(1)}, f32[528,128]{1,0:T(8,128)}, u32[]{:S(2)}) copy-start(f32[528,128]{1,0:T(8,128)} %copy-done.11) | copy-start | bytes 811012
  75.4 1.0 copy-start.4
  75.4 1.0 copy-start.6
  105.4 6.0 %collective-permute-start.7 = (f32[256,128]{1,0:T(8,128)S(1)}, f32[256,128]{1,0:T(8,128)S(1)}, u32[]{:S(2)}, u32[]{:S(2)}) collective-permute-start(f32[256,128]{1,0:T(8,128)S(1)} %get-tuple-element.66), channel_id=1, source_target_pairs={{0,8},{4,12},{8,0},{12,4},{16,24},{20,28},{24,16},{28,20},{1,9},{5... | collective-permute-start | bytes 393224 | tf_op jit(solution)/shard_map/ppermute | solution.py:398
  106.9 5.6 %collective-permute-start.9 = (f32[256,128]{1,0:T(8,128)S(1)}, f32[256,128]{1,0:T(8,128)S(1)}, u32[]{:S(2)}, u32[]{:S(2)}) collective-permute-start(f32[256,128]{1,0:T(8,128)S(1)} %get-tuple-element.67), channel_id=1, source_target_pairs={{0,16},{4,20},{8,24},{12,28},{16,0},{20,4},{24,8},{28,12},{1,17},{... | collective-permute-start | bytes 393224 | tf_op jit(solution)/shard_map/ppermute | solution.py:398
  112.6 5.0 %collective-permute-start.10 = (f32[256,128]{1,0:T(8,128)S(1)}, f32[256,128]{1,0:T(8,128)S(1)}, u32[]{:S(2)}, u32[]{:S(2)}) collective-permute-start(f32[256,128]{1,0:T(8,128)S(1)} %get-tuple-element.65), channel_id=1, source_target_pairs={{0,8},{4,12},{8,0},{12,4},{16,24},{20,28},{24,16},{28,20},{1,9},{5... | collective-permute-start | bytes 393224 | tf_op jit(solution)/shard_map/ppermute | solution.py:398
  113.9 5.0 %collective-permute-start.8 = (f32[256,128]{1,0:T(8,128)S(1)}, f32[256,128]{1,0:T(8,128)S(1)}, u32[]{:S(2)}, u32[]{:S(2)}) collective-permute-start(f32[256,128]{1,0:T(8,128)S(1)} %get-tuple-element.64), channel_id=1, source_target_pairs={{0,16},{4,20},{8,24},{12,28},{16,0},{20,4},{24,8},{28,12},{1,17},{... | collective-permute-start | bytes 393224 | tf_op jit(solution)/shard_map/ppermute | solution.py:398
  114.0 5.7 %collective-permute-start.12 = (f32[512,128]{1,0:T(8,128)S(1)}, f32[512,128]{1,0:T(8,128)S(1)}, u32[]{:S(2)}, u32[]{:S(2)}) collective-permute-start(f32[512,128]{1,0:T(8,128)S(1)} %get-tuple-element.61), channel_id=1, source_target_pairs={{0,4},{4,0},{8,12},{12,8},{16,20},{20,16},{24,28},{28,24},{1,5},{5... | collective-permute-start | bytes 786440 | tf_op jit(solution)/shard_map/ppermute | solution.py:461
  119.7 1.6 %collective-permute-start.11 = (f32[512,128]{1,0:T(8,128)S(1)}, f32[512,128]{1,0:T(8,128)S(1)}, u32[]{:S(2)}, u32[]{:S(2)}) collective-permute-start(f32[512,128]{1,0:T(8,128)S(1)} %get-tuple-element.59), channel_id=1, source_target_pairs={{0,4},{4,0},{8,12},{12,8},{16,20},{20,16},{24,28},{28,24},{1,5},{5... | collective-permute-start | bytes 786440 | tf_op jit(solution)/shard_map/ppermute | solution.py:466
  (12 other events, 8.0 us)

commit v2 on v1

v2 whole, which is shorter than its diff:
```python
import functools

import jax
import jax.numpy as jnp
import numpy as np
from jax import lax
from jax.experimental import pallas as pl
from jax.experimental.pallas import tpu as pltpu
from jax.sharding import PartitionSpec as P

STEPS = 3
ITERS = 2
HALO = 2 * STEPS * ITERS
J_HALO = HALO - 2
ID_HALO = HALO - 1
REACH = 2 * STEPS
PAD = 8
CHUNK = 88
FOLD = 8
VMEM = pl.BlockSpec(memory_space=pltpu.VMEM)
FLAGS = 3
SMEM = pl.BlockSpec(memory_space=pltpu.SMEM)
PARAMS = pltpu.CompilerParams(vmem_limit_bytes=14 * 1024 * 1024)


def lanes_of(rows, lanes):
    return lax.broadcasted_iota(jnp.int32, (rows, lanes), 1)


def roll(x, amount):
    amount = amount % x.shape[1]
    return pltpu.roll(x, amount, 1) if amount else x


def inside(lane, *spans):
    hit = None
    for low, high in spans:
        one = (lane >= low) & (lane < high)
        hit = one if hit is None else hit | one
    return hit


def over_chunks(rows, body):
    chunk = max(n for n in range(8, CHUNK + 1, 8) if rows % n == 0)
    for base in range(0, rows, chunk):
        body(base, chunk)


def aligned(at):
    return at if isinstance(at, int) else pl.multiple_of(at, 8)


def coefficients(region, nu_tab, sat_tab, mob_tab):
    base = jnp.zeros(region.shape, jnp.float32)
    satur, mobile = base, base
    for r in range(nu_tab.shape[0]):
        hit = region == r
        base = jnp.where(hit, nu_tab[r], base)
        satur = jnp.where(hit, sat_tab[r], satur)
        mobile = jnp.where(hit, mob_tab[r], mobile)
    gain = 1.0 / (1.0 + 12.0 * mobile * base)
    slope = base * satur
    return base + slope, slope, mobile * 0.5, gain


def fine_steps(units, rows, work):
    chunk = max(n for n in range(8, CHUNK + 1, 8) if rows % n == 0)
    chunks = rows // chunk
    for step in range(STEPS):
        moved = {}
        for turn in range(chunks + 4):
            for u, (bufs, top, slope, mob, drive) in enumerate(units):
                old, new = bufs[step], bufs[step + 1]
                nu, east, flow, face = work[4 * u : 4 * u + 4]
                c = turn - 3
                if 0 <= c < chunks:
                    at = c * chunk + PAD
                    nu0 = nu[pl.ds(at, chunk), :]
                    out = (nu0 + moved.pop((u, 3, c))) * east[pl.ds(at, chunk), :]
                    flow[pl.ds(at, chunk), :] = out
                    moved[u, 4, c] = roll(out, 1)
                    face[pl.ds(at, chunk), :] = (nu0 + nu[pl.ds(at - 1, chunk), :]) * (
                        old[pl.ds(at, chunk), :] - old[pl.ds(at - 1, chunk), :]
                    )
                    if c == chunks - 1:
                        at = PAD + rows
                        nu[at : at + 1, :] = nu[at - 1 : at, :]
                        face[pl.ds(at, 8), :] = (nu[pl.ds(at, 8), :] + nu[pl.ds(at - 1, 8), :]) * (
                            old[pl.ds(at, 8), :] - old[pl.ds(at - 1, 8), :]
                        )
                c = turn - 4
                if 0 <= c < chunks:
                    at, here_rows = c * chunk + PAD, pl.ds(c * chunk, chunk)
                    total = flow[pl.ds(at, chunk), :] - moved.pop((u, 4, c))
                    total = total + (face[pl.ds(at + 1, chunk), :] - face[pl.ds(at, chunk), :])
                    total = total + drive[here_rows, :]
                    new[pl.ds(at, chunk), :] = old[pl.ds(at, chunk), :] + mob[here_rows, :] * total
                c = turn - 2
                if 0 <= c < chunks:
                    at, here_rows = c * chunk + PAD, pl.ds(c * chunk, chunk)
                    dr = old[pl.ds(at + 1, chunk), :] - old[pl.ds(at - 1, chunk), :]
                    dt = east[pl.ds(at, chunk), :] + moved.pop((u, 2, c))
                    bottom = 1.0 + (dr * dr + dt * dt)
                    out = top[here_rows, :] - slope[here_rows, :] / bottom
                    nu[pl.ds(at, chunk), :] = out
                    if c == 0:
                        nu[PAD - 1 : PAD, :] = nu[PAD : PAD + 1, :]
                    moved[u, 3, c] = roll(out, -1)
                c = turn - 1
                if 0 <= c < chunks:
                    at = c * chunk + PAD
                    out = moved.pop((u, 1, c)) - old[pl.ds(at, chunk), :]
                    east[pl.ds(at, chunk), :] = out
                    moved[u, 2, c] = roll(out, 1)
                c = turn
                if 0 <= c < chunks:
                    moved[u, 1, c] = roll(old[pl.ds(c * chunk + PAD, chunk), :], -1)


def clear_pads(ref, rows):
    ref[0:PAD, :] = jnp.zeros((PAD, ref.shape[1]), jnp.float32)
    ref[PAD + rows : rows + 2 * PAD, :] = jnp.zeros((PAD, ref.shape[1]), jnp.float32)


def pack_kernel(rows, start, flags, own_a, own_j, got, region, a0, a1, j0, j1, to_west, to_east):
    lanes = a0.shape[1]
    q, both, tall = lanes // 4, HALO + J_HALO, rows // 2
    mine = flags[0] == 0
    first = flags[0] * start
    clear_pads(a0, rows)
    clear_pads(a1, rows)

    def body(low, n):
        lane = lanes_of(n, lanes)
        west = jnp.zeros((n, lanes), jnp.float32)
        east = west
        for k in range(2):
            base = low + k * tall
            src = pl.ds(aligned(first + base), n)
            a_own, j_own = own_a[src, :], own_j[src, :]
            a_got, j_got = got[pl.ds(base, n), :], got[pl.ds(base + rows, n), :]
            a_0, a_1 = jnp.where(mine, a_own, a_got) * 0.5, jnp.where(mine, a_got, a_own) * 0.5
            j_0, j_1 = jnp.where(mine, j_own, j_got), jnp.where(mine, j_got, j_own)
            a0[pl.ds(base + PAD, n), :] = a_0
            a1[pl.ds(base + PAD, n), :] = a_1
            j0[pl.ds(base, n), :] = j_0
            j1[pl.ds(base, n), :] = j_1
            ids = region[src, :].astype(jnp.float32)
            for s, (a, j) in enumerate(((a_0, j_0), (a_1, j_1))):
                at = (2 * s + 2) * q - HALO - k * both
                west = jnp.where(inside(lane, (at, at + HALO)), roll(a, at), west)
                at = at - J_HALO
                west = jnp.where(inside(lane, (at, at + J_HALO)), roll(j, at), west)
                at = 2 * s * q + k * both
                east = jnp.where(inside(lane, (at, at + HALO)), roll(a, at + HALO), east)
                at = at + HALO
                east = jnp.where(inside(lane, (at, at + J_HALO)), roll(j, at + J_HALO), east)
            at = 2 * q * (1 - k)
            west = jnp.where(inside(lane, (at, at + ID_HALO)), roll(ids, at), west)
            at = (3 - 2 * k) * q + HALO
            east = jnp.where(inside(lane, (at, at + ID_HALO)), roll(ids, at + ID_HALO), east)
        to_west[pl.ds(low, n), :] = west
        to_east[pl.ds(low, n), :] = east

    over_chunks(tall, body)


def own_part(s0, s1, lane):
    q = s0.shape[1] // 4
    out = jnp.zeros(s0.shape, jnp.float32)
    for s, x in enumerate((s0, s1)):
        w = 2 * s * q
        out = jnp.where(inside(lane, (w + HALO, w + q)), roll(x, w + HALO), out)
        out = jnp.where(inside(lane, (w + q, w + 2 * q - HALO)), roll(x, w + 2 * q - HALO), out)
    return out


def merge_edges(main, strip, s, lane):
    lanes = main.shape[1]
    q = lanes // 4
    w = 2 * s * q
    out = jnp.where(lane < REACH, roll(strip, -(w + HALO)), main)
    return jnp.where(lane >= lanes - REACH, roll(strip, -(w + 2 * q - HALO)), out)


def main_kernel(
    rows, start, flags, nu_tab, sat_tab, mob_tab, region, a0, a1, j0, j1,
    f0, f1, top, slope, mob, gain, a_own, j_own, id_own, b0, c0, b1, c1, *work,
):
    first = flags[0] * start
    for ref in (b0, c0, b1, c1):
        clear_pads(ref, rows)

    def body(base, n):
        lane = lanes_of(n, a0.shape[1])
        ids = region[pl.ds(aligned(first + base), n), :]
        here, padded = pl.ds(base, n), pl.ds(base + PAD, n)
        top[here, :], slope[here, :], mob[here, :], gain[here, :] = coefficients(ids, nu_tab, sat_tab, mob_tab)
        a_own[here, :] = own_part(a0[padded, :], a1[padded, :], lane)
        j_own[here, :] = own_part(j0[here, :], j1[here, :], lane)
        ids = ids.astype(jnp.float32)
        id_own[here, :] = own_part(ids, ids, lane)

    over_chunks(rows, body)
    fine_steps((((a0, b0, c0, f0), top, slope, mob, j0), ((a1, b1, c1, f1), top, slope, mob, j1)), rows, work)


def strip_kernel(
    rows, cut, tail_cut, flags, nu_tab, sat_tab, mob_tab, west, east, a_own, j_own, id_own,
    a0, a1, f0, f1, gain,
    top_s, slope_s, mob_s, gain_s, j_s, corr, corr_s, d_a, d_b, g_a, g_b, a_s, b_s, c_s, d_s, folded, *work,
):
    lanes = a0.shape[1]
    q, both, tall = lanes // 4, HALO + J_HALO, rows // 2
    last = flags[1] == 1
    for ref in (a_s, b_s, c_s):
        clear_pads(ref, rows)

    def build(low, n):
        lane = lanes_of(n, lanes)
        heads = inside(lane, (0, HALO), (2 * q, 2 * q + HALO))
        tails = inside(lane, (2 * q - HALO, 2 * q), (4 * q - HALO, 4 * q))
        w, e = west[pl.ds(low, n), :], east[pl.ds(low, n), :]
        w_ids = roll(w, 1 - (3 * q + HALO)), roll(w, 1 - (q + HALO))
        e_ids = roll(e, -HALO), roll(e, 2 * q - HALO)
        for k in range(2):
            base = low + k * tall
            here, padded = pl.ds(base, n), pl.ds(base + PAD, n)

            def halo(from_west, from_east, rest):
                return jnp.where(heads, from_west, jnp.where(tails, from_east, rest))

            a_s[padded, :] = halo(roll(w, -both) if k else w, roll(e, both) if k else e, a_own[here, :])
            j_s[here, :] = halo(
                roll(w, -J_HALO - k * both), roll(e, J_HALO + k * both), j_own[here, :]
            )
            lower = lane < 2 * q
            ids = halo(
                jnp.where(lower, w_ids[k], w_ids[1 - k]), jnp.where(lower, e_ids[k], e_ids[1 - k]), id_own[here, :]
            )
            top_s[here, :], slope_s[here, :], mob_s[here, :], gain_s[here, :] = coefficients(
                ids.astype(jnp.int32), nu_tab, sat_tab, mob_tab
            )

    over_chunks(tall, build)
    fine_steps((((a_s, b_s, c_s, b_s), top_s, slope_s, mob_s, j_s),), rows, work)

    def finish(base, n):
        lane = lanes_of(n, lanes)
        here, padded = pl.ds(base, n), pl.ds(base + PAD, n)
        strip = b_s[padded, :]
        g_s = gain_s[here, :]
        c = strip - g_s * a_s[padded, :]
        corr_s[here, :] = c
        d_s[here, :] = roll(jnp.where(last, strip, c), 2 * q) + jnp.where(last, 0.0, g_s * c)
        g = gain[here, :]
        end0 = merge_edges(f0[padded, :], strip, 0, lane)
        end1 = merge_edges(f1[padded, :], strip, 1, lane)
        change = end0 - g * a0[padded, :]
        corr[here, :] = change
        out = jnp.where(last, end1, g * change + end1 - g * a1[padded, :])
        to, g_to, at = (d_a, g_a, base) if base < cut else (d_b, g_b, base - cut)
        to[pl.ds(at, n), :] = out
        g_to[pl.ds(at, n), :] = g

    over_chunks(rows, finish)
    for src, part_a, part_b in ((d_s, d_a, d_b), (gain_s, g_a, g_b)):
        fold(src, folded, rows)
        part_a[cut : cut + tail_cut, :] = folded[0:tail_cut, :]
        part_b[rows - cut : rows - cut + folded.shape[0] - tail_cut, :] = folded[tail_cut:, :]


def fold_tiles(rows):
    return -(-(rows // 8) // FOLD)


def fold(src, dst, rows):
    lanes = src.shape[1]
    q, width = lanes // 4, lanes // FOLD
    lane = lanes_of(8, lanes)
    tiles = fold_tiles(rows)
    for r in range(tiles):
        out = jnp.zeros((8, lanes), jnp.float32)
        for k in range(FOLD):
            t = k * tiles + r
            if 8 * t >= rows:
                continue
            x = src[8 * t : 8 * t + 8, :]
            at_w, at_e = width * k, width * k + width // 2
            out = jnp.where(inside(lane, (at_w, at_w + REACH)), roll(x, at_w - (HALO - REACH)), out)
            out = jnp.where(inside(lane, (at_e, at_e + REACH)), roll(x, at_e - (2 * q - HALO)), out)
        dst[8 * r : 8 * r + 8, :] = out


def unfold(src, dst, rows):
    lanes = src.shape[1]
    q, width = lanes // 4, lanes // FOLD
    lane = lanes_of(8, lanes)
    tiles = fold_tiles(rows)
    for r in range(tiles):
        x = src[8 * r : 8 * r + 8, :]
        for k in range(FOLD):
            t = k * tiles + r
            if 8 * t >= rows:
                continue
            at_w, at_e = width * k, width * k + width // 2
            out = jnp.where(lane < q, roll(x, HALO - REACH - at_w), roll(x, 2 * q - HALO - at_e))
            dst[8 * t : 8 * t + 8, :] = out


def second_kernel(
    rows, half, cut, tail_cut, flags, s_a, s_b, r_a, r_b, corr, corr_s, gain, top, slope, mob, j0, j1,
    gain_s, top_s, slope_s, mob_s, j_s,
    end_own, end_send, d_a, d_b, g_a, g_b, corr_out,
    a0, a1, a_s, b0, b1, b_s, c0, c1, c_s, spread, folded, *work,
):
    lanes = a0.shape[1]
    q = lanes // 4
    h = flags[0]
    last = flags[1] == 1
    for ref in (a0, a1, a_s, b0, b1, b_s, c0, c1, c_s):
        clear_pads(ref, rows)
    folded[0:tail_cut, :] = s_a[cut:, :] + r_a[cut:, :]
    folded[tail_cut:, :] = s_b[rows - cut :, :] + r_b[rows - cut :, :]
    unfold(folded, spread, rows)

    def build(base, n):
        lane = lanes_of(n, lanes)
        here, padded = pl.ds(base, n), pl.ds(base + PAD, n)
        part, came, at = (s_a, r_a, base) if base < cut else (s_b, r_b, base - cut)
        s = part[pl.ds(at, n), :] + came[pl.ds(at, n), :]
        a0[padded, :] = s
        a1[padded, :] = gain[here, :] * s + corr[here, :]
        strip = spread[here, :]
        strip = jnp.where(inside(lane, (HALO, q)), roll(s, HALO), strip)
        strip = jnp.where(inside(lane, (q, 2 * q - HALO)), roll(s, 2 * q - HALO), strip)
        other = roll(gain_s[here, :] * strip + corr_s[here, :], 2 * q)
        a_s[padded, :] = jnp.where(lane < 2 * q, strip, other)

    over_chunks(rows, build)
    fine_steps(
        (
            ((a0, b0, c0, b0), top, slope, mob, j0),
            ((a1, b1, c1, b1), top, slope, mob, j1),
            ((a_s, b_s, c_s, b_s), top_s, slope_s, mob_s, j_s),
        ),
        rows,
        work,
    )

    def finish(base, n):
        lane = lanes_of(n, lanes)
        here = pl.ds(base, n)
        at = aligned(base + h * (rows - half))
        inner, padded = pl.ds(at, n), pl.ds(at + PAD, n)
        strip = b_s[padded, :]
        end0 = merge_edges(b0[padded, :], strip, 0, lane)
        end1 = merge_edges(b1[padded, :], strip, 1, lane)
        end_own[here, :] = jnp.where(h == 0, end0, end1) * 2.0
        end_send[here, :] = jnp.where(h == 0, end1, end0) * 2.0
        g = gain[inner, :]
        change = end0 - g * a0[padded, :]
        corr_out[here, :] = change * 2.0
        d_to, g_to, to = (d_a, g_a, base) if base < half // 2 else (d_b, g_b, base - half // 2)
        d_to[pl.ds(to, n), :] = jnp.where(last, end1, g * change + end1 - g * a1[padded, :]) * 2.0
        g_to[pl.ds(to, n), :] = g

    over_chunks(half, finish)


def stage_kernel(order, flags, g, d, came, out, passed):
    def body(base, n):
        here = pl.ds(base, n)
        gain = g[here, :]
        square = gain * gain
        fourth = square * square

        def weight(e):
            value = jnp.where(e % 2 == 1, square, 1.0) * jnp.where(e >= 2, fourth, 1.0)
            return jnp.where(e < 0, 0.0, value)

        mine, its = d[here, :], came[here, :]
        at = FLAGS + 3 * order
        out[here, :] = weight(flags[FLAGS - 1]) * mine + weight(flags[at]) * its
        passed[here, :] = weight(flags[at + 1]) * mine + weight(flags[at + 2]) * its

    over_chunks(d.shape[0], body)


def last_kernel(flags, s_a, s_b, r_a, r_b, g_a, g_b, corr, own, send):
    h = flags[0]
    tall = s_a.shape[0]
    for k, (s, r, g) in enumerate(((s_a, r_a, g_a), (s_b, r_b, g_b))):

        def body(base, n, k=k, s=s, r=r, g=g):
            here, there = pl.ds(base, n), pl.ds(base + k * tall, n)
            new0 = s[here, :] + r[here, :]
            new1 = g[here, :] * new0 + corr[there, :]
            own[there, :] = jnp.where(h == 0, new0, new1)
            send[there, :] = jnp.where(h == 0, new1, new0)

        over_chunks(tall, body)


def put_kernel(half, other, flags, piece, *rest):
    out, sem = rest[-2:]
    side = 1 - flags[0] if other else flags[0]
    copy = pltpu.make_async_copy(piece, out.at[pl.ds(aligned(side * half), half), :], sem)
    copy.start()
    copy.wait()


def put(half, flags, piece, into=None):
    anywhere = pl.BlockSpec(memory_space=pl.ANY)
    return pl.pallas_call(
        functools.partial(put_kernel, half, into is not None),
        out_shape=jax.ShapeDtypeStruct((2 * half, piece.shape[1]), jnp.float32),
        in_specs=[SMEM, VMEM] + ([anywhere] if into is not None else []),
        out_specs=anywhere,
        scratch_shapes=[pltpu.SemaphoreType.DMA],
        input_output_aliases={2: 0} if into is not None else {},
        compiler_params=PARAMS,
        cost_estimate=pl.CostEstimate(flops=0, bytes_accessed=piece.size * 8, transcendentals=0),
    )(flags, piece, *(() if into is None else (into,)))


def call(kernel, outs, scratch=(), smem=1, cost=None):
    def run(*operands):
        return pl.pallas_call(
            kernel,
            out_shape=[jax.ShapeDtypeStruct(shape, jnp.float32) for shape in outs],
            in_specs=[SMEM] * smem + [VMEM] * (len(operands) - smem),
            out_specs=[VMEM] * len(outs),
            scratch_shapes=[pltpu.VMEM(shape, jnp.float32) for shape in scratch],
            compiler_params=PARAMS,
            cost_estimate=cost,
        )(*operands)

    return run


def scan_plan(chips):
    levels = chips.bit_length() - 1
    every = range(chips)
    end = chips - 1
    own = [end if c == end else -1 for c in every]
    rising = []
    for b in range(levels):
        size = 1 << b
        into, keep, came = [], [], []
        for c in every:
            closes = (c >> (b + 1)) == (end >> (b + 1))
            if c & size:
                into.append(c % size)
                keep.append(0)
                came.append(-1 if closes else size)
            else:
                into.append(c if closes else -1)
                keep.append(-1 if closes else size)
                came.append(0)
        rising.append((b, into, keep, came))
    if levels != 2:
        return own, (rising, rising)

    def weight(to, at):
        return max(to - (at + 1) % chips, -1)

    both = []
    for one, two in ((1, 2), (2, 1)):
        first = [[weight(c, c ^ one) for c in every], [weight(c ^ two, c) for c in every]]
        first.append([weight(c ^ two, c ^ one) for c in every])
        both.append([(one.bit_length() - 1, *first), (two.bit_length() - 1,)])
    return own, tuple(both)


def power(square, exponents, chip):
    e = jnp.asarray(np.array(exponents, np.int32))[chip]
    value, factor = jnp.ones_like(square), square
    for k in range(max(max(exponents), 0).bit_length()):
        value = jnp.where((e >> k) & 1 == 1, value * factor, value)
        factor = factor * factor
    return jnp.where(e < 0, jnp.float32(0.0), value)


def exchange(value, bit, count):
    return lax.ppermute(value, "tm", [(i, i ^ (2 << bit)) for i in range(count)])


def scan(parts, gains, flags, chip, chips, count):
    own, orders = scan_plan(chips)
    if len(orders[0]) == 2:
        arrived = [exchange(d, order[0][0], count) for d, order in zip(parts, orders)]
        mid = [
            call(functools.partial(stage_kernel, p), (d.shape, d.shape))(flags, g, d, r)
            for p, (d, g, r) in enumerate(zip(parts, gains, arrived))
        ]
        came = [exchange(passed, order[1][0], count) for (_, passed), order in zip(mid, orders)]
        return [out for out, _ in mid], came
    squares = [g * g for g in gains]
    sums = [power(sq, own, chip) * d for sq, d in zip(squares, parts)]
    passed = list(parts)
    for stage in range(len(orders[0])):
        arrived = [exchange(d, order[stage][0], count) for d, order in zip(passed, orders)]
        for p, order in enumerate(orders):
            _, into, keep, came = order[stage]
            sums[p] = sums[p] + power(squares[p], into, chip) * arrived[p]
            passed[p] = power(squares[p], keep, chip) * passed[p] + power(squares[p], came, chip) * arrived[p]
    return sums, [jnp.zeros_like(x) for x in sums]


def local(initial_starts, source, region, base_reluctivity, saturation, mobility):
    potential, driver = initial_starts[0], source[0]
    radial, lanes = potential.shape
    count = lax.axis_size("tm")
    chips = count // 2
    spaces = lax.axis_size("space")
    slot = lax.axis_index("tm")
    chip = slot // 2
    half = radial // 2
    margin = -(-HALO // 8) * 8
    rows, start = half + margin, half - margin
    own, orders = scan_plan(chips)
    table = []
    for i in range(count):
        c = i // 2
        row = [i % 2, int(c == chips - 1), own[c]]
        for order in orders:
            row += [exponents[c] for exponents in order[0][1:]]
        table.append(row)
    flags = lax.dynamic_index_in_dim(jnp.asarray(np.array(table, np.int32)), slot, keepdims=False)
    tables = (base_reluctivity, saturation, mobility)
    partner = [(i, i ^ 1) for i in range(count)]
    slab, padded = (rows, lanes), (rows + 2 * PAD, lanes)
    cost = pl.CostEstimate(flops=240 * rows * lanes, bytes_accessed=40 * rows * lanes, transcendentals=0)

    there = (1 - slot % 2) * start
    send = jnp.concatenate(
        [lax.dynamic_slice(x, (there, 0), slab) for x in (potential, driver)], axis=0
    )
    got = lax.ppermute(send, "tm", partner)
    message = (rows // 2, lanes)
    a0, a1, j0, j1, to_west, to_east = call(
        functools.partial(pack_kernel, rows, start), (padded, padded, slab, slab, message, message), cost=cost
    )(flags, potential, driver, got, region)
    from_east = lax.ppermute(to_west, "space", [((i + 1) % spaces, i) for i in range(spaces)])
    from_west = lax.ppermute(to_east, "space", [(i, (i + 1) % spaces) for i in range(spaces)])
    f0, f1, top, slope, mob, gain, a_own, j_own, id_own = call(
        functools.partial(main_kernel, rows, start),
        (padded, padded) + (slab,) * 7, (padded,) * 12, smem=4, cost=cost,
    )(flags, *tables, region, a0, a1, j0, j1)

    tail = 8 * fold_tiles(rows)
    cut, tail_cut = rows // 2, 8 * (tail // 16)
    part_a, part_b = (cut + tail_cut, lanes), (rows - cut + tail - tail_cut, lanes)
    top_s, slope_s, mob_s, gain_s, j_s, corr, corr_s, d_a, d_b, g_a, g_b = call(
        functools.partial(strip_kernel, rows, cut, tail_cut),
        (slab,) * 7 + (part_a, part_b, part_a, part_b),
        (padded, padded, padded, slab, (tail, lanes)) + (padded,) * 4, smem=4, cost=cost,
    )(flags, *tables, from_west, from_east, a_own, j_own, id_own, a0, a1, f0, f1, gain)
    (s_a, s_b), (r_a, r_b) = scan((d_a, d_b), (g_a, g_b), flags, chip, chips, count)

    own_rows, quarter = (half, lanes), (half // 2, lanes)
    end_own, end_send, d_a, d_b, g_a, g_b, corr = call(
        functools.partial(second_kernel, rows, half, cut, tail_cut),
        (own_rows, own_rows, quarter, quarter, quarter, quarter, own_rows),
        (padded,) * 9 + (slab, (tail, lanes)) + (padded,) * 12, cost=cost,
    )(flags, s_a, s_b, r_a, r_b, corr, corr_s, gain, top, slope, mob, j0, j1, gain_s, top_s, slope_s, mob_s, j_s)
    end_got = lax.ppermute(end_send, "tm", partner)
    (s_a, s_b), (r_a, r_b) = scan((d_a, d_b), (g_a, g_b), flags, chip, chips, count)
    ends = put(half, flags, end_got, put(half, flags, end_own))
    new_own, new_send = call(last_kernel, (own_rows, own_rows))(flags, s_a, s_b, r_a, r_b, g_a, g_b, corr)
    new_got = lax.ppermute(new_send, "tm", partner)
    starts = put(half, flags, new_got, put(half, flags, new_own))
    return (starts[None], ends[None])


def solution(mesh):
    placed = (P("tm", None, "space"), P("tm", None, "space"), P(None, "space"), P(), P(), P())
    return jax.shard_map(
        local,
        mesh=mesh,
        in_specs=placed,
        out_specs=(P("tm", None, "space"), P("tm", None, "space")),
        check_vma=False,
    )
```

time: 123 us -> 58.3 us (0.47)
  Pallas kernels: 64.7 us -> 23 us
  between operations: 11.3 us -> 0.81 us
  local copies, waits for them, and re-layouts: 11.6 us -> 2.52 us
  waiting for transfers between devices: 21 us -> 15.2 us
  starting transfers between devices: 13.5 us -> 16.5 us
    pallas_call x7 -> x9, Pallas kernels: 64.7 us -> 18 us  [run(): pl.pallas_call(kernel, out_shape=[jax.ShapeDtypeStruct(shape, jnp.float32...]
    ppermute x8, waiting for transfers between devices: 19.4 us -> 13.2 us  [exchange(): return lax.ppermute(value, 'tm', [(i, i ^ 2 << bit) for i in range(count)])]
    unnamed x46 -> x12, local copies, waits for them, and re-layouts: 6.21 us -> 0.7 us
    pallas_call x0 -> x4, Pallas kernels: none -> 5.03 us  [put(): pl.pallas_call(functools.partial(put_kernel, half, into is not None), out...]
    dynamic_slice x7 -> x0, local copies, waits for them, and re-layouts: 4.2 us -> none  [power(): e = jnp.asarray(np.array(exponents, np.int32))[chip]]
    ppermute x8, starting transfers between devices: 7.76 us -> 10.7 us  [exchange(): return lax.ppermute(value, 'tm', [(i, i ^ 2 << bit) for i in range(count)])]
  transfers between devices with their start and end apart: 13 -> 13, of which waited for: 9 -> 7; matrix products, arithmetic and copies ran while one was open for 4% -> 1% of each run, Pallas kernels for 16% -> 19%
where the time goes in v2:
time: 58.3 us; the launch traced here: 58.1 us
  Pallas kernels  23 us (39%)
  starting transfers between devices  16.5 us (28%)
  waiting for transfers between devices  15.2 us (26%)
  local copies, waits for them, and re-layouts  2.52 us (4%)
  between operations  0.81 us (1%)
    pallas_call x9, Pallas kernels, run(): pl.pallas_call(kernel, out_shape=[jax.ShapeDtypeStruct(shape, jnp.float32...  18 us
    ppermute x8, waiting for transfers between devices, exchange(): return lax.ppermute(value, 'tm', [(i, i ^ 2 << bit) for i in range(count)])  13.2 us
    ppermute x8, starting transfers between devices, exchange(): return lax.ppermute(value, 'tm', [(i, i ^ 2 << bit) for i in range(count)])  10.7 us
    pallas_call x4, Pallas kernels, put(): pl.pallas_call(functools.partial(put_kernel, half, into is not None), out...  5.03 us
    ppermute x1, starting transfers between devices, local(): lax.ppermute(to_east, 'space', [(i, (i + 1) % spaces) for i in range(spac...  2.99 us
    ppermute x1, starting transfers between devices, local(): lax.ppermute(to_west, 'space', [((i + 1) % spaces, i) for i in range(spac...  2.09 us
    ppermute x1, waiting for transfers between devices, local(): lax.ppermute(to_west, 'space', [((i + 1) % spaces, i) for i in range(spac...  1.21 us
  transfers between devices with their start and end apart: 13, of which 7 were waited for; matrix products, arithmetic and copies ran while one was open for 1% of the time, Pallas kernels for 19%

profile of v2, /device:TPU:0, one launch (start us, length us, event | category | flops | bytes accessed | tf_op | source)
XLA Modules:
  0.0 58.1 jit_solution(10338217232567193844)
XLA Ops:
  0.7 1.1 %dynamic-slice_bitcast_fusion = (f32[528,128]{1,0:T(8,128)S(1)}, f32[528,128]{1,0:T(8,128)S(1)}) fusion(f32[1,1024,128]{2,1,0:T(8,128)} %param.8, s32[]{:T(128)S(6)} %select_n.17, f32[1,1024,128]{2,1,0:T(8,128)} %param.7), kind=kLoop, calls=%fused_computation.1 | loop fusion | bytes 1081348 | tf_op jit(solution)/shard_map/dynamic_slice | solution.py:538
  3.1 0.9 %collective-permute-done.got = f32[1056,128]{1,0:T(8,128)S(1)} collective-permute-done((f32[1056,128]{1,0:T(8,128)S(1)}, f32[1056,128]{1,0:T(8,128)S(1)}, u32[]{:S(2)}, u32[]{:S(2)}) %collective-permute-start) | collective-permute-done | bytes 540704 | tf_op jit(solution)/shard_map/ppermute | solution.py:540
  4.0 1.3 %shard_map.86 = (f32[544,128]{1,0:T(8,128)S(1)}, f32[544,128]{1,0:T(8,128)S(1)}, f32[528,128]{1,0:T(8,128)S(1)}, f32[528,128]{1,0:T(8,128)S(1)}, f32[264,128]{1,0:T(8,128)S(1)}, /*index=5*/f32[264,128]{1,0:T(8,128)S(1)}) custom-call(s32[9]{0:T(128)S(1)} %fusion.flags, f32[1024,128]{1,0:T(8,128)S(1)} %bitcast.10, f32[1024,128]{1,0:T(8,128)S(1)} %bitcast.11, ...), custom_call_target="tpu_custom_call" | custom-call | flops 16220160 | bytes 2703360 | tf_op jit(solution)/shard_map/pallas_call | solution.py:429
  5.3 3.0 %collective-permute-start.1 = (f32[264,128]{1,0:T(8,128)S(1)}, f32[264,128]{1,0:T(8,128)S(1)}, u32[]{:S(2)}, u32[]{:S(2)}) collective-permute-start(f32[264,128]{1,0:T(8,128)S(1)} %get-tuple-element.45), channel_id=1, source_target_pairs={{0,1},{1,2},{2,3},{3,0},{4,5},{5,6},{6,7},{7,4},{8,9},{9,10},{10,1... | collective-permute-start | bytes 405512 | tf_op jit(solution)/shard_map/ppermute | solution.py:546
  8.3 2.1 %collective-permute-start.2 = (f32[264,128]{1,0:T(8,128)S(1)}, f32[264,128]{1,0:T(8,128)S(1)}, u32[]{:S(2)}, u32[]{:S(2)}) collective-permute-start(f32[264,128]{1,0:T(8,128)S(1)} %get-tuple-element.46), channel_id=1, source_target_pairs={{1,0},{2,1},{3,2},{0,3},{5,4},{6,5},{7,6},{4,7},{9,8},{10,9},{11,1... | collective-permute-start | bytes 405512 | tf_op jit(solution)/shard_map/ppermute | solution.py:545
  11.0 4.2 %shard_map.87 = (f32[544,128]{1,0:T(8,128)S(1)}, f32[544,128]{1,0:T(8,128)S(1)}, f32[528,128]{1,0:T(8,128)S(1)}, f32[528,128]{1,0:T(8,128)S(1)}, f32[528,128]{1,...) custom-call(s32[9]{0:T(128)S(1)} %fusion.flags, ...), custom_call_target="tpu_custom_call" | custom-call | flops 16220160 | bytes 2703360 | tf_op jit(solution)/shard_map/pallas_call | solution.py:429
  15.3 1.2 %collective-permute-done.2.east = f32[264,128]{1,0:T(8,128)S(1)} collective-permute-done((f32[264,128]{1,0:T(8,128)S(1)}, f32[264,128]{1,0:T(8,128)S(1)}, u32[]{:S(2)}, u32[]{:S(2)}) %collective-permute-start.2) | collective-permute-done | bytes 135200 | tf_op jit(solution)/shard_map/ppermute | solution.py:545
  16.5 4.0 %shard_map.88 = (f32[528,128]{1,0:T(8,128)S(1)}, f32[528,128]{1,0:T(8,128)S(1)}, f32[528,128]{1,0:T(8,128)S(1)}, f32[528,128]{1,0:T(8,128)S(1)}, f32[528,128]{1,...) custom-call(s32[9]{0:T(128)S(1)} %fusion.flags, ...), custom_call_target="tpu_custom_call" | custom-call | flops 16220160 | bytes 2703360 | tf_op jit(solution)/shard_map/pallas_call | solution.py:429
  20.5 1.6 %collective-permute-start.4 = (f32[304,128]{1,0:T(8,128)S(1)}, f32[304,128]{1,0:T(8,128)S(1)}, u32[]{:S(2)}, u32[]{:S(2)}) collective-permute-start(f32[304,128]{1,0:T(8,128)S(1)} %get-tuple-element.61.d), channel_id=1, source_target_pairs={{0,16},{4,20},{8,24},{12,28},{16,0},{20,4},{24,8},{28,12},{1,17},{... | collective-permute-start | bytes 466952 | tf_op jit(solution)/shard_map/ppermute | solution.py:486
  22.1 1.5 %collective-permute-start.3 = (f32[296,128]{1,0:T(8,128)S(1)}, f32[296,128]{1,0:T(8,128)S(1)}, u32[]{:S(2)}, u32[]{:S(2)}) collective-permute-start(f32[296,128]{1,0:T(8,128)S(1)} %get-tuple-element.58.d), channel_id=1, source_target_pairs={{0,8},{4,12},{8,0},{12,4},{16,24},{20,28},{24,16},{28,20},{1,9},{5... | collective-permute-start | bytes 454664 | tf_op jit(solution)/shard_map/ppermute | solution.py:486
  23.6 2.4 %collective-permute-done.4.came = f32[304,128]{1,0:T(8,128)S(1)} collective-permute-done((f32[304,128]{1,0:T(8,128)S(1)}, f32[304,128]{1,0:T(8,128)S(1)}, u32[]{:S(2)}, u32[]{:S(2)}) %collective-permute-start.4) | collective-permute-done | bytes 155680 | tf_op jit(solution)/shard_map/ppermute | solution.py:486
  26.6 1.6 %collective-permute-start.6 = (f32[304,128]{1,0:T(8,128)S(1)}, f32[304,128]{1,0:T(8,128)S(1)}, u32[]{:S(2)}, u32[]{:S(2)}) collective-permute-start(f32[304,128]{1,0:T(8,128)S(1)} %get-tuple-element.64), channel_id=1, source_target_pairs={{0,8},{4,12},{8,0},{12,4},{16,24},{20,28},{24,16},{28,20},{1,9},{5... | collective-permute-start | bytes 466952 | tf_op jit(solution)/shard_map/ppermute | solution.py:486
  28.9 1.6 %collective-permute-start.5 = (f32[296,128]{1,0:T(8,128)S(1)}, f32[296,128]{1,0:T(8,128)S(1)}, u32[]{:S(2)}, u32[]{:S(2)}) collective-permute-start(f32[296,128]{1,0:T(8,128)S(1)} %get-tuple-element.63), channel_id=1, source_target_pairs={{0,16},{4,20},{8,24},{12,28},{16,0},{20,4},{24,8},{28,12},{1,17},{... | collective-permute-start | bytes 454664 | tf_op jit(solution)/shard_map/ppermute | solution.py:486
  30.5 3.7 %collective-permute-done.5.r_a = f32[296,128]{1,0:T(8,128)S(1)} collective-permute-done((f32[296,128]{1,0:T(8,128)S(1)}, f32[296,128]{1,0:T(8,128)S(1)}, u32[]{:S(2)}, u32[]{:S(2)}) %collective-permute-start.5) | collective-permute-done | bytes 151584 | tf_op jit(solution)/shard_map/ppermute | solution.py:486
  34.2 5.2 %shard_map.91 = (f32[512,128]{1,0:T(8,128)S(1)}, f32[512,128]{1,0:T(8,128)S(1)}, f32[256,128]{1,0:T(8,128)S(1)}, f32[256,128]{1,0:T(8,128)S(1)}, f32[256,128]{1,...) custom-call(s32[9]{0:T(128)S(1)} %fusion.flags, f32[296,128]{1,0:T(8,128)S(1)} %get-tuple-element.59.s_a, ...), custom_call_target="tpu_custom_call" | custom-call | flops 16220160 | bytes 2703360 | tf_op jit(solution)/shard_map/pallas_call | solution.py:429
  40.0 1.5 %collective-permute-start.8 = (f32[256,128]{1,0:T(8,128)S(1)}, f32[256,128]{1,0:T(8,128)S(1)}, u32[]{:S(2)}, u32[]{:S(2)}) collective-permute-start(f32[256,128]{1,0:T(8,128)S(1)} %get-tuple-element.79.d), channel_id=1, source_target_pairs={{0,16},{4,20},{8,24},{12,28},{16,0},{20,4},{24,8},{28,12},{1,17},{... | collective-permute-start | bytes 393224 | tf_op jit(solution)/shard_map/ppermute | solution.py:486
  41.5 2.9 %collective-permute-done.7.came = f32[256,128]{1,0:T(8,128)S(1)} collective-permute-done((f32[256,128]{1,0:T(8,128)S(1)}, f32[256,128]{1,0:T(8,128)S(1)}, u32[]{:S(2)}, u32[]{:S(2)}) %collective-permute-start.7) | collective-permute-done | bytes 131104 | tf_op jit(solution)/shard_map/ppermute | solution.py:486
  45.0 1.6 %collective-permute-start.9 = (f32[256,128]{1,0:T(8,128)S(1)}, f32[256,128]{1,0:T(8,128)S(1)}, u32[]{:S(2)}, u32[]{:S(2)}) collective-permute-start(f32[256,128]{1,0:T(8,128)S(1)} %get-tuple-element.81), channel_id=1, source_target_pairs={{0,16},{4,20},{8,24},{12,28},{16,0},{20,4},{24,8},{28,12},{1,17},{... | collective-permute-start | bytes 393224 | tf_op jit(solution)/shard_map/ppermute | solution.py:486
  48.1 2.0 %collective-permute-done.9.r_a = f32[256,128]{1,0:T(8,128)S(1)} collective-permute-done((f32[256,128]{1,0:T(8,128)S(1)}, f32[256,128]{1,0:T(8,128)S(1)}, u32[]{:S(2)}, u32[]{:S(2)}) %collective-permute-start.9) | collective-permute-done | bytes 131104 | tf_op jit(solution)/shard_map/ppermute | solution.py:486
  50.1 2.3 %collective-permute-done.10.r_b = f32[256,128]{1,0:T(8,128)S(1)} collective-permute-done((f32[256,128]{1,0:T(8,128)S(1)}, f32[256,128]{1,0:T(8,128)S(1)}, u32[]{:S(2)}, u32[]{:S(2)}) %collective-permute-start.10) | collective-permute-done | bytes 131104 | tf_op jit(solution)/shard_map/ppermute | solution.py:486
  53.0 1.3 %shard_map.97.rest_0_ = f32[1024,128]{1,0:T(8,128)} custom-call(s32[9]{0:T(128)S(1)} %fusion.flags, f32[512,128]{1,0:T(8,128)S(1)} %get-tuple-element.87.piece), custom_call_target="tpu_custom_call" | custom-call | bytes 524288 | tf_op jit(solution)/shard_map/pallas_call | solution.py:415
  54.3 1.3 %shard_map.95.rest_0_ = f32[1024,128]{1,0:T(8,128)} custom-call(s32[9]{0:T(128)S(1)} %fusion.flags, f32[512,128]{1,0:T(8,128)S(1)} %get-tuple-element.85.piece), custom_call_target="tpu_custom_call" | custom-call | bytes 524288 | tf_op jit(solution)/shard_map/pallas_call | solution.py:415
  55.5 1.3 %shard_map.98 = f32[1024,128]{1,0:T(8,128)} custom-call(s32[9]{0:T(128)S(1)} %fusion.flags, f32[512,128]{1,0:T(8,128)S(1)} %collective-permute-done.12.piece, f32[1024,128]{1,0:T(8,128)} %shard_map.97.rest_0_), custom_call_target="tpu_custom_call", output_to_operand_aliasing={{}: (2, {})} | custom-call | bytes 524288 | tf_op jit(solution)/shard_map/pallas_call | solution.py:415
  56.8 1.3 %shard_map.96 = f32[1024,128]{1,0:T(8,128)} custom-call(s32[9]{0:T(128)S(1)} %fusion.flags, f32[512,128]{1,0:T(8,128)S(1)} %collective-permute-done.11.piece, f32[1024,128]{1,0:T(8,128)} %shard_map.95.rest_0_), custom_call_target="tpu_custom_call", output_to_operand_aliasing={{}: (2, {})} | custom-call | bytes 524288 | tf_op jit(solution)/shard_map/pallas_call | solution.py:415
  (30 shorter events, 6.8 us)
Async XLA Ops:
  0.6 3.3 %copy-start.2 = (f32[1,1024,128]{2,1,0:T(8,128)S(1)}, f32[1,1024,128]{2,1,0:T(8,128)}, u32[]{:S(2)}) copy-start(f32[1,1024,128]{2,1,0:T(8,128)} %param.8) | copy-start | bytes 1572868
  1.8 2.2 %copy-start = (s32[1024,128]{1,0:T(8,128)S(1)}, s32[1024,128]{1,0:T(8,128)}, u32[]{:S(2)}) copy-start(s32[1024,128]{1,0:T(8,128)} %region.3) | copy-start | bytes 1572868
  1.8 2.2 %copy-start.1 = (f32[1,1024,128]{2,1,0:T(8,128)S(1)}, f32[1,1024,128]{2,1,0:T(8,128)}, u32[]{:S(2)}) copy-start(f32[1,1024,128]{2,1,0:T(8,128)} %param.7) | copy-start | bytes 1572868
  1.9 2.1 %collective-permute-start = (f32[1056,128]{1,0:T(8,128)S(1)}, f32[1056,128]{1,0:T(8,128)S(1)}, u32[]{:S(2)}, u32[]{:S(2)}) collective-permute-start(f32[1056,128]{1,0:T(8,128)S(1)} %pad_maximum_fusion), channel_id=1, source_target_pairs={{0,4},{4,0},{8,12},{12,8},{16,20},{20,16},{24,28},{28,24},{1,5},{5... | collective-permute-start | bytes 1622024 | tf_op jit(solution)/shard_map/ppermute | solution.py:540
  5.3 10.0 %collective-permute-start.1 = (f32[264,128]{1,0:T(8,128)S(1)}, f32[264,128]{1,0:T(8,128)S(1)}, u32[]{:S(2)}, u32[]{:S(2)}) collective-permute-start(f32[264,128]{1,0:T(8,128)S(1)} %get-tuple-element.45), channel_id=1, source_target_pairs={{0,1},{1,2},{2,3},{3,0},{4,5},{5,6},{6,7},{7,4},{8,9},{9,10},{10,1... | collective-permute-start | bytes 405512 | tf_op jit(solution)/shard_map/ppermute | solution.py:546
  8.3 8.3 %collective-permute-start.2 = (f32[264,128]{1,0:T(8,128)S(1)}, f32[264,128]{1,0:T(8,128)S(1)}, u32[]{:S(2)}, u32[]{:S(2)}) collective-permute-start(f32[264,128]{1,0:T(8,128)S(1)} %get-tuple-element.46), channel_id=1, source_target_pairs={{1,0},{2,1},{3,2},{0,3},{5,4},{6,5},{7,6},{4,7},{9,8},{10,9},{11,1... | collective-permute-start | bytes 405512 | tf_op jit(solution)/shard_map/ppermute | solution.py:545
  10.4 0.7 %copy-start.3 = (f32[8]{0:T(128)S(1)}, f32[8]{0:T(128)}, u32[]{:S(2)}) copy-start(f32[8]{0:T(128)} %nu_tab.3) | copy-start | bytes 100
  10.4 0.7 %copy-start.4 = (f32[8]{0:T(128)S(1)}, f32[8]{0:T(128)}, u32[]{:S(2)}) copy-start(f32[8]{0:T(128)} %sat_tab.3) | copy-start | bytes 100
  10.4 0.7 %copy-start.5 = (f32[8]{0:T(128)S(1)}, f32[8]{0:T(128)}, u32[]{:S(2)}) copy-start(f32[8]{0:T(128)} %mob_tab.3) | copy-start | bytes 100
  20.5 5.4 %collective-permute-start.4 = (f32[304,128]{1,0:T(8,128)S(1)}, f32[304,128]{1,0:T(8,128)S(1)}, u32[]{:S(2)}, u32[]{:S(2)}) collective-permute-start(f32[304,128]{1,0:T(8,128)S(1)} %get-tuple-element.61.d), channel_id=1, source_target_pairs={{0,16},{4,20},{8,24},{12,28},{16,0},{20,4},{24,8},{28,12},{1,17},{... | collective-permute-start | bytes 466952 | tf_op jit(solution)/shard_map/ppermute | solution.py:486
  22.1 6.1 %collective-permute-start.3 = (f32[296,128]{1,0:T(8,128)S(1)}, f32[296,128]{1,0:T(8,128)S(1)}, u32[]{:S(2)}, u32[]{:S(2)}) collective-permute-start(f32[296,128]{1,0:T(8,128)S(1)} %get-tuple-element.58.d), channel_id=1, source_target_pairs={{0,8},{4,12},{8,0},{12,4},{16,24},{20,28},{24,16},{28,20},{1,9},{5... | collective-permute-start | bytes 454664 | tf_op jit(solution)/shard_map/ppermute | solution.py:486
  26.6 7.5 %collective-permute-start.6 = (f32[304,128]{1,0:T(8,128)S(1)}, f32[304,128]{1,0:T(8,128)S(1)}, u32[]{:S(2)}, u32[]{:S(2)}) collective-permute-start(f32[304,128]{1,0:T(8,128)S(1)} %get-tuple-element.64), channel_id=1, source_target_pairs={{0,8},{4,12},{8,0},{12,4},{16,24},{20,28},{24,16},{28,20},{1,9},{5... | collective-permute-start | bytes 466952 | tf_op jit(solution)/shard_map/ppermute | solution.py:486
  28.9 5.3 %collective-permute-start.5 = (f32[296,128]{1,0:T(8,128)S(1)}, f32[296,128]{1,0:T(8,128)S(1)}, u32[]{:S(2)}, u32[]{:S(2)}) collective-permute-start(f32[296,128]{1,0:T(8,128)S(1)} %get-tuple-element.63), channel_id=1, source_target_pairs={{0,16},{4,20},{8,24},{12,28},{16,0},{20,4},{24,8},{28,12},{1,17},{... | collective-permute-start | bytes 454664 | tf_op jit(solution)/shard_map/ppermute | solution.py:486
  39.3 5.0 %collective-permute-start.7 = (f32[256,128]{1,0:T(8,128)S(1)}, f32[256,128]{1,0:T(8,128)S(1)}, u32[]{:S(2)}, u32[]{:S(2)}) collective-permute-start(f32[256,128]{1,0:T(8,128)S(1)} %get-tuple-element.76.d), channel_id=1, source_target_pairs={{0,8},{4,12},{8,0},{12,4},{16,24},{20,28},{24,16},{28,20},{1,9},{5... | collective-permute-start | bytes 393224 | tf_op jit(solution)/shard_map/ppermute | solution.py:486
  40.0 6.7 %collective-permute-start.8 = (f32[256,128]{1,0:T(8,128)S(1)}, f32[256,128]{1,0:T(8,128)S(1)}, u32[]{:S(2)}, u32[]{:S(2)}) collective-permute-start(f32[256,128]{1,0:T(8,128)S(1)} %get-tuple-element.79.d), channel_id=1, source_target_pairs={{0,16},{4,20},{8,24},{12,28},{16,0},{20,4},{24,8},{28,12},{1,17},{... | collective-permute-start | bytes 393224 | tf_op jit(solution)/shard_map/ppermute | solution.py:486
  45.0 5.0 %collective-permute-start.9 = (f32[256,128]{1,0:T(8,128)S(1)}, f32[256,128]{1,0:T(8,128)S(1)}, u32[]{:S(2)}, u32[]{:S(2)}) collective-permute-start(f32[256,128]{1,0:T(8,128)S(1)} %get-tuple-element.81), channel_id=1, source_target_pairs={{0,16},{4,20},{8,24},{12,28},{16,0},{20,4},{24,8},{28,12},{1,17},{... | collective-permute-start | bytes 393224 | tf_op jit(solution)/shard_map/ppermute | solution.py:486
  47.3 5.0 %collective-permute-start.10 = (f32[256,128]{1,0:T(8,128)S(1)}, f32[256,128]{1,0:T(8,128)S(1)}, u32[]{:S(2)}, u32[]{:S(2)}) collective-permute-start(f32[256,128]{1,0:T(8,128)S(1)} %get-tuple-element.82), channel_id=1, source_target_pairs={{0,8},{4,12},{8,0},{12,4},{16,24},{20,28},{24,16},{28,20},{1,9},{5... | collective-permute-start | bytes 393224 | tf_op jit(solution)/shard_map/ppermute | solution.py:486
  48.1 7.4 %collective-permute-start.12 = (f32[512,128]{1,0:T(8,128)S(1)}, f32[512,128]{1,0:T(8,128)S(1)}, u32[]{:S(2)}, u32[]{:S(2)}) collective-permute-start(f32[512,128]{1,0:T(8,128)S(1)} %get-tuple-element.86), channel_id=1, source_target_pairs={{0,4},{4,0},{8,12},{12,8},{16,20},{20,16},{24,28},{28,24},{1,5},{5... | collective-permute-start | bytes 786440 | tf_op jit(solution)/shard_map/ppermute | solution.py:568
  52.9 3.9 %collective-permute-start.11 = (f32[512,128]{1,0:T(8,128)S(1)}, f32[512,128]{1,0:T(8,128)S(1)}, u32[]{:S(2)}, u32[]{:S(2)}) collective-permute-start(f32[512,128]{1,0:T(8,128)S(1)} %get-tuple-element.84), channel_id=1, source_target_pairs={{0,4},{4,0},{8,12},{12,8},{16,20},{20,16},{24,28},{28,24},{1,5},{5... | collective-permute-start | bytes 786440 | tf_op jit(solution)/shard_map/ppermute | solution.py:572

commit v3 on v2

--- a/solution.py
+++ b/solution.py
@@ -15,7 +15,7 @@
 ID_HALO = HALO - 1
 REACH = 2 * STEPS
 PAD = 8
-CHUNK = 88
+CHUNK = 96
 FOLD = 8
 VMEM = pl.BlockSpec(memory_space=pltpu.VMEM)
 FLAGS = 3
@@ -40,10 +40,16 @@
     return hit
 
 
+def pieces(rows):
+    tiles = rows // 8
+    count = -(-tiles // (CHUNK // 8))
+    edges = [8 * (tiles * c // count) for c in range(count + 1)]
+    return [(low, high - low) for low, high in zip(edges[:-1], edges[1:])]
+
+
 def over_chunks(rows, body):
-    chunk = max(n for n in range(8, CHUNK + 1, 8) if rows % n == 0)
-    for base in range(0, rows, chunk):
-        body(base, chunk)
+    for base, n in pieces(rows):
+        body(base, n)
 
 
 def aligned(at):
@@ -63,58 +69,60 @@
     return base + slope, slope, mobile * 0.5, gain
 
 
-def fine_steps(units, rows, work):
-    chunk = max(n for n in range(8, CHUNK + 1, 8) if rows % n == 0)
-    chunks = rows // chunk
+def fine_steps(units, rows, work, off=0):
+    chunks = pieces(rows)
     for step in range(STEPS):
         moved = {}
-        for turn in range(chunks + 4):
+        for turn in range(len(chunks) + 4):
             for u, (bufs, top, slope, mob, drive) in enumerate(units):
                 old, new = bufs[step], bufs[step + 1]
                 nu, east, flow, face = work[4 * u : 4 * u + 4]
+
+                def place(c):
+                    if not 0 <= c < len(chunks):
+                        return None
+                    base, n = chunks[c]
+                    return pl.ds(base + PAD, n), pl.ds(base + PAD - 1, n), pl.ds(base + PAD + 1, n), pl.ds(aligned(off + base), n)
+
                 c = turn - 3
-                if 0 <= c < chunks:
-                    at = c * chunk + PAD
-                    nu0 = nu[pl.ds(at, chunk), :]
-                    out = (nu0 + moved.pop((u, 3, c))) * east[pl.ds(at, chunk), :]
-                    flow[pl.ds(at, chunk), :] = out
+                if spot := place(c):
+                    at, above, _, _ = spot
+                    nu0 = nu[at, :]
+                    out = (nu0 + moved.pop((u, 3, c))) * east[at, :]
+                    flow[at, :] = out
                     moved[u, 4, c] = roll(out, 1)
-                    face[pl.ds(at, chunk), :] = (nu0 + nu[pl.ds(at - 1, chunk), :]) * (
-                        old[pl.ds(at, chunk), :] - old[pl.ds(at - 1, chunk), :]
-                    )
-                    if c == chunks - 1:
-                        at = PAD + rows
-                        nu[at : at + 1, :] = nu[at - 1 : at, :]
-                        face[pl.ds(at, 8), :] = (nu[pl.ds(at, 8), :] + nu[pl.ds(at - 1, 8), :]) * (
-                            old[pl.ds(at, 8), :] - old[pl.ds(at - 1, 8), :]
-                        )
+                    face[at, :] = (nu0 + nu[above, :]) * (old[at, :] - old[above, :])
+                    if c == len(chunks) - 1:
+                        end = PAD + rows
+                        nu[end : end + 1, :] = nu[end - 1 : end, :]
+                        at, above = pl.ds(end, 8), pl.ds(end - 1, 8)
+                        face[at, :] = (nu[at, :] + nu[above, :]) * (old[at, :] - old[above, :])
                 c = turn - 4
-                if 0 <= c < chunks:
-                    at, here_rows = c * chunk + PAD, pl.ds(c * chunk, chunk)
-                    total = flow[pl.ds(at, chunk), :] - moved.pop((u, 4, c))
-                    total = total + (face[pl.ds(at + 1, chunk), :] - face[pl.ds(at, chunk), :])
-                    total = total + drive[here_rows, :]
-                    new[pl.ds(at, chunk), :] = old[pl.ds(at, chunk), :] + mob[here_rows, :] * total
+                if spot := place(c):
+                    at, _, below, coef = spot
+                    total = flow[at, :] - moved.pop((u, 4, c))
+                    total = total + (face[below, :] - face[at, :])
+                    new[at, :] = old[at, :] + mob[coef, :] * (total + drive[coef, :])
                 c = turn - 2
-                if 0 <= c < chunks:
-                    at, here_rows = c * chunk + PAD, pl.ds(c * chunk, chunk)
-                    dr = old[pl.ds(at + 1, chunk), :] - old[pl.ds(at - 1, chunk), :]
-                    dt = east[pl.ds(at, chunk), :] + moved.pop((u, 2, c))
+                if spot := place(c):
+                    at, above, below, coef = spot
+                    dr = old[below, :] - old[above, :]
+                    dt = east[at, :] + moved.pop((u, 2, c))
                     bottom = 1.0 + (dr * dr + dt * dt)
-                    out = top[here_rows, :] - slope[here_rows, :] / bottom
-                    nu[pl.ds(at, chunk), :] = out
+                    out = top[coef, :] - slope[coef, :] / bottom
+                    nu[at, :] = out
                     if c == 0:
                         nu[PAD - 1 : PAD, :] = nu[PAD : PAD + 1, :]
                     moved[u, 3, c] = roll(out, -1)
                 c = turn - 1
-                if 0 <= c < chunks:
-                    at = c * chunk + PAD
-                    out = moved.pop((u, 1, c)) - old[pl.ds(at, chunk), :]
-                    east[pl.ds(at, chunk), :] = out
+                if spot := place(c):
+                    at = spot[0]
+                    out = moved.pop((u, 1, c)) - old[at, :]
+                    east[at, :] = out
                     moved[u, 2, c] = roll(out, 1)
                 c = turn
-                if 0 <= c < chunks:
-                    moved[u, 1, c] = roll(old[pl.ds(c * chunk + PAD, chunk), :], -1)
+                if spot := place(c):
+                    moved[u, 1, c] = roll(old[spot[0], :], -1)
 
 
 def clear_pads(ref, rows):
@@ -122,7 +130,7 @@
     ref[PAD + rows : rows + 2 * PAD, :] = jnp.zeros((PAD, ref.shape[1]), jnp.float32)
 
 
-def pack_kernel(rows, start, flags, own_a, own_j, got, region, a0, a1, j0, j1, to_west, to_east):
+def pack_kernel(rows, start, flags, own_a, own_j, got, region, a0, a1, j0, j1, kind, to_west, to_east):
     lanes = a0.shape[1]
     q, both, tall = lanes // 4, HALO + J_HALO, rows // 2
     mine = flags[0] == 0
@@ -146,6 +154,7 @@
             j0[pl.ds(base, n), :] = j_0
             j1[pl.ds(base, n), :] = j_1
             ids = region[src, :].astype(jnp.float32)
+            kind[pl.ds(base, n), :] = ids
             for s, (a, j) in enumerate(((a_0, j_0), (a_1, j_1))):
                 at = (2 * s + 2) * q - HALO - k * both
                 west = jnp.where(inside(lane, (at, at + HALO)), roll(a, at), west)
@@ -184,31 +193,30 @@
 
 
 def main_kernel(
-    rows, start, flags, nu_tab, sat_tab, mob_tab, region, a0, a1, j0, j1,
+    rows, flags, nu_tab, sat_tab, mob_tab, kind, a0, a1, j0, j1,
     f0, f1, top, slope, mob, gain, a_own, j_own, id_own, b0, c0, b1, c1, *work,
 ):
-    first = flags[0] * start
     for ref in (b0, c0, b1, c1):
         clear_pads(ref, rows)
 
     def body(base, n):
         lane = lanes_of(n, a0.shape[1])
-        ids = region[pl.ds(aligned(first + base), n), :]
         here, padded = pl.ds(base, n), pl.ds(base + PAD, n)
-        top[here, :], slope[here, :], mob[here, :], gain[here, :] = coefficients(ids, nu_tab, sat_tab, mob_tab)
+        top[here, :], slope[here, :], mob[here, :], gain[here, :] = coefficients(
+            kind[here, :].astype(jnp.int32), nu_tab, sat_tab, mob_tab
+        )
         a_own[here, :] = own_part(a0[padded, :], a1[padded, :], lane)
         j_own[here, :] = own_part(j0[here, :], j1[here, :], lane)
-        ids = ids.astype(jnp.float32)
-        id_own[here, :] = own_part(ids, ids, lane)
+        id_own[here, :] = own_part(kind[here, :], kind[here, :], lane)
 
     over_chunks(rows, body)
     fine_steps((((a0, b0, c0, f0), top, slope, mob, j0), ((a1, b1, c1, f1), top, slope, mob, j1)), rows, work)
 
 
 def strip_kernel(
-    rows, cut, tail_cut, flags, nu_tab, sat_tab, mob_tab, west, east, a_own, j_own, id_own,
+    rows, span, flags, nu_tab, sat_tab, mob_tab, west, east, a_own, j_own, id_own,
     a0, a1, f0, f1, gain,
-    top_s, slope_s, mob_s, gain_s, j_s, corr, corr_s, d_a, d_b, g_a, g_b, a_s, b_s, c_s, d_s, folded, *work,
+    top_s, slope_s, mob_s, gain_s, j_s, corr, corr_s, d_a, d_b, a_s, b_s, c_s, d_s, d_m, *work,
 ):
     lanes = a0.shape[1]
     q, both, tall = lanes // 4, HALO + J_HALO, rows // 2
@@ -258,23 +266,30 @@
         end1 = merge_edges(f1[padded, :], strip, 1, lane)
         change = end0 - g * a0[padded, :]
         corr[here, :] = change
-        out = jnp.where(last, end1, g * change + end1 - g * a1[padded, :])
-        to, g_to, at = (d_a, g_a, base) if base < cut else (d_b, g_b, base - cut)
-        to[pl.ds(at, n), :] = out
-        g_to[pl.ds(at, n), :] = g
+        d_m[here, :] = jnp.where(last, end1, g * change + end1 - g * a1[padded, :])
 
     over_chunks(rows, finish)
-    for src, part_a, part_b in ((d_s, d_a, d_b), (gain_s, g_a, g_b)):
-        fold(src, folded, rows)
-        part_a[cut : cut + tail_cut, :] = folded[0:tail_cut, :]
-        part_b[rows - cut : rows - cut + folded.shape[0] - tail_cut, :] = folded[tail_cut:, :]
+    for p, out in enumerate((d_a, d_b)):
+        off = part_start(flags, p, rows)
+        out[0:span, :] = d_m[pl.ds(off, span), :]
+        fold(d_s, off, out, span, span)
+
+
+def part_start(flags, p, rows):
+    half = rows - 2 * PAD
+    return aligned(PAD * flags[0] + p * (half // 2 - PAD))
+
+
+def fold_kernel(rows, span, flags, gain_s, g_a, g_b):
+    for p, out in enumerate((g_a, g_b)):
+        fold(gain_s, part_start(flags, p, rows), out, span, 0)
 
 
 def fold_tiles(rows):
     return -(-(rows // 8) // FOLD)
 
 
-def fold(src, dst, rows):
+def fold(src, off, dst, rows, to):
     lanes = src.shape[1]
     q, width = lanes // 4, lanes // FOLD
     lane = lanes_of(8, lanes)
@@ -285,11 +300,11 @@
             t = k * tiles + r
             if 8 * t >= rows:
                 continue
-            x = src[8 * t : 8 * t + 8, :]
+            x = src[pl.ds(aligned(off + 8 * t), 8), :]
             at_w, at_e = width * k, width * k + width // 2
             out = jnp.where(inside(lane, (at_w, at_w + REACH)), roll(x, at_w - (HALO - REACH)), out)
             out = jnp.where(inside(lane, (at_e, at_e + REACH)), roll(x, at_e - (2 * q - HALO)), out)
-        dst[8 * r : 8 * r + 8, :] = out
+        dst[to + 8 * r : to + 8 * r + 8, :] = out
 
 
 def unfold(src, dst, rows):
@@ -309,119 +324,128 @@
 
 
 def second_kernel(
-    rows, half, cut, tail_cut, flags, s_a, s_b, r_a, r_b, corr, corr_s, gain, top, slope, mob, j0, j1,
+    rows, span, p, flags, sums, came, corr, corr_s, gain, top, slope, mob, j0, j1,
     gain_s, top_s, slope_s, mob_s, j_s,
-    end_own, end_send, d_a, d_b, g_a, g_b, corr_out,
-    a0, a1, a_s, b0, b1, b_s, c0, c1, c_s, spread, folded, *work,
+    end_own, end_send, d_out, corr_out, a0, a1, a_s, b0, b1, b_s, c0, c1, c_s, spread, folded, *work,
 ):
     lanes = a0.shape[1]
     q = lanes // 4
     h = flags[0]
     last = flags[1] == 1
+    off = part_start(flags, p, rows)
     for ref in (a0, a1, a_s, b0, b1, b_s, c0, c1, c_s):
-        clear_pads(ref, rows)
-    folded[0:tail_cut, :] = s_a[cut:, :] + r_a[cut:, :]
-    folded[tail_cut:, :] = s_b[rows - cut :, :] + r_b[rows - cut :, :]
-    unfold(folded, spread, rows)
+        clear_pads(ref, span)
+    folded[...] = sums[span:, :] + came[span:, :]
+    unfold(folded, spread, span)
 
     def build(base, n):
         lane = lanes_of(n, lanes)
-        here, padded = pl.ds(base, n), pl.ds(base + PAD, n)
-        part, came, at = (s_a, r_a, base) if base < cut else (s_b, r_b, base - cut)
-        s = part[pl.ds(at, n), :] + came[pl.ds(at, n), :]
+        here, padded, slab = pl.ds(base, n), pl.ds(base + PAD, n), pl.ds(aligned(off + base), n)
+        s = sums[here, :] + came[here, :]
         a0[padded, :] = s
-        a1[padded, :] = gain[here, :] * s + corr[here, :]
+        a1[padded, :] = gain[slab, :] * s + corr[slab, :]
         strip = spread[here, :]
         strip = jnp.where(inside(lane, (HALO, q)), roll(s, HALO), strip)
         strip = jnp.where(inside(lane, (q, 2 * q - HALO)), roll(s, 2 * q - HALO), strip)
-        other = roll(gain_s[here, :] * strip + corr_s[here, :], 2 * q)
+        other = roll(gain_s[slab, :] * strip + corr_s[slab, :], 2 * q)
         a_s[padded, :] = jnp.where(lane < 2 * q, strip, other)
 
-    over_chunks(rows, build)
+    over_chunks(span, build)
     fine_steps(
         (
             ((a0, b0, c0, b0), top, slope, mob, j0),
             ((a1, b1, c1, b1), top, slope, mob, j1),
             ((a_s, b_s, c_s, b_s), top_s, slope_s, mob_s, j_s),
         ),
-        rows,
+        span,
         work,
+        off,
     )
 
     def finish(base, n):
         lane = lanes_of(n, lanes)
         here = pl.ds(base, n)
-        at = aligned(base + h * (rows - half))
-        inner, padded = pl.ds(at, n), pl.ds(at + PAD, n)
+        at = PAD * (h + p) + base
+        padded, slab = pl.ds(aligned(at + PAD), n), pl.ds(aligned(off + at), n)
         strip = b_s[padded, :]
         end0 = merge_edges(b0[padded, :], strip, 0, lane)
         end1 = merge_edges(b1[padded, :], strip, 1, lane)
         end_own[here, :] = jnp.where(h == 0, end0, end1) * 2.0
         end_send[here, :] = jnp.where(h == 0, end1, end0) * 2.0
-        g = gain[inner, :]
+        g = gain[slab, :]
         change = end0 - g * a0[padded, :]
         corr_out[here, :] = change * 2.0
-        d_to, g_to, to = (d_a, g_a, base) if base < half // 2 else (d_b, g_b, base - half // 2)
-        d_to[pl.ds(to, n), :] = jnp.where(last, end1, g * change + end1 - g * a1[padded, :]) * 2.0
-        g_to[pl.ds(to, n), :] = g
-
-    over_chunks(half, finish)
-
-
-def stage_kernel(order, flags, g, d, came, out, passed):
+        d_out[here, :] = jnp.where(last, end1, g * change + end1 - g * a1[padded, :]) * 2.0
+
+    over_chunks(span - 2 * PAD, finish)
+
+
+def own_start(flags, p, rows):
+    return aligned(part_start(flags, p, rows) + PAD * (flags[0] + p))
+
+
+def stage_kernel(rows, p, flags, gain, d, came, *rest):
+    out, passed = rest[-2:]
+    tail = rest[0].shape[0] if len(rest) == 3 else 0
+    body_rows = d.shape[0] - tail
+    off = part_start(flags, p, rows) if tail else own_start(flags, p, rows)
+
+    def weight(e, square, fourth):
+        value = jnp.where(e % 2 == 1, square, 1.0) * jnp.where(e >= 2, fourth, 1.0)
+        return jnp.where(e < 0, 0.0, value)
+
+    def one(here, g):
+        square = g * g
+        fourth = square * square
+        mine, its = d[here, :], came[here, :]
+        at = FLAGS + 3 * p
+        out[here, :] = weight(flags[FLAGS - 1], square, fourth) * mine + weight(flags[at], square, fourth) * its
+        passed[here, :] = weight(flags[at + 1], square, fourth) * mine + weight(flags[at + 2], square, fourth) * its
+
+    over_chunks(body_rows, lambda base, n: one(pl.ds(base, n), gain[pl.ds(aligned(off + base), n), :]))
+    if tail:
+        one(pl.ds(body_rows, tail), rest[0][...])
+
+
+def last_kernel(rows, p, flags, sums, came, gain, corr, own, send):
+    h = flags[0]
+    off = own_start(flags, p, rows)
+
     def body(base, n):
         here = pl.ds(base, n)
-        gain = g[here, :]
-        square = gain * gain
-        fourth = square * square
-
-        def weight(e):
-            value = jnp.where(e % 2 == 1, square, 1.0) * jnp.where(e >= 2, fourth, 1.0)
-            return jnp.where(e < 0, 0.0, value)
-
-        mine, its = d[here, :], came[here, :]
-        at = FLAGS + 3 * order
-        out[here, :] = weight(flags[FLAGS - 1]) * mine + weight(flags[at]) * its
-        passed[here, :] = weight(flags[at + 1]) * mine + weight(flags[at + 2]) * its
-
-    over_chunks(d.shape[0], body)
-
-
-def last_kernel(flags, s_a, s_b, r_a, r_b, g_a, g_b, corr, own, send):
-    h = flags[0]
-    tall = s_a.shape[0]
-    for k, (s, r, g) in enumerate(((s_a, r_a, g_a), (s_b, r_b, g_b))):
-
-        def body(base, n, k=k, s=s, r=r, g=g):
-            here, there = pl.ds(base, n), pl.ds(base + k * tall, n)
-            new0 = s[here, :] + r[here, :]
-            new1 = g[here, :] * new0 + corr[there, :]
-            own[there, :] = jnp.where(h == 0, new0, new1)
-            send[there, :] = jnp.where(h == 0, new1, new0)
-
-        over_chunks(tall, body)
-
-
-def put_kernel(half, other, flags, piece, *rest):
-    out, sem = rest[-2:]
-    side = 1 - flags[0] if other else flags[0]
-    copy = pltpu.make_async_copy(piece, out.at[pl.ds(aligned(side * half), half), :], sem)
-    copy.start()
-    copy.wait()
-
-
-def put(half, flags, piece, into=None):
+        new0 = sums[here, :] + came[here, :]
+        new1 = gain[pl.ds(aligned(off + base), n), :] * new0 + corr[here, :]
+        own[here, :] = jnp.where(h == 0, new0, new1)
+        send[here, :] = jnp.where(h == 0, new1, new0)
+
+    over_chunks(sums.shape[0], body)
+
+
+def put_kernel(half, places, flags, *refs):
+    out, sems = refs[-2:]
+    copies = []
+    for i, (other, p) in enumerate(places):
+        side = 1 - flags[0] if other else flags[0]
+        to = out.at[pl.ds(aligned(side * half + p * (half // 2)), half // 2), :]
+        copies.append(pltpu.make_async_copy(refs[i], to, sems.at[i]))
+        copies[-1].start()
+    for copy in copies:
+        copy.wait()
+
+
+def put(half, places, flags, parts, into=None):
     anywhere = pl.BlockSpec(memory_space=pl.ANY)
+    count = len(parts)
     return pl.pallas_call(
-        functools.partial(put_kernel, half, into is not None),
-        out_shape=jax.ShapeDtypeStruct((2 * half, piece.shape[1]), jnp.float32),
-        in_specs=[SMEM, VMEM] + ([anywhere] if into is not None else []),
+        functools.partial(put_kernel, half, places),
+        out_shape=jax.ShapeDtypeStruct((2 * half, parts[0].shape[1]), jnp.float32),
+        in_specs=[SMEM] + [VMEM] * count + ([anywhere] if into is not None else []),
         out_specs=anywhere,
-        scratch_shapes=[pltpu.SemaphoreType.DMA],
-        input_output_aliases={2: 0} if into is not None else {},
+        scratch_shapes=[pltpu.SemaphoreType.DMA((count,))],
+        input_output_aliases={count + 1: 0} if into is not None else {},
         compiler_params=PARAMS,
-        cost_estimate=pl.CostEstimate(flops=0, bytes_accessed=piece.size * 8, transcendentals=0),
-    )(flags, piece, *(() if into is None else (into,)))
+        cost_estimate=pl.CostEstimate(flops=0, bytes_accessed=count * parts[0].size * 8, transcendentals=0),
+    )(flags, *parts, *(() if into is None else (into,)))
 
 
 def call(kernel, outs, scratch=(), smem=1, cost=None):
@@ -486,17 +510,24 @@
     return lax.ppermute(value, "tm", [(i, i ^ (2 << bit)) for i in range(count)])
 
 
-def scan(parts, gains, flags, chip, chips, count):
+def scan(parts, gain, folds, rows, flags, chip, chips, count):
     own, orders = scan_plan(chips)
     if len(orders[0]) == 2:
         arrived = [exchange(d, order[0][0], count) for d, order in zip(parts, orders)]
         mid = [
-            call(functools.partial(stage_kernel, p), (d.shape, d.shape))(flags, g, d, r)
-            for p, (d, g, r) in enumerate(zip(parts, gains, arrived))
+            call(functools.partial(stage_kernel, rows, p), (d.shape, d.shape))(flags, gain, d, r, *fold)
+            for p, (d, r, fold) in enumerate(zip(parts, arrived, folds))
         ]
         came = [exchange(passed, order[1][0], count) for (_, passed), order in zip(mid, orders)]
         return [out for out, _ in mid], came
-    squares = [g * g for g in gains]
+    squares = []
+    for p, (d, fold) in enumerate(zip(parts, folds)):
+        plain = d.shape[0] - sum(f.shape[0] for f in fold)
+        off = PAD * flags[0] + p * ((rows - 2 * PAD) // 2 - PAD)
+        if not fold:
+            off = off + PAD * (flags[0] + p)
+        g = jnp.concatenate([lax.dynamic_slice(gain, (off, 0), (plain, d.shape[1])), *fold], axis=0)
+        squares.append(g * g)
     sums = [power(sq, own, chip) * d for sq, d in zip(squares, parts)]
     passed = list(parts)
     for stage in range(len(orders[0])):
@@ -539,38 +570,46 @@
     )
     got = lax.ppermute(send, "tm", partner)
     message = (rows // 2, lanes)
-    a0, a1, j0, j1, to_west, to_east = call(
-        functools.partial(pack_kernel, rows, start), (padded, padded, slab, slab, message, message), cost=cost
+    a0, a1, j0, j1, kind, to_west, to_east = call(
+        functools.partial(pack_kernel, rows, start), (padded, padded, slab, slab, slab, message, message), cost=cost
     )(flags, potential, driver, got, region)
     from_east = lax.ppermute(to_west, "space", [((i + 1) % spaces, i) for i in range(spaces)])
     from_west = lax.ppermute(to_east, "space", [(i, (i + 1) % spaces) for i in range(spaces)])
     f0, f1, top, slope, mob, gain, a_own, j_own, id_own = call(
-        functools.partial(main_kernel, rows, start),
-        (padded, padded) + (slab,) * 7, (padded,) * 12, smem=4, cost=cost,
-    )(flags, *tables, region, a0, a1, j0, j1)
-
-    tail = 8 * fold_tiles(rows)
-    cut, tail_cut = rows // 2, 8 * (tail // 16)
-    part_a, part_b = (cut + tail_cut, lanes), (rows - cut + tail - tail_cut, lanes)
-    top_s, slope_s, mob_s, gain_s, j_s, corr, corr_s, d_a, d_b, g_a, g_b = call(
-        functools.partial(strip_kernel, rows, cut, tail_cut),
-        (slab,) * 7 + (part_a, part_b, part_a, part_b),
-        (padded, padded, padded, slab, (tail, lanes)) + (padded,) * 4, smem=4, cost=cost,
+        functools.partial(main_kernel, rows), (padded, padded) + (slab,) * 7, (padded,) * 12, smem=4, cost=cost
+    )(flags, *tables, kind, a0, a1, j0, j1)
+
+    span = half // 2 + 2 * PAD
+    tail = 8 * fold_tiles(span)
+    part = (span + tail, lanes)
+    top_s, slope_s, mob_s, gain_s, j_s, corr, corr_s, *sums = call(
+        functools.partial(strip_kernel, rows, span),
+        (slab,) * 7 + (part, part), (padded, padded, padded, slab, slab) + (padded,) * 4, smem=4, cost=cost,
     )(flags, *tables, from_west, from_east, a_own, j_own, id_own, a0, a1, f0, f1, gain)
-    (s_a, s_b), (r_a, r_b) = scan((d_a, d_b), (g_a, g_b), flags, chip, chips, count)
-
-    own_rows, quarter = (half, lanes), (half // 2, lanes)
-    end_own, end_send, d_a, d_b, g_a, g_b, corr = call(
-        functools.partial(second_kernel, rows, half, cut, tail_cut),
-        (own_rows, own_rows, quarter, quarter, quarter, quarter, own_rows),
-        (padded,) * 9 + (slab, (tail, lanes)) + (padded,) * 12, cost=cost,
-    )(flags, s_a, s_b, r_a, r_b, corr, corr_s, gain, top, slope, mob, j0, j1, gain_s, top_s, slope_s, mob_s, j_s)
-    end_got = lax.ppermute(end_send, "tm", partner)
-    (s_a, s_b), (r_a, r_b) = scan((d_a, d_b), (g_a, g_b), flags, chip, chips, count)
-    ends = put(half, flags, end_got, put(half, flags, end_own))
-    new_own, new_send = call(last_kernel, (own_rows, own_rows))(flags, s_a, s_b, r_a, r_b, g_a, g_b, corr)
-    new_got = lax.ppermute(new_send, "tm", partner)
-    starts = put(half, flags, new_got, put(half, flags, new_own))
+    folds = call(functools.partial(fold_kernel, rows, span), ((tail, lanes),) * 2)(flags, gain_s)
+    sums, came = scan(sums, gain, [(f,) for f in folds], rows, flags, chip, chips, count)
+
+    quarter, room = (half // 2, lanes), (span + 2 * PAD, lanes)
+    ends, starts, sums_2, corrs = [], [], [], []
+    for p in range(2):
+        end_own, end_send, d, change = call(
+            functools.partial(second_kernel, rows, span, p),
+            (quarter,) * 4, (room,) * 9 + ((span, lanes), (tail, lanes)) + (room,) * 12, cost=cost,
+        )(flags, sums[p], came[p], corr, corr_s, gain, top, slope, mob, j0, j1, gain_s, top_s, slope_s, mob_s, j_s)
+        ends += [end_own, lax.ppermute(end_send, "tm", partner)]
+        sums_2.append(d)
+        corrs.append(change)
+    places = ((0, 0), (1, 0), (0, 1), (1, 1))
+    sums, came = scan(sums_2, gain, [(), ()], rows, flags, chip, chips, count)
+    ends = put(half, places, flags, ends)
+    for p in range(2):
+        if p == 1:
+            flags, ends = lax.optimization_barrier((flags, ends))
+        new_own, new_send = call(functools.partial(last_kernel, rows, p), (quarter, quarter))(
+            flags, sums[p], came[p], gain, corrs[p]
+        )
+        starts += [new_own, lax.ppermute(new_send, "tm", partner)]
+    starts = put(half, places[3:], flags, starts[3:], put(half, places[:3], flags, starts[:3]))
     return (starts[None], ends[None])
 
 

time: 58.3 us -> 53.6 us (0.919)
  waiting for transfers between devices: 15.2 us -> 9.43 us
  Pallas kernels: 23 us -> 23.8 us
    ppermute x8, waiting for transfers between devices: 13.2 us -> 7.32 us  [exchange(): return lax.ppermute(value, 'tm', [(i, i ^ 2 << bit) for i in range(count)])]
    pallas_call x9 -> x12, Pallas kernels: 18 us -> 19.9 us  [run(): pl.pallas_call(kernel, out_shape=[jax.ShapeDtypeStruct(shape, jnp.float32...]
    pallas_call x4 -> x3, Pallas kernels: 5.03 us -> 3.89 us  [put(): pl.pallas_call(functools.partial(put_kernel, half, places), out_shape=jax...]
  transfers between devices with their start and end apart: 13 -> 15, of which waited for: 7 -> 7; matrix products, arithmetic and copies ran while one was open for 1% -> 1% of each run, Pallas kernels for 19% -> 33%
where the time goes in v3:
time: 53.6 us; the launch traced here: 53.4 us
  Pallas kernels  23.8 us (44%)
  starting transfers between devices  16.8 us (31%)
  waiting for transfers between devices  9.43 us (18%)
  local copies, waits for them, and re-layouts  2.52 us (5%)
  between operations  0.82 us (2%)
    pallas_call x12, Pallas kernels, run(): pl.pallas_call(kernel, out_shape=[jax.ShapeDtypeStruct(shape, jnp.float32...  19.9 us
    ppermute x8, starting transfers between devices, exchange(): return lax.ppermute(value, 'tm', [(i, i ^ 2 << bit) for i in range(count)])  10.5 us
    ppermute x8, waiting for transfers between devices, exchange(): return lax.ppermute(value, 'tm', [(i, i ^ 2 << bit) for i in range(count)])  7.32 us
    pallas_call x3, Pallas kernels, put(): pl.pallas_call(functools.partial(put_kernel, half, places), out_shape=jax...  3.89 us
    ppermute x1, starting transfers between devices, local(): lax.ppermute(to_east, 'space', [(i, (i + 1) % spaces) for i in range(spac...  2.99 us
    ppermute x1, starting transfers between devices, local(): lax.ppermute(to_west, 'space', [((i + 1) % spaces, i) for i in range(spac...  2.09 us
    ppermute x1, waiting for transfers between devices, local(): lax.ppermute(to_west, 'space', [((i + 1) % spaces, i) for i in range(spac...  1.23 us
    dynamic_slice x1, local copies, waits for them, and re-layouts, local(): lax.dynamic_slice(x, (there, 0), slab)  1.13 us
  transfers between devices with their start and end apart: 15, of which 7 were waited for; matrix products, arithmetic and copies ran while one was open for 1% of the time, Pallas kernels for 33%

profile of v3, /device:TPU:0, one launch (start us, length us, event | category | flops | bytes accessed | tf_op | source)
XLA Modules:
  0.0 53.4 jit_solution(9320565312545880757)
XLA Ops:
  0.7 1.1 %dynamic-slice_bitcast_fusion = (f32[528,128]{1,0:T(8,128)S(1)}, f32[528,128]{1,0:T(8,128)S(1)}) fusion(f32[1,1024,128]{2,1,0:T(8,128)} %param.8, s32[]{:T(128)S(6)} %select_n.17, f32[1,1024,128]{2,1,0:T(8,128)} %param.7), kind=kLoop, calls=%fused_computation.1 | loop fusion | bytes 1081348 | tf_op jit(solution)/shard_map/dynamic_slice | solution.py:569
  3.1 0.9 %collective-permute-done.got = f32[1056,128]{1,0:T(8,128)S(1)} collective-permute-done((f32[1056,128]{1,0:T(8,128)S(1)}, f32[1056,128]{1,0:T(8,128)S(1)}, u32[]{:S(2)}, u32[]{:S(2)}) %collective-permute-start) | collective-permute-done | bytes 540704 | tf_op jit(solution)/shard_map/ppermute | solution.py:571
  4.0 1.3 %shard_map.86 = (f32[544,128]{1,0:T(8,128)S(1)}, f32[544,128]{1,0:T(8,128)S(1)}, f32[528,128]{1,0:T(8,128)S(1)}, f32[528,128]{1,0:T(8,128)S(1)}, f32[528,128]{1,...) custom-call(s32[9]{0:T(128)S(1)} %fusion.flags, f32[1024,128]{1,0:T(8,128)S(1)} %bitcast.10, ...), custom_call_target="tpu_custom_call" | custom-call | flops 16220160 | bytes 2703360 | tf_op jit(solution)/shard_map/pallas_call | solution.py:453
  5.3 3.0 %collective-permute-start.1 = (f32[264,128]{1,0:T(8,128)S(1)}, f32[264,128]{1,0:T(8,128)S(1)}, u32[]{:S(2)}, u32[]{:S(2)}) collective-permute-start(f32[264,128]{1,0:T(8,128)S(1)} %get-tuple-element.57), channel_id=1, source_target_pairs={{0,1},{1,2},{2,3},{3,0},{4,5},{5,6},{6,7},{7,4},{8,9},{9,10},{10,1... | collective-permute-start | bytes 405512 | tf_op jit(solution)/shard_map/ppermute | solution.py:577
  8.3 2.1 %collective-permute-start.2 = (f32[264,128]{1,0:T(8,128)S(1)}, f32[264,128]{1,0:T(8,128)S(1)}, u32[]{:S(2)}, u32[]{:S(2)}) collective-permute-start(f32[264,128]{1,0:T(8,128)S(1)} %get-tuple-element.58), channel_id=1, source_target_pairs={{1,0},{2,1},{3,2},{0,3},{5,4},{6,5},{7,6},{4,7},{9,8},{10,9},{11,1... | collective-permute-start | bytes 405512 | tf_op jit(solution)/shard_map/ppermute | solution.py:576
  11.1 4.2 %shard_map.87 = (f32[544,128]{1,0:T(8,128)S(1)}, f32[544,128]{1,0:T(8,128)S(1)}, f32[528,128]{1,0:T(8,128)S(1)}, f32[528,128]{1,0:T(8,128)S(1)}, f32[528,128]{1,...) custom-call(s32[9]{0:T(128)S(1)} %fusion.flags, ...), custom_call_target="tpu_custom_call" | custom-call | flops 16220160 | bytes 2703360 | tf_op jit(solution)/shard_map/pallas_call | solution.py:453
  15.3 1.2 %collective-permute-done.2.east = f32[264,128]{1,0:T(8,128)S(1)} collective-permute-done((f32[264,128]{1,0:T(8,128)S(1)}, f32[264,128]{1,0:T(8,128)S(1)}, u32[]{:S(2)}, u32[]{:S(2)}) %collective-permute-start.2) | collective-permute-done | bytes 135200 | tf_op jit(solution)/shard_map/ppermute | solution.py:576
  16.5 3.8 %shard_map.88 = (f32[528,128]{1,0:T(8,128)S(1)}, f32[528,128]{1,0:T(8,128)S(1)}, f32[528,128]{1,0:T(8,128)S(1)}, f32[528,128]{1,0:T(8,128)S(1)}, f32[528,128]{1,...) custom-call(s32[9]{0:T(128)S(1)} %fusion.flags, ...), custom_call_target="tpu_custom_call" | custom-call | flops 16220160 | bytes 2703360 | tf_op jit(solution)/shard_map/pallas_call | solution.py:453
  20.3 1.6 %collective-permute-start.3 = (f32[312,128]{1,0:T(8,128)S(1)}, f32[312,128]{1,0:T(8,128)S(1)}, u32[]{:S(2)}, u32[]{:S(2)}) collective-permute-start(f32[312,128]{1,0:T(8,128)S(1)} %get-tuple-element.64.d), channel_id=1, source_target_pairs={{0,8},{4,12},{8,0},{12,4},{16,24},{20,28},{24,16},{28,20},{1,9},{5... | collective-permute-start | bytes 479240 | tf_op jit(solution)/shard_map/ppermute | solution.py:510
  21.9 1.5 %collective-permute-start.6 = (f32[312,128]{1,0:T(8,128)S(1)}, f32[312,128]{1,0:T(8,128)S(1)}, u32[]{:S(2)}, u32[]{:S(2)}) collective-permute-start(f32[312,128]{1,0:T(8,128)S(1)} %get-tuple-element.80.d), channel_id=1, source_target_pairs={{0,16},{4,20},{8,24},{12,28},{16,0},{20,4},{24,8},{28,12},{1,17},{... | collective-permute-start | bytes 479240 | tf_op jit(solution)/shard_map/ppermute | solution.py:510
  23.4 0.7 %shard_map.89 = (f32[40,128]{1,0:T(8,128)S(1)}, f32[40,128]{1,0:T(8,128)S(1)}) custom-call(s32[9]{0:T(128)S(1)} %fusion.flags, f32[528,128]{1,0:T(8,128)S(1)} %get-tuple-element.65.gain_s), custom_call_target="tpu_custom_call" | custom-call | tf_op jit(solution)/shard_map/pallas_call | solution.py:453
  24.2 1.7 %collective-permute-done.3.came = f32[312,128]{1,0:T(8,128)S(1)} collective-permute-done((f32[312,128]{1,0:T(8,128)S(1)}, f32[312,128]{1,0:T(8,128)S(1)}, u32[]{:S(2)}, u32[]{:S(2)}) %collective-permute-start.3) | collective-permute-done | bytes 159776 | tf_op jit(solution)/shard_map/ppermute | solution.py:510
  26.6 1.6 %collective-permute-start.4 = (f32[312,128]{1,0:T(8,128)S(1)}, f32[312,128]{1,0:T(8,128)S(1)}, u32[]{:S(2)}, u32[]{:S(2)}) collective-permute-start(f32[312,128]{1,0:T(8,128)S(1)} %get-tuple-element.68), channel_id=1, source_target_pairs={{0,16},{4,20},{8,24},{12,28},{16,0},{20,4},{24,8},{28,12},{1,17},{... | collective-permute-start | bytes 479240 | tf_op jit(solution)/shard_map/ppermute | solution.py:510
  28.8 1.6 %collective-permute-start.7 = (f32[312,128]{1,0:T(8,128)S(1)}, f32[312,128]{1,0:T(8,128)S(1)}, u32[]{:S(2)}, u32[]{:S(2)}) collective-permute-start(f32[312,128]{1,0:T(8,128)S(1)} %get-tuple-element.83), channel_id=1, source_target_pairs={{0,8},{4,12},{8,0},{12,4},{16,24},{20,28},{24,16},{28,20},{1,9},{5... | collective-permute-start | bytes 479240 | tf_op jit(solution)/shard_map/ppermute | solution.py:510
  30.4 1.5 %collective-permute-done.4.came = f32[312,128]{1,0:T(8,128)S(1)} collective-permute-done((f32[312,128]{1,0:T(8,128)S(1)}, f32[312,128]{1,0:T(8,128)S(1)}, u32[]{:S(2)}, u32[]{:S(2)}) %collective-permute-start.4) | collective-permute-done | bytes 159776 | tf_op jit(solution)/shard_map/ppermute | solution.py:510
  31.9 3.0 %shard_map.91 = (f32[256,128]{1,0:T(8,128)S(1)}, f32[256,128]{1,0:T(8,128)S(1)}, f32[256,128]{1,0:T(8,128)S(1)}, f32[256,128]{1,0:T(8,128)S(1)}) custom-call(s32[9]{0:T(128)S(1)} %fusion.flags, f32[312,128]{1,0:T(8,128)S(1)} %get-tuple-element.67.sums, f32[312,128]{1,0:T(8,128)S(1)} %collective-permute-done.4.came, f32[528,128]{1,0:T(8,128)S(1)} %get-tuple-element.69.corr, ...), custom_call_target="tpu_custom_call" | custom-call | flops 16220160 | bytes 2703360 | tf_op jit(solution)/shard_map/pallas_call | solution.py:453
  34.9 1.6 %collective-permute-start.12 = (f32[256,128]{1,0:T(8,128)S(1)}, f32[256,128]{1,0:T(8,128)S(1)}, u32[]{:S(2)}, u32[]{:S(2)}) collective-permute-start(f32[256,128]{1,0:T(8,128)S(1)} %get-tuple-element.92.d), channel_id=1, source_target_pairs={{0,8},{4,12},{8,0},{12,4},{16,24},{20,28},{24,16},{28,20},{1,9},{5... | collective-permute-start | bytes 393224 | tf_op jit(solution)/shard_map/ppermute | solution.py:510
  36.5 3.0 %shard_map.93 = (f32[256,128]{1,0:T(8,128)S(1)}, f32[256,128]{1,0:T(8,128)S(1)}, f32[256,128]{1,0:T(8,128)S(1)}, f32[256,128]{1,0:T(8,128)S(1)}) custom-call(s32[9]{0:T(128)S(1)} %fusion.flags, f32[312,128]{1,0:T(8,128)S(1)} %get-tuple-element.82.sums, f32[312,128]{1,0:T(8,128)S(1)} %collective-permute-done.7.came, f32[528,128]{1,0:T(8,128)S(1)} %get-tuple-element.69.corr, ...), custom_call_target="tpu_custom_call" | custom-call | flops 16220160 | bytes 2703360 | tf_op jit(solution)/shard_map/pallas_call | solution.py:453
  39.5 1.6 %collective-permute-start.9 = (f32[256,128]{1,0:T(8,128)S(1)}, f32[256,128]{1,0:T(8,128)S(1)}, u32[]{:S(2)}, u32[]{:S(2)}) collective-permute-start(f32[256,128]{1,0:T(8,128)S(1)} %get-tuple-element.87.d), channel_id=1, source_target_pairs={{0,16},{4,20},{8,24},{12,28},{16,0},{20,4},{24,8},{28,12},{1,17},{... | collective-permute-start | bytes 393224 | tf_op jit(solution)/shard_map/ppermute | solution.py:510
  42.8 1.7 %collective-permute-done.9.came = f32[256,128]{1,0:T(8,128)S(1)} collective-permute-done((f32[256,128]{1,0:T(8,128)S(1)}, f32[256,128]{1,0:T(8,128)S(1)}, u32[]{:S(2)}, u32[]{:S(2)}) %collective-permute-start.9) | collective-permute-done | bytes 131104 | tf_op jit(solution)/shard_map/ppermute | solution.py:510
  45.8 1.4 %shard_map.94 = f32[1024,128]{1,0:T(8,128)} custom-call(s32[9]{0:T(128)S(1)} %fusion.flags, f32[256,128]{1,0:T(8,128)S(1)} %get-tuple-element.78.refs_0_, f32[256,128]{1,0:T(8,128)S(1)} %collective-permute-done.5.refs_1_, f32[256,128]{1,0:T(8,128)S(1)} %get-tuple-element.84.refs_2_, f32[256,128]{1,0:T(8,128)S(1)} %collective-permute-done.8.refs_3_), custom_call_target="tpu_custom_call" | custom-call | bytes 1048576 | tf_op jit(solution)/shard_map/pallas_call | solution.py:439
  48.4 1.8 %collective-permute-done.10.came = f32[256,128]{1,0:T(8,128)S(1)} collective-permute-done((f32[256,128]{1,0:T(8,128)S(1)}, f32[256,128]{1,0:T(8,128)S(1)}, u32[]{:S(2)}, u32[]{:S(2)}) %collective-permute-start.10) | collective-permute-done | bytes 131104 | tf_op jit(solution)/shard_map/ppermute | solution.py:510
  50.9 1.3 %shard_map.99.refs_1_ = f32[1024,128]{1,0:T(8,128)} custom-call(s32[9]{0:T(128)S(1)} %fusion.flags, f32[256,128]{1,0:T(8,128)S(1)} %get-tuple-element.96.refs_0_, f32[256,128]{1,0:T(8,128)S(1)} %collective-permute-done.14.refs_1_, f32[256,128]{1,0:T(8,128)S(1)} %get-tuple-element.98.refs_2_), custom_call_target="tpu_custom_call" | custom-call | bytes 786432 | tf_op jit(solution)/shard_map/pallas_call | solution.py:439
  52.2 1.2 %shard_map.100 = f32[1024,128]{1,0:T(8,128)} custom-call(s32[9]{0:T(128)S(1)} %fusion.flags, f32[256,128]{1,0:T(8,128)S(1)} %collective-permute-done.11.refs_0_, f32[1024,128]{1,0:T(8,128)} %shard_map.99.refs_1_), custom_call_target="tpu_custom_call", output_to_operand_aliasing={{}: (2, {})} | custom-call | bytes 262144 | tf_op jit(solution)/shard_map/pallas_call | solution.py:439
  (36 shorter events, 8.2 us)
Async XLA Ops:
  0.6 3.3 %copy-start.2 = (s32[1024,128]{1,0:T(8,128)S(1)}, s32[1024,128]{1,0:T(8,128)}, u32[]{:S(2)}) copy-start(s32[1024,128]{1,0:T(8,128)} %region.1) | copy-start | bytes 1572868
  1.8 2.2 %copy-start = (f32[1,1024,128]{2,1,0:T(8,128)S(1)}, f32[1,1024,128]{2,1,0:T(8,128)}, u32[]{:S(2)}) copy-start(f32[1,1024,128]{2,1,0:T(8,128)} %param.7) | copy-start | bytes 1572868
  1.8 2.2 %copy-start.1 = (f32[1,1024,128]{2,1,0:T(8,128)S(1)}, f32[1,1024,128]{2,1,0:T(8,128)}, u32[]{:S(2)}) copy-start(f32[1,1024,128]{2,1,0:T(8,128)} %param.8) | copy-start | bytes 1572868
  1.9 2.1 %collective-permute-start = (f32[1056,128]{1,0:T(8,128)S(1)}, f32[1056,128]{1,0:T(8,128)S(1)}, u32[]{:S(2)}, u32[]{:S(2)}) collective-permute-start(f32[1056,128]{1,0:T(8,128)S(1)} %pad_maximum_fusion), channel_id=1, source_target_pairs={{0,4},{4,0},{8,12},{12,8},{16,20},{20,16},{24,28},{28,24},{1,5},{5... | collective-permute-start | bytes 1622024 | tf_op jit(solution)/shard_map/ppermute | solution.py:571
  5.3 10.0 %collective-permute-start.1 = (f32[264,128]{1,0:T(8,128)S(1)}, f32[264,128]{1,0:T(8,128)S(1)}, u32[]{:S(2)}, u32[]{:S(2)}) collective-permute-start(f32[264,128]{1,0:T(8,128)S(1)} %get-tuple-element.57), channel_id=1, source_target_pairs={{0,1},{1,2},{2,3},{3,0},{4,5},{5,6},{6,7},{7,4},{8,9},{9,10},{10,1... | collective-permute-start | bytes 405512 | tf_op jit(solution)/shard_map/ppermute | solution.py:577
  8.3 8.3 %collective-permute-start.2 = (f32[264,128]{1,0:T(8,128)S(1)}, f32[264,128]{1,0:T(8,128)S(1)}, u32[]{:S(2)}, u32[]{:S(2)}) collective-permute-start(f32[264,128]{1,0:T(8,128)S(1)} %get-tuple-element.58), channel_id=1, source_target_pairs={{1,0},{2,1},{3,2},{0,3},{5,4},{6,5},{7,6},{4,7},{9,8},{10,9},{11,1... | collective-permute-start | bytes 405512 | tf_op jit(solution)/shard_map/ppermute | solution.py:576
  10.4 0.7 %copy-start.3 = (f32[8]{0:T(128)S(1)}, f32[8]{0:T(128)}, u32[]{:S(2)}) copy-start(f32[8]{0:T(128)} %nu_tab.3) | copy-start | bytes 100
  10.4 0.7 %copy-start.4 = (f32[8]{0:T(128)S(1)}, f32[8]{0:T(128)}, u32[]{:S(2)}) copy-start(f32[8]{0:T(128)} %sat_tab.3) | copy-start | bytes 100
  10.4 0.7 %copy-start.5 = (f32[8]{0:T(128)S(1)}, f32[8]{0:T(128)}, u32[]{:S(2)}) copy-start(f32[8]{0:T(128)} %mob_tab.3) | copy-start | bytes 100
  20.3 5.5 %collective-permute-start.3 = (f32[312,128]{1,0:T(8,128)S(1)}, f32[312,128]{1,0:T(8,128)S(1)}, u32[]{:S(2)}, u32[]{:S(2)}) collective-permute-start(f32[312,128]{1,0:T(8,128)S(1)} %get-tuple-element.64.d), channel_id=1, source_target_pairs={{0,8},{4,12},{8,0},{12,4},{16,24},{20,28},{24,16},{28,20},{1,9},{5... | collective-permute-start | bytes 479240 | tf_op jit(solution)/shard_map/ppermute | solution.py:510
  21.9 6.3 %collective-permute-start.6 = (f32[312,128]{1,0:T(8,128)S(1)}, f32[312,128]{1,0:T(8,128)S(1)}, u32[]{:S(2)}, u32[]{:S(2)}) collective-permute-start(f32[312,128]{1,0:T(8,128)S(1)} %get-tuple-element.80.d), channel_id=1, source_target_pairs={{0,16},{4,20},{8,24},{12,28},{16,0},{20,4},{24,8},{28,12},{1,17},{... | collective-permute-start | bytes 479240 | tf_op jit(solution)/shard_map/ppermute | solution.py:510
  26.6 5.3 %collective-permute-start.4 = (f32[312,128]{1,0:T(8,128)S(1)}, f32[312,128]{1,0:T(8,128)S(1)}, u32[]{:S(2)}, u32[]{:S(2)}) collective-permute-start(f32[312,128]{1,0:T(8,128)S(1)} %get-tuple-element.68), channel_id=1, source_target_pairs={{0,16},{4,20},{8,24},{12,28},{16,0},{20,4},{24,8},{28,12},{1,17},{... | collective-permute-start | bytes 479240 | tf_op jit(solution)/shard_map/ppermute | solution.py:510
  28.8 7.6 %collective-permute-start.7 = (f32[312,128]{1,0:T(8,128)S(1)}, f32[312,128]{1,0:T(8,128)S(1)}, u32[]{:S(2)}, u32[]{:S(2)}) collective-permute-start(f32[312,128]{1,0:T(8,128)S(1)} %get-tuple-element.83), channel_id=1, source_target_pairs={{0,8},{4,12},{8,0},{12,4},{16,24},{20,28},{24,16},{28,20},{1,9},{5... | collective-permute-start | bytes 479240 | tf_op jit(solution)/shard_map/ppermute | solution.py:510
  34.9 6.7 %collective-permute-start.12 = (f32[256,128]{1,0:T(8,128)S(1)}, f32[256,128]{1,0:T(8,128)S(1)}, u32[]{:S(2)}, u32[]{:S(2)}) collective-permute-start(f32[256,128]{1,0:T(8,128)S(1)} %get-tuple-element.92.d), channel_id=1, source_target_pairs={{0,8},{4,12},{8,0},{12,4},{16,24},{20,28},{24,16},{28,20},{1,9},{5... | collective-permute-start | bytes 393224 | tf_op jit(solution)/shard_map/ppermute | solution.py:510
  39.5 5.0 %collective-permute-start.9 = (f32[256,128]{1,0:T(8,128)S(1)}, f32[256,128]{1,0:T(8,128)S(1)}, u32[]{:S(2)}, u32[]{:S(2)}) collective-permute-start(f32[256,128]{1,0:T(8,128)S(1)} %get-tuple-element.87.d), channel_id=1, source_target_pairs={{0,16},{4,20},{8,24},{12,28},{16,0},{20,4},{24,8},{28,12},{1,17},{... | collective-permute-start | bytes 393224 | tf_op jit(solution)/shard_map/ppermute | solution.py:510
  41.0 4.7 %collective-permute-start.8 = (f32[256,128]{1,0:T(8,128)S(1)}, f32[256,128]{1,0:T(8,128)S(1)}, u32[]{:S(2)}, u32[]{:S(2)}) collective-permute-start(f32[256,128]{1,0:T(8,128)S(1)} %get-tuple-element.85), channel_id=1, source_target_pairs={{0,4},{4,0},{8,12},{12,8},{16,20},{20,16},{24,28},{28,24},{1,5},{5... | collective-permute-start | bytes 393224 | tf_op jit(solution)/shard_map/ppermute | solution.py:599
  41.0 4.7 %collective-permute-start.5 = (f32[256,128]{1,0:T(8,128)S(1)}, f32[256,128]{1,0:T(8,128)S(1)}, u32[]{:S(2)}, u32[]{:S(2)}) collective-permute-start(f32[256,128]{1,0:T(8,128)S(1)} %get-tuple-element.79), channel_id=1, source_target_pairs={{0,4},{4,0},{8,12},{12,8},{16,20},{20,16},{24,28},{28,24},{1,5},{5... | collective-permute-start | bytes 393224 | tf_op jit(solution)/shard_map/ppermute | solution.py:599
  42.2 5.5 %collective-permute-start.13 = (f32[256,128]{1,0:T(8,128)S(1)}, f32[256,128]{1,0:T(8,128)S(1)}, u32[]{:S(2)}, u32[]{:S(2)}) collective-permute-start(f32[256,128]{1,0:T(8,128)S(1)} %get-tuple-element.94), channel_id=1, source_target_pairs={{0,16},{4,20},{8,24},{12,28},{16,0},{20,4},{24,8},{28,12},{1,17},{... | collective-permute-start | bytes 393224 | tf_op jit(solution)/shard_map/ppermute | solution.py:510
  45.2 5.0 %collective-permute-start.10 = (f32[256,128]{1,0:T(8,128)S(1)}, f32[256,128]{1,0:T(8,128)S(1)}, u32[]{:S(2)}, u32[]{:S(2)}) collective-permute-start(f32[256,128]{1,0:T(8,128)S(1)} %get-tuple-element.89), channel_id=1, source_target_pairs={{0,8},{4,12},{8,0},{12,4},{16,24},{20,28},{24,16},{28,20},{1,9},{5... | collective-permute-start | bytes 393224 | tf_op jit(solution)/shard_map/ppermute | solution.py:510
  48.3 2.6 %collective-permute-start.14 = (f32[256,128]{1,0:T(8,128)S(1)}, f32[256,128]{1,0:T(8,128)S(1)}, u32[]{:S(2)}, u32[]{:S(2)}) collective-permute-start(f32[256,128]{1,0:T(8,128)S(1)} %get-tuple-element.97), channel_id=1, source_target_pairs={{0,4},{4,0},{8,12},{12,8},{16,20},{20,16},{24,28},{28,24},{1,5},{5... | collective-permute-start | bytes 393224 | tf_op jit(solution)/shard_map/ppermute | solution.py:611
  50.8 1.4 %collective-permute-start.11 = (f32[256,128]{1,0:T(8,128)S(1)}, f32[256,128]{1,0:T(8,128)S(1)}, u32[]{:S(2)}, u32[]{:S(2)}) collective-permute-start(f32[256,128]{1,0:T(8,128)S(1)} %get-tuple-element.91), channel_id=1, source_target_pairs={{0,4},{4,0},{8,12},{12,8},{16,20},{20,16},{24,28},{28,24},{1,5},{5... | collective-permute-start | bytes 393224 | tf_op jit(solution)/shard_map/ppermute | solution.py:611

commit v4 on v3

v4 whole, which is shorter than its diff:
```python
import functools

import jax
import jax.numpy as jnp
import numpy as np
from jax import lax
from jax.experimental import pallas as pl
from jax.experimental.pallas import tpu as pltpu
from jax.sharding import PartitionSpec as P

STEPS = 3
ITERS = 2
HALO = 2 * STEPS * ITERS
J_HALO = HALO - 2
ID_HALO = HALO - 1
REACH = 2 * STEPS
PAD = 8
CHUNK = 96
FOLD = 8
VMEM = pl.BlockSpec(memory_space=pltpu.VMEM)
PARAMS = pltpu.CompilerParams(vmem_limit_bytes=14 * 1024 * 1024)


def place(chips):
    slot = lax.axis_index("tm")
    chip = slot // 2
    return slot % 2, chip, chip == chips - 1


def lanes_of(rows, lanes):
    return lax.broadcasted_iota(jnp.int32, (rows, lanes), 1)


def roll(x, amount):
    amount = amount % x.shape[1]
    return pltpu.roll(x, amount, 1) if amount else x


def inside(lane, *spans):
    hit = None
    for low, high in spans:
        one = (lane >= low) & (lane < high)
        hit = one if hit is None else hit | one
    return hit


def pieces(rows):
    tiles = rows // 8
    count = -(-tiles // (CHUNK // 8))
    edges = [8 * (tiles * c // count) for c in range(count + 1)]
    return [(low, high - low) for low, high in zip(edges[:-1], edges[1:])]


def over_chunks(rows, body):
    for base, n in pieces(rows):
        body(base, n)


def aligned(at):
    return at if isinstance(at, int) else pl.multiple_of(at, 8)


def coefficients(kind, table):
    regions = table.shape[0] // 3
    base, satur, mobile = (table[t * regions : t * regions + 1, :] for t in range(3))
    base, satur, mobile = (jnp.broadcast_to(x, kind.shape) for x in (base, satur, mobile))
    for r in range(1, regions):
        hit = kind == r
        base = jnp.where(hit, table[r : r + 1, :], base)
        satur = jnp.where(hit, table[regions + r : regions + r + 1, :], satur)
        mobile = jnp.where(hit, table[2 * regions + r : 2 * regions + r + 1, :], mobile)
    gain = 1.0 / (1.0 + 12.0 * mobile * base)
    slope = base * satur
    return base + slope, slope, mobile * 0.5, gain


def fine_steps(units, rows, work):
    chunks = pieces(rows)
    for step in range(STEPS):
        moved = {}
        for turn in range(len(chunks) + 4):
            for u, (bufs, top, slope, mob, drive, *skip) in enumerate(units):
                off = skip[0] if skip else 0
                old, new = bufs[step], bufs[step + 1]
                nu, east, flow, face = work[4 * u : 4 * u + 4]

                def rows_of(c, off=off):
                    if not 0 <= c < len(chunks):
                        return None
                    base, n = chunks[c]
                    return pl.ds(base + PAD, n), pl.ds(base + PAD - 1, n), pl.ds(base + PAD + 1, n), pl.ds(aligned(off + base), n)

                c = turn - 3
                if spot := rows_of(c):
                    at, above, _, _ = spot
                    nu0 = nu[at, :]
                    out = (nu0 + moved.pop((u, 3, c))) * east[at, :]
                    flow[at, :] = out
                    moved[u, 4, c] = roll(out, 1)
                    face[at, :] = (nu0 + nu[above, :]) * (old[at, :] - old[above, :])
                    if c == len(chunks) - 1:
                        end = PAD + rows
                        nu[end : end + 1, :] = nu[end - 1 : end, :]
                        at, above = pl.ds(end, 8), pl.ds(end - 1, 8)
                        face[at, :] = (nu[at, :] + nu[above, :]) * (old[at, :] - old[above, :])
                c = turn - 4
                if spot := rows_of(c):
                    at, _, below, coef = spot
                    total = flow[at, :] - moved.pop((u, 4, c))
                    total = total + (face[below, :] - face[at, :])
                    new[at, :] = old[at, :] + mob[coef, :] * (total + drive[coef, :])
                c = turn - 2
                if spot := rows_of(c):
                    at, above, below, coef = spot
                    dr = old[below, :] - old[above, :]
                    dt = east[at, :] + moved.pop((u, 2, c))
                    bottom = 1.0 + (dr * dr + dt * dt)
                    out = top[coef, :] - slope[coef, :] / bottom
                    nu[at, :] = out
                    if c == 0:
                        nu[PAD - 1 : PAD, :] = nu[PAD : PAD + 1, :]
                    moved[u, 3, c] = roll(out, -1)
                c = turn - 1
                if spot := rows_of(c):
                    at = spot[0]
                    out = moved.pop((u, 1, c)) - old[at, :]
                    east[at, :] = out
                    moved[u, 2, c] = roll(out, 1)
                c = turn
                if spot := rows_of(c):
                    moved[u, 1, c] = roll(old[spot[0], :], -1)


def clear_pads(ref, rows):
    ref[0:PAD, :] = jnp.zeros((PAD, ref.shape[1]), jnp.float32)
    ref[PAD + rows : rows + 2 * PAD, :] = jnp.zeros((PAD, ref.shape[1]), jnp.float32)


def pack_kernel(rows, start, chips, own_a, own_j, got, region, a0, a1, j0, j1, kind, to_west, to_east):
    lanes = a0.shape[1]
    q, both = lanes // 4, HALO + J_HALO
    h, _, _ = place(chips)
    mine = h == 0
    first = h * start
    clear_pads(a0, rows)
    clear_pads(a1, rows)

    def gather(base, n):
        src = pl.ds(aligned(first + base), n)
        a_own, j_own = own_a[src, :] * 0.5, own_j[src, :]
        a_got, j_got = got[pl.ds(base, n), :] * 0.5, got[pl.ds(base + rows, n), :]
        here, padded = pl.ds(base, n), pl.ds(base + PAD, n)
        a0[padded, :], a1[padded, :] = jnp.where(mine, a_own, a_got), jnp.where(mine, a_got, a_own)
        j0[here, :], j1[here, :] = jnp.where(mine, j_own, j_got), jnp.where(mine, j_got, j_own)
        kind[here, :] = region[src, :].astype(jnp.float32)

    over_chunks(rows, gather)

    def body(low, n):
        lane = lanes_of(n, lanes)
        west = jnp.zeros((n, lanes), jnp.float32)
        east = west
        for k in range(2):
            base = part_start(h, k, rows) + low
            here, padded = pl.ds(aligned(base), n), pl.ds(aligned(base + PAD), n)
            ids = kind[here, :]
            for s, (a, j) in enumerate(((a0[padded, :], j0[here, :]), (a1[padded, :], j1[here, :]))):
                at = (2 * s + 2) * q - HALO - k * both
                west = jnp.where(inside(lane, (at, at + HALO)), roll(a, at), west)
                at = at - J_HALO
                west = jnp.where(inside(lane, (at, at + J_HALO)), roll(j, at), west)
                at = 2 * s * q + k * both
                east = jnp.where(inside(lane, (at, at + HALO)), roll(a, at + HALO), east)
                at = at + HALO
                east = jnp.where(inside(lane, (at, at + J_HALO)), roll(j, at + J_HALO), east)
            at = 2 * q * (1 - k)
            west = jnp.where(inside(lane, (at, at + ID_HALO)), roll(ids, at), west)
            at = (3 - 2 * k) * q + HALO
            east = jnp.where(inside(lane, (at, at + ID_HALO)), roll(ids, at + ID_HALO), east)
        to_west[pl.ds(low, n), :] = west
        to_east[pl.ds(low, n), :] = east

    over_chunks(to_west.shape[0], body)


def own_part(s0, s1, lane):
    q = s0.shape[1] // 4
    out = jnp.zeros(s0.shape, jnp.float32)
    for s, x in enumerate((s0, s1)):
        w = 2 * s * q
        out = jnp.where(inside(lane, (w + HALO, w + q)), roll(x, w + HALO), out)
        out = jnp.where(inside(lane, (w + q, w + 2 * q - HALO)), roll(x, w + 2 * q - HALO), out)
    return out


def merge_edges(main, strip, s, lane):
    lanes = main.shape[1]
    q = lanes // 4
    w = 2 * s * q
    out = jnp.where(lane < REACH, roll(strip, -(w + HALO)), main)
    return jnp.where(lane >= lanes - REACH, roll(strip, -(w + 2 * q - HALO)), out)


def main_kernel(
    rows, table, kind, a0, a1, j0, j1,
    f0, f1, top, slope, mob, gain, a_own, j_own, id_own, b0, c0, b1, c1, *work,
):
    for ref in (b0, c0, b1, c1):
        clear_pads(ref, rows)

    def body(base, n):
        lane = lanes_of(n, a0.shape[1])
        here, padded = pl.ds(base, n), pl.ds(base + PAD, n)
        top[here, :], slope[here, :], mob[here, :], gain[here, :] = coefficients(kind[here, :], table)
        a_own[here, :] = own_part(a0[padded, :], a1[padded, :], lane)
        j_own[here, :] = own_part(j0[here, :], j1[here, :], lane)
        id_own[here, :] = own_part(kind[here, :], kind[here, :], lane)

    over_chunks(rows, body)
    fine_steps((((a0, b0, c0, f0), top, slope, mob, j0), ((a1, b1, c1, f1), top, slope, mob, j1)), rows, work)


def strip_kernel(
    rows, span, p, chips, table, west, east, a_own, j_own, id_own, a0, a1, f0, f1, gain,
    d_out, corr, corr_s, top_s, slope_s, mob_s, gain_s, j_s, a_s, b_s, c_s, d_s, *work,
):
    lanes = a0.shape[1]
    q, both = lanes // 4, HALO + J_HALO
    h, _, last = place(chips)
    off = part_start(h, p, rows)
    for ref in (a_s, b_s, c_s):
        clear_pads(ref, span)

    def build(base, n):
        lane = lanes_of(n, lanes)
        heads = inside(lane, (0, HALO), (2 * q, 2 * q + HALO))
        tails = inside(lane, (2 * q - HALO, 2 * q), (4 * q - HALO, 4 * q))
        here, padded, slab = pl.ds(base, n), pl.ds(base + PAD, n), pl.ds(aligned(off + base), n)
        w, e = west[here, :], east[here, :]
        w_ids = roll(w, 1 - (3 * q + HALO)), roll(w, 1 - (q + HALO))
        e_ids = roll(e, -HALO), roll(e, 2 * q - HALO)

        def halo(from_west, from_east, rest):
            return jnp.where(heads, from_west, jnp.where(tails, from_east, rest))

        a_s[padded, :] = halo(roll(w, -p * both), roll(e, p * both), a_own[slab, :])
        j_s[here, :] = halo(roll(w, -J_HALO - p * both), roll(e, J_HALO + p * both), j_own[slab, :])
        lower = lane < 2 * q
        kind = halo(
            jnp.where(lower, w_ids[p], w_ids[1 - p]), jnp.where(lower, e_ids[p], e_ids[1 - p]), id_own[slab, :]
        )
        top_s[here, :], slope_s[here, :], mob_s[here, :], gain_s[here, :] = coefficients(kind, table)

    over_chunks(span, build)
    fine_steps((((a_s, b_s, c_s, b_s), top_s, slope_s, mob_s, j_s),), span, work)

    def finish(base, n):
        lane = lanes_of(n, lanes)
        here, padded = pl.ds(base, n), pl.ds(base + PAD, n)
        slab, deep = pl.ds(aligned(off + base), n), pl.ds(aligned(off + base + PAD), n)
        strip = b_s[padded, :]
        g_s = gain_s[here, :]
        c = strip - g_s * a_s[padded, :]
        corr_s[here, :] = c
        d_s[here, :] = roll(jnp.where(last, strip, c), 2 * q) + jnp.where(last, 0.0, g_s * c)
        g = gain[slab, :]
        end0 = merge_edges(f0[deep, :], strip, 0, lane)
        end1 = merge_edges(f1[deep, :], strip, 1, lane)
        change = end0 - g * a0[deep, :]
        corr[here, :] = change
        d_out[here, :] = jnp.where(last, end1, g * change + end1 - g * a1[deep, :])

    over_chunks(span, finish)
    fold(d_s, d_out, span, span)


def part_start(h, p, rows):
    return aligned(PAD * h + p * ((rows - 2 * PAD) // 2 - PAD))


def fold_kernel(span, gain_s, out):
    fold(gain_s, out, span, 0)


def fold_tiles(rows):
    return -(-(rows // 8) // FOLD)


def fold(src, dst, rows, to):
    lanes = src.shape[1]
    q, width = lanes // 4, lanes // FOLD
    lane = lanes_of(8, lanes)
    tiles = fold_tiles(rows)
    for r in range(tiles):
        out = jnp.zeros((8, lanes), jnp.float32)
        for k in range(FOLD):
            t = k * tiles + r
            if 8 * t >= rows:
                continue
            x = src[8 * t : 8 * t + 8, :]
            at_w, at_e = width * k, width * k + width // 2
            out = jnp.where(inside(lane, (at_w, at_w + REACH)), roll(x, at_w - (HALO - REACH)), out)
            out = jnp.where(inside(lane, (at_e, at_e + REACH)), roll(x, at_e - (2 * q - HALO)), out)
        dst[to + 8 * r : to + 8 * r + 8, :] = out


def unfold(src, dst, rows):
    lanes = src.shape[1]
    q, width = lanes // 4, lanes // FOLD
    lane = lanes_of(8, lanes)
    tiles = fold_tiles(rows)
    for r in range(tiles):
        x = src[8 * r : 8 * r + 8, :]
        for k in range(FOLD):
            t = k * tiles + r
            if 8 * t >= rows:
                continue
            at_w, at_e = width * k, width * k + width // 2
            out = jnp.where(lane < q, roll(x, HALO - REACH - at_w), roll(x, 2 * q - HALO - at_e))
            dst[8 * t : 8 * t + 8, :] = out


def second_kernel(
    rows, span, p, chips, sums, came, corr, corr_s, gain, top, slope, mob, j0, j1,
    gain_s, top_s, slope_s, mob_s, j_s,
    end_own, end_send, d_out, corr_out, a0, a1, a_s, b0, b1, b_s, c0, c1, c_s, spread, folded, *work,
):
    lanes = a0.shape[1]
    q = lanes // 4
    h, _, last = place(chips)
    off = part_start(h, p, rows)
    for ref in (a0, a1, a_s, b0, b1, b_s, c0, c1, c_s):
        clear_pads(ref, span)
    folded[...] = sums[span:, :] + came[span:, :]
    unfold(folded, spread, span)

    def build(base, n):
        lane = lanes_of(n, lanes)
        here, padded, slab = pl.ds(base, n), pl.ds(base + PAD, n), pl.ds(aligned(off + base), n)
        s = sums[here, :] + came[here, :]
        a0[padded, :] = s
        a1[padded, :] = gain[slab, :] * s + corr[here, :]
        strip = spread[here, :]
        strip = jnp.where(inside(lane, (HALO, q)), roll(s, HALO), strip)
        strip = jnp.where(inside(lane, (q, 2 * q - HALO)), roll(s, 2 * q - HALO), strip)
        other = roll(gain_s[here, :] * strip + corr_s[here, :], 2 * q)
        a_s[padded, :] = jnp.where(lane < 2 * q, strip, other)

    over_chunks(span, build)
    fine_steps(
        (
            ((a0, b0, c0, b0), top, slope, mob, j0, off),
            ((a1, b1, c1, b1), top, slope, mob, j1, off),
            ((a_s, b_s, c_s, b_s), top_s, slope_s, mob_s, j_s, 0),
        ),
        span,
        work,
    )

    def finish(base, n):
        lane = lanes_of(n, lanes)
        here = pl.ds(base, n)
        at = PAD * (h + p) + base
        padded, slab = pl.ds(aligned(at + PAD), n), pl.ds(aligned(off + at), n)
        strip = b_s[padded, :]
        end0 = merge_edges(b0[padded, :], strip, 0, lane)
        end1 = merge_edges(b1[padded, :], strip, 1, lane)
        end_own[here, :] = jnp.where(h == 0, end0, end1) * 2.0
        end_send[here, :] = jnp.where(h == 0, end1, end0) * 2.0
        g = gain[slab, :]
        change = end0 - g * a0[padded, :]
        corr_out[here, :] = change * 2.0
        d_out[here, :] = jnp.where(last, end1, g * change + end1 - g * a1[padded, :]) * 2.0

    over_chunks(span - 2 * PAD, finish)


def own_start(h, p, rows):
    return aligned(part_start(h, p, rows) + PAD * (h + p))


def stage_kernel(rows, p, chips, gain, d, came, *rest):
    out, passed = rest[-2:]
    tail = rest[0].shape[0] if len(rest) == 3 else 0
    body_rows = d.shape[0] - tail
    h, chip, last = place(chips)
    off = part_start(h, p, rows) if tail else own_start(h, p, rows)
    near, far = chip ^ (1 + p), chip ^ (2 - p)

    def exponent(to, at):
        return to - (at + 1) % chips

    def weight(e, square, fourth):
        value = jnp.where((e & 1) == 1, square, 1.0) * jnp.where(e >= 2, fourth, 1.0)
        return jnp.where(e < 0, 0.0, value)

    def one(here, g):
        square = g * g
        fourth = square * square
        mine, its = d[here, :], came[here, :]
        out[here, :] = (
            weight(exponent(chip, chip), square, fourth) * mine + weight(exponent(chip, near), square, fourth) * its
        )
        passed[here, :] = (
            weight(exponent(far, chip), square, fourth) * mine + weight(exponent(far, near), square, fourth) * its
        )

    over_chunks(body_rows, lambda base, n: one(pl.ds(base, n), gain[pl.ds(aligned(off + base), n), :]))
    if tail:
        one(pl.ds(body_rows, tail), rest[0][...])


def last_kernel(rows, p, chips, sums, came, gain, corr, own, send):
    h, _, _ = place(chips)
    off = own_start(h, p, rows)

    def body(base, n):
        here = pl.ds(base, n)
        new0 = sums[here, :] + came[here, :]
        new1 = gain[pl.ds(aligned(off + base), n), :] * new0 + corr[here, :]
        own[here, :] = jnp.where(h == 0, new0, new1)
        send[here, :] = jnp.where(h == 0, new1, new0)

    over_chunks(sums.shape[0], body)


def put_kernel(half, places, chips, *refs):
    out, sems = refs[-2:]
    h, _, _ = place(chips)
    copies = []
    for i, (other, p) in enumerate(places):
        side = 1 - h if other else h
        to = out.at[pl.ds(aligned(side * half + p * (half // 2)), half // 2), :]
        copies.append(pltpu.make_async_copy(refs[i], to, sems.at[i]))
        copies[-1].start()
    for copy in copies:
        copy.wait()


def put(half, places, chips, parts, into=None):
    anywhere = pl.BlockSpec(memory_space=pl.ANY)
    count = len(parts)
    return pl.pallas_call(
        functools.partial(put_kernel, half, places, chips),
        out_shape=jax.ShapeDtypeStruct((2 * half, parts[0].shape[1]), jnp.float32),
        in_specs=[VMEM] * count + ([anywhere] if into is not None else []),
        out_specs=anywhere,
        scratch_shapes=[pltpu.SemaphoreType.DMA((count,))],
        input_output_aliases={count: 0} if into is not None else {},
        compiler_params=PARAMS,
        cost_estimate=pl.CostEstimate(flops=0, bytes_accessed=count * parts[0].size * 8, transcendentals=0),
    )(*parts, *(() if into is None else (into,)))


def call(kernel, outs, scratch=(), cost=None):
    def run(*operands):
        return pl.pallas_call(
            kernel,
            out_shape=[jax.ShapeDtypeStruct(shape, jnp.float32) for shape in outs],
            in_specs=[VMEM] * len(operands),
            out_specs=[VMEM] * len(outs),
            scratch_shapes=[pltpu.VMEM(shape, jnp.float32) for shape in scratch],
            compiler_params=PARAMS,
            cost_estimate=cost,
        )(*operands)

    return run


def scan_plan(chips):
    levels = chips.bit_length() - 1
    every = range(chips)
    end = chips - 1
    own = [end if c == end else -1 for c in every]
    rising = []
    for b in range(levels):
        size = 1 << b
        into, keep, came = [], [], []
        for c in every:
            closes = (c >> (b + 1)) == (end >> (b + 1))
            if c & size:
                into.append(c % size)
                keep.append(0)
                came.append(-1 if closes else size)
            else:
                into.append(c if closes else -1)
                keep.append(-1 if closes else size)
                came.append(0)
        rising.append((b, into, keep, came))
    if levels != 2:
        return own, (rising, rising)

    def weight(to, at):
        return max(to - (at + 1) % chips, -1)

    both = []
    for one, two in ((1, 2), (2, 1)):
        first = [[weight(c, c ^ one) for c in every], [weight(c ^ two, c) for c in every]]
        first.append([weight(c ^ two, c ^ one) for c in every])
        both.append([(one.bit_length() - 1, *first), (two.bit_length() - 1,)])
    return own, tuple(both)


def power(square, exponents, chip):
    e = jnp.asarray(np.array(exponents, np.int32))[chip]
    value, factor = jnp.ones_like(square), square
    for k in range(max(max(exponents), 0).bit_length()):
        value = jnp.where((e >> k) & 1 == 1, value * factor, value)
        factor = factor * factor
    return jnp.where(e < 0, jnp.float32(0.0), value)


def exchange(value, bit, count):
    return lax.ppermute(value, "tm", [(i, i ^ (2 << bit)) for i in range(count)])


def scan(parts, gain, folds, rows, h, chip, chips, count):
    own, orders = scan_plan(chips)
    if len(orders[0]) == 2:
        arrived = [exchange(d, order[0][0], count) for d, order in zip(parts, orders)]
        arrived = [lax.optimization_barrier((r, parts[1 - p]))[0] for p, r in enumerate(arrived)]
        mid = [
            call(functools.partial(stage_kernel, rows, p, chips), (d.shape, d.shape))(gain, d, r, *fold)
            for p, (d, r, fold) in enumerate(zip(parts, arrived, folds))
        ]
        came = [exchange(passed, order[1][0], count) for (_, passed), order in zip(mid, orders)]
        return [out for out, _ in mid], came
    squares = []
    for p, (d, fold) in enumerate(zip(parts, folds)):
        plain = d.shape[0] - sum(f.shape[0] for f in fold)
        off = PAD * h + p * ((rows - 2 * PAD) // 2 - PAD)
        if not fold:
            off = off + PAD * (h + p)
        g = jnp.concatenate([lax.dynamic_slice(gain, (off, 0), (plain, d.shape[1])), *fold], axis=0)
        squares.append(g * g)
    sums = [power(sq, own, chip) * d for sq, d in zip(squares, parts)]
    passed = list(parts)
    for stage in range(len(orders[0])):
        arrived = [exchange(d, order[stage][0], count) for d, order in zip(passed, orders)]
        for p, order in enumerate(orders):
            _, into, keep, came = order[stage]
            sums[p] = sums[p] + power(squares[p], into, chip) * arrived[p]
            passed[p] = power(squares[p], keep, chip) * passed[p] + power(squares[p], came, chip) * arrived[p]
    return sums, [jnp.zeros_like(x) for x in sums]


def local(initial_starts, source, region, base_reluctivity, saturation, mobility):
    potential, driver = initial_starts[0], source[0]
    radial, lanes = potential.shape
    count = lax.axis_size("tm")
    chips = count // 2
    spaces = lax.axis_size("space")
    slot = lax.axis_index("tm")
    h, chip = slot % 2, slot // 2
    half = radial // 2
    margin = -(-HALO // 8) * 8
    rows, start = half + margin, half - margin
    table = jnp.concatenate([base_reluctivity, saturation, mobility])
    table = jnp.broadcast_to(table[:, None], (table.shape[0], lanes))
    partner = [(i, i ^ 1) for i in range(count)]
    slab, padded = (rows, lanes), (rows + 2 * PAD, lanes)
    span = half // 2 + 2 * PAD
    tail = 8 * fold_tiles(span)
    part, plain, room = (span + tail, lanes), (span, lanes), (span + 2 * PAD, lanes)
    cost = pl.CostEstimate(flops=240 * rows * lanes, bytes_accessed=40 * rows * lanes, transcendentals=0)

    there = (1 - h) * start
    send = jnp.concatenate(
        [lax.dynamic_slice(x, (there, 0), slab) for x in (potential, driver)], axis=0
    )
    got = lax.ppermute(send, "tm", partner)
    a0, a1, j0, j1, kind, to_west, to_east = call(
        functools.partial(pack_kernel, rows, start, chips), (padded, padded, slab, slab, slab, plain, plain), cost=cost
    )(potential, driver, got, region)
    from_east = lax.ppermute(to_west, "space", [((i + 1) % spaces, i) for i in range(spaces)])
    from_west = lax.ppermute(to_east, "space", [(i, (i + 1) % spaces) for i in range(spaces)])
    f0, f1, top, slope, mob, gain, a_own, j_own, id_own = call(
        functools.partial(main_kernel, rows), (padded, padded) + (slab,) * 7, (padded,) * 12, cost=cost
    )(table, kind, a0, a1, j0, j1)

    sums, strips, folds = [], [], []
    for p in range(2):
        d, *strip = call(
            functools.partial(strip_kernel, rows, span, p, chips),
            (part,) + (plain,) * 7, (room,) * 3 + (plain,) + (room,) * 4, cost=cost,
        )(table, from_west, from_east, a_own, j_own, id_own, a0, a1, f0, f1, gain)
        sums.append(d)
        strips.append(strip)
        folds.append(call(functools.partial(fold_kernel, span), ((tail, lanes),))(strip[5]))
    sums, came = scan(sums, gain, folds, rows, h, chip, chips, count)

    quarter = (half // 2, lanes)
    ends, sums_2, corrs = [], [], []
    for p in range(2):
        corr, corr_s, top_s, slope_s, mob_s, gain_s, j_s = strips[p]
        end_own, end_send, d, change = call(
            functools.partial(second_kernel, rows, span, p, chips),
            (quarter,) * 4, (room,) * 9 + (plain, (tail, lanes)) + (room,) * 12, cost=cost,
        )(sums[p], came[p], corr, corr_s, gain, top, slope, mob, j0, j1, gain_s, top_s, slope_s, mob_s, j_s)
        ends += [end_own, lax.ppermute(end_send, "tm", partner)]
        sums_2.append(d)
        corrs.append(change)
    places = ((0, 0), (1, 0), (0, 1), (1, 1))
    sums, came = scan(sums_2, gain, [(), ()], rows, h, chip, chips, count)
    ends = put(half, places, chips, ends)
    starts = None
    for p in range(2):
        change = corrs[p]
        if p == 1:
            change, ends, starts = lax.optimization_barrier((change, ends, starts))
        new_own, new_send = call(functools.partial(last_kernel, rows, p, chips), (quarter, quarter))(
            sums[p], came[p], gain, change
        )
        new_got = lax.ppermute(new_send, "tm", partner)
        starts = put(half, places[2 * p : 2 * p + 2], chips, (new_own, new_got), starts)
    return (starts[None], ends[None])


def solution(mesh):
    placed = (P("tm", None, "space"), P("tm", None, "space"), P(None, "space"), P(), P(), P())
    return jax.shard_map(
        local,
        mesh=mesh,
        in_specs=placed,
        out_specs=(P("tm", None, "space"), P("tm", None, "space")),
        check_vma=False,
    )
```

time: 53.6 us -> 51.8 us (0.966)
  waiting for transfers between devices: 9.43 us -> 18.8 us
  Pallas kernels: 23.8 us -> 16.1 us
  starting transfers between devices: 16.8 us -> 14.6 us
  local copies, waits for them, and re-layouts: 2.52 us -> 1.24 us
    ppermute x8, waiting for transfers between devices: 7.32 us -> 13.3 us  [exchange(): return lax.ppermute(value, 'tm', [(i, i ^ 2 << bit) for i in range(count)])]
    pallas_call x12 -> x14, Pallas kernels: 19.9 us -> 13.9 us  [run(): pl.pallas_call(kernel, out_shape=[jax.ShapeDtypeStruct(shape, jnp.float32...]
    ppermute x8, starting transfers between devices: 10.5 us -> 8.27 us  [exchange(): return lax.ppermute(value, 'tm', [(i, i ^ 2 << bit) for i in range(count)])]
    pallas_call x3, Pallas kernels: 3.89 us -> 2.26 us  [put(): pl.pallas_call(functools.partial(put_kernel, half, places, chips), out_sh...]
    ppermute x2, waiting for transfers between devices: 0.01 us -> 1.34 us  [local(): new_got = lax.ppermute(new_send, 'tm', partner)]
    ppermute x1, waiting for transfers between devices: 0.01 us -> 0.71 us  [local(): lax.ppermute(to_east, 'space', [(i, (i + 1) % spaces) for i in range(spac...]
    ppermute x1, waiting for transfers between devices: 0.87 us -> 1.56 us  [local(): got = lax.ppermute(send, 'tm', partner)]
    squeeze x1 -> x0, local copies, waits for them, and re-layouts: 0.69 us -> none  [local(): lax.dynamic_index_in_dim(jnp.asarray(np.array(table, np.int32)), slot, ke...]
  transfers between devices with their start and end apart: 15 -> 15, of which waited for: 7 -> 12; matrix products, arithmetic and copies ran while one was open for 1% -> 0% of each run, Pallas kernels for 33% -> 25%
where the time goes in v4:
time: 51.8 us; the launch traced here: 51.7 us
  waiting for transfers between devices  18.8 us (36%)
  Pallas kernels  16.1 us (31%)
  starting transfers between devices  14.6 us (28%)
  local copies, waits for them, and re-layouts  1.24 us (2%)
  between operations  0.82 us (2%)
    pallas_call x14, Pallas kernels, run(): pl.pallas_call(kernel, out_shape=[jax.ShapeDtypeStruct(shape, jnp.float32...  13.9 us
    ppermute x8, waiting for transfers between devices, exchange(): return lax.ppermute(value, 'tm', [(i, i ^ 2 << bit) for i in range(count)])  13.3 us
    ppermute x8, starting transfers between devices, exchange(): return lax.ppermute(value, 'tm', [(i, i ^ 2 << bit) for i in range(count)])  8.27 us
    ppermute x1, starting transfers between devices, local(): lax.ppermute(to_east, 'space', [(i, (i + 1) % spaces) for i in range(spac...  2.99 us
    pallas_call x3, Pallas kernels, put(): pl.pallas_call(functools.partial(put_kernel, half, places, chips), out_sh...  2.26 us
    ppermute x1, starting transfers between devices, local(): lax.ppermute(to_west, 'space', [((i + 1) % spaces, i) for i in range(spac...  2.09 us
    ppermute x1, waiting for transfers between devices, local(): lax.ppermute(to_west, 'space', [((i + 1) % spaces, i) for i in range(spac...  1.83 us
    ppermute x1, waiting for transfers between devices, local(): got = lax.ppermute(send, 'tm', partner)  1.56 us
  transfers between devices with their start and end apart: 15, of which 12 were waited for; matrix products, arithmetic and copies ran while one was open for 0% of the time, Pallas kernels for 25%

profile of v4, /device:TPU:0, one launch (start us, length us, event | category | flops | bytes accessed | tf_op | source)
XLA Modules:
  0.0 51.7 jit_solution(1000791036075778806)
XLA Ops:
  0.7 1.1 %dynamic-slice_bitcast_fusion = (f32[528,128]{1,0:T(8,128)S(1)}, f32[528,128]{1,0:T(8,128)S(1)}) fusion(f32[1,1024,128]{2,1,0:T(8,128)} %param.7, s32[]{:T(128)S(6)} %select_n.12, f32[1,1024,128]{2,1,0:T(8,128)} %param.6), kind=kLoop, calls=%fused_computation.1 | loop fusion | bytes 1081348 | tf_op jit(solution)/shard_map/dynamic_slice | solution.py:569
  2.4 1.6 %collective-permute-done.got = f32[1056,128]{1,0:T(8,128)S(1)} collective-permute-done((f32[1056,128]{1,0:T(8,128)S(1)}, f32[1056,128]{1,0:T(8,128)S(1)}, u32[]{:S(2)}, u32[]{:S(2)}) %collective-permute-start) | collective-permute-done | bytes 540704 | tf_op jit(solution)/shard_map/ppermute | solution.py:571
  4.0 0.8 %shard_map.77 = (f32[544,128]{1,0:T(8,128)S(1)}, f32[544,128]{1,0:T(8,128)S(1)}, f32[528,128]{1,0:T(8,128)S(1)}, f32[528,128]{1,0:T(8,128)S(1)}, f32[528,128]{1,...) custom-call(f32[1024,128]{1,0:T(8,128)S(1)} %bitcast.8, f32[1024,128]{1,0:T(8,128)S(1)} %bitcast.9, ...), custom_call_target="tpu_custom_call" | custom-call | flops 16220160 | bytes 2703360 | tf_op jit(solution)/shard_map/pallas_call | solution.py:457
  4.8 3.0 %collective-permute-start.1 = (f32[272,128]{1,0:T(8,128)S(1)}, f32[272,128]{1,0:T(8,128)S(1)}, u32[]{:S(2)}, u32[]{:S(2)}) collective-permute-start(f32[272,128]{1,0:T(8,128)S(1)} %get-tuple-element.67), channel_id=1, source_target_pairs={{0,1},{1,2},{2,3},{3,0},{4,5},{5,6},{6,7},{7,4},{8,9},{9,10},{10,1... | collective-permute-start | bytes 417800 | tf_op jit(solution)/shard_map/ppermute | solution.py:576
  7.8 2.1 %collective-permute-start.2 = (f32[272,128]{1,0:T(8,128)S(1)}, f32[272,128]{1,0:T(8,128)S(1)}, u32[]{:S(2)}, u32[]{:S(2)}) collective-permute-start(f32[272,128]{1,0:T(8,128)S(1)} %get-tuple-element.68), channel_id=1, source_target_pairs={{1,0},{2,1},{3,2},{0,3},{5,4},{6,5},{7,6},{4,7},{9,8},{10,9},{11,1... | collective-permute-start | bytes 417800 | tf_op jit(solution)/shard_map/ppermute | solution.py:575
  10.1 3.6 %shard_map.78 = (f32[544,128]{1,0:T(8,128)S(1)}, f32[544,128]{1,0:T(8,128)S(1)}, f32[528,128]{1,0:T(8,128)S(1)}, f32[528,128]{1,0:T(8,128)S(1)}, f32[528,128]{1,...) custom-call(f32[24,128]{1,0:T(8,128)S(1)} %broadcast_in_dim.12.table, ...), custom_call_target="tpu_custom_call" | custom-call | flops 16220160 | bytes 2703360 | tf_op jit(solution)/shard_map/pallas_call | solution.py:457
  14.4 1.8 %collective-permute-done.2.east = f32[272,128]{1,0:T(8,128)S(1)} collective-permute-done((f32[272,128]{1,0:T(8,128)S(1)}, f32[272,128]{1,0:T(8,128)S(1)}, u32[]{:S(2)}, u32[]{:S(2)}) %collective-permute-start.2) | collective-permute-done | bytes 139296 | tf_op jit(solution)/shard_map/ppermute | solution.py:575
  16.2 1.8 %shard_map.80 = (f32[312,128]{1,0:T(8,128)S(1)}, f32[272,128]{1,0:T(8,128)S(1)}, f32[272,128]{1,0:T(8,128)S(1)}, f32[272,128]{1,0:T(8,128)S(1)}, f32[272,128]{1,...) custom-call(f32[24,128]{1,0:T(8,128)S(1)} %broadcast_in_dim.12.table, ...), custom_call_target="tpu_custom_call" | custom-call | flops 16220160 | bytes 2703360 | tf_op jit(solution)/shard_map/pallas_call | solution.py:457
  18.0 1.6 %collective-permute-start.6 = (f32[312,128]{1,0:T(8,128)S(1)}, f32[312,128]{1,0:T(8,128)S(1)}, u32[]{:S(2)}, u32[]{:S(2)}) collective-permute-start(f32[312,128]{1,0:T(8,128)S(1)} %get-tuple-element.75.d), channel_id=1, source_target_pairs={{0,8},{4,12},{8,0},{12,4},{16,24},{20,28},{24,16},{28,20},{1,9},{5... | collective-permute-start | bytes 479240 | tf_op jit(solution)/shard_map/ppermute | solution.py:514
  19.6 1.9 %shard_map.79 = (f32[312,128]{1,0:T(8,128)S(1)}, f32[272,128]{1,0:T(8,128)S(1)}, f32[272,128]{1,0:T(8,128)S(1)}, f32[272,128]{1,0:T(8,128)S(1)}, f32[272,128]{1,...) custom-call(f32[24,128]{1,0:T(8,128)S(1)} %broadcast_in_dim.12.table, ...), custom_call_target="tpu_custom_call" | custom-call | flops 16220160 | bytes 2703360 | tf_op jit(solution)/shard_map/pallas_call | solution.py:457
  21.5 1.6 %collective-permute-start.3 = (f32[312,128]{1,0:T(8,128)S(1)}, f32[312,128]{1,0:T(8,128)S(1)}, u32[]{:S(2)}, u32[]{:S(2)}) collective-permute-start(f32[312,128]{1,0:T(8,128)S(1)} %get-tuple-element.74.d), channel_id=1, source_target_pairs={{0,16},{4,20},{8,24},{12,28},{16,0},{20,4},{24,8},{28,12},{1,17},{... | collective-permute-start | bytes 479240 | tf_op jit(solution)/shard_map/ppermute | solution.py:514
  23.7 1.6 %collective-permute-start.7 = (f32[312,128]{1,0:T(8,128)S(1)}, f32[312,128]{1,0:T(8,128)S(1)}, u32[]{:S(2)}, u32[]{:S(2)}) collective-permute-start(f32[312,128]{1,0:T(8,128)S(1)} %get-tuple-element.93), channel_id=1, source_target_pairs={{0,16},{4,20},{8,24},{12,28},{16,0},{20,4},{24,8},{28,12},{1,17},{... | collective-permute-start | bytes 479240 | tf_op jit(solution)/shard_map/ppermute | solution.py:514
  25.4 3.0 %collective-permute-done.3.came = f32[312,128]{1,0:T(8,128)S(1)} collective-permute-done((f32[312,128]{1,0:T(8,128)S(1)}, f32[312,128]{1,0:T(8,128)S(1)}, u32[]{:S(2)}, u32[]{:S(2)}) %collective-permute-start.3) | collective-permute-done | bytes 159776 | tf_op jit(solution)/shard_map/ppermute | solution.py:514
  28.7 1.5 %collective-permute-done.7.came = f32[312,128]{1,0:T(8,128)S(1)} collective-permute-done((f32[312,128]{1,0:T(8,128)S(1)}, f32[312,128]{1,0:T(8,128)S(1)}, u32[]{:S(2)}, u32[]{:S(2)}) %collective-permute-start.7) | collective-permute-done | bytes 159776 | tf_op jit(solution)/shard_map/ppermute | solution.py:514
  30.2 2.5 %shard_map.86 = (f32[256,128]{1,0:T(8,128)S(1)}, f32[256,128]{1,0:T(8,128)S(1)}, f32[256,128]{1,0:T(8,128)S(1)}, f32[256,128]{1,0:T(8,128)S(1)}) custom-call(f32[312,128]{1,0:T(8,128)S(1)} %get-tuple-element.92.sums, f32[312,128]{1,0:T(8,128)S(1)} %collective-permute-done.7.came, f32[272,128]{1,0:T(8,128)S(1)} %get-tuple-element.94.corr, ...), custom_call_target="tpu_custom_call" | custom-call | flops 16220160 | bytes 2703360 | tf_op jit(solution)/shard_map/pallas_call | solution.py:457
  33.3 0.9 %collective-permute-done.4.came = f32[312,128]{1,0:T(8,128)S(1)} collective-permute-done((f32[312,128]{1,0:T(8,128)S(1)}, f32[312,128]{1,0:T(8,128)S(1)}, u32[]{:S(2)}, u32[]{:S(2)}) %collective-permute-start.4) | collective-permute-done | bytes 159776 | tf_op jit(solution)/shard_map/ppermute | solution.py:514
  34.3 2.5 %shard_map.83 = (f32[256,128]{1,0:T(8,128)S(1)}, f32[256,128]{1,0:T(8,128)S(1)}, f32[256,128]{1,0:T(8,128)S(1)}, f32[256,128]{1,0:T(8,128)S(1)}) custom-call(f32[312,128]{1,0:T(8,128)S(1)} %get-tuple-element.78.sums, f32[312,128]{1,0:T(8,128)S(1)} %collective-permute-done.4.came, f32[272,128]{1,0:T(8,128)S(1)} %get-tuple-element.80.corr, ...), custom_call_target="tpu_custom_call" | custom-call | flops 16220160 | bytes 2703360 | tf_op jit(solution)/shard_map/pallas_call | solution.py:457
  36.7 0.9 %collective-permute-done.11.came = f32[256,128]{1,0:T(8,128)S(1)} collective-permute-done((f32[256,128]{1,0:T(8,128)S(1)}, f32[256,128]{1,0:T(8,128)S(1)}, u32[]{:S(2)}, u32[]{:S(2)}) %collective-permute-start.11) | collective-permute-done | bytes 131104 | tf_op jit(solution)/shard_map/ppermute | solution.py:514
  37.8 1.6 %collective-permute-start.12 = (f32[256,128]{1,0:T(8,128)S(1)}, f32[256,128]{1,0:T(8,128)S(1)}, u32[]{:S(2)}, u32[]{:S(2)}) collective-permute-start(f32[256,128]{1,0:T(8,128)S(1)} %get-tuple-element.111), channel_id=1, source_target_pairs={{0,16},{4,20},{8,24},{12,28},{16,0},{20,4},{24,8},{28,12},{1,17},{... | collective-permute-start | bytes 393224 | tf_op jit(solution)/shard_map/ppermute | solution.py:514
  40.4 2.4 %collective-permute-done.12.came = f32[256,128]{1,0:T(8,128)S(1)} collective-permute-done((f32[256,128]{1,0:T(8,128)S(1)}, f32[256,128]{1,0:T(8,128)S(1)}, u32[]{:S(2)}, u32[]{:S(2)}) %collective-permute-start.12) | collective-permute-done | bytes 131104 | tf_op jit(solution)/shard_map/ppermute | solution.py:514
  42.9 1.4 %collective-permute-done.5.came = f32[256,128]{1,0:T(8,128)S(1)} collective-permute-done((f32[256,128]{1,0:T(8,128)S(1)}, f32[256,128]{1,0:T(8,128)S(1)}, u32[]{:S(2)}, u32[]{:S(2)}) %collective-permute-start.5) | collective-permute-done | bytes 131104 | tf_op jit(solution)/shard_map/ppermute | solution.py:514
  45.1 0.8 %shard_map.88 = f32[1024,128]{1,0:T(8,128)} custom-call(f32[256,128]{1,0:T(8,128)S(1)} %get-tuple-element.105.refs_0_, f32[256,128]{1,0:T(8,128)S(1)} %collective-permute-done.9.refs_1_, f32[256,128]{1,0:T(8,128)S(1)} %get-tuple-element.107.refs_2_, f32[256,128]{1,0:T(8,128)S(1)} %collective-permute-done.10.refs_3_), custom_call_target="tpu_custom_call" | custom-call | bytes 1048576 | tf_op jit(solution)/shard_map/pallas_call | solution.py:443
  46.7 2.8 %collective-permute-done.8.came = f32[256,128]{1,0:T(8,128)S(1)} collective-permute-done((f32[256,128]{1,0:T(8,128)S(1)}, f32[256,128]{1,0:T(8,128)S(1)}, u32[]{:S(2)}, u32[]{:S(2)}) %collective-permute-start.8) | collective-permute-done | bytes 131104 | tf_op jit(solution)/shard_map/ppermute | solution.py:514
  49.6 1.3 %collective-permute-done.14.refs_1_ = f32[256,128]{1,0:T(8,128)S(1)} collective-permute-done((f32[256,128]{1,0:T(8,128)S(1)}, f32[256,128]{1,0:T(8,128)S(1)}, u32[]{:S(2)}, u32[]{:S(2)}) %collective-permute-start.14) | collective-permute-done | bytes 131104 | tf_op jit(solution)/shard_map/ppermute | solution.py:614
  (39 shorter events, 6.7 us)
Async XLA Ops:
  0.6 3.3 %copy-start.2 = (s32[1024,128]{1,0:T(8,128)S(1)}, s32[1024,128]{1,0:T(8,128)}, u32[]{:S(2)}) copy-start(s32[1024,128]{1,0:T(8,128)} %region.1) | copy-start | bytes 1572868
  1.8 2.2 %copy-start = (f32[1,1024,128]{2,1,0:T(8,128)S(1)}, f32[1,1024,128]{2,1,0:T(8,128)}, u32[]{:S(2)}) copy-start(f32[1,1024,128]{2,1,0:T(8,128)} %param.6) | copy-start | bytes 1572868
  1.8 2.2 %copy-start.1 = (f32[1,1024,128]{2,1,0:T(8,128)S(1)}, f32[1,1024,128]{2,1,0:T(8,128)}, u32[]{:S(2)}) copy-start(f32[1,1024,128]{2,1,0:T(8,128)} %param.7) | copy-start | bytes 1572868
  1.9 2.1 %collective-permute-start = (f32[1056,128]{1,0:T(8,128)S(1)}, f32[1056,128]{1,0:T(8,128)S(1)}, u32[]{:S(2)}, u32[]{:S(2)}) collective-permute-start(f32[1056,128]{1,0:T(8,128)S(1)} %pad_maximum_fusion), channel_id=1, source_target_pairs={{0,4},{4,0},{8,12},{12,8},{16,20},{20,16},{24,28},{28,24},{1,5},{5... | collective-permute-start | bytes 1622024 | tf_op jit(solution)/shard_map/ppermute | solution.py:571
  4.8 5.1 %copy-start.3 = (f32[8]{0:T(128)S(1)}, f32[8]{0:T(128)}, u32[]{:S(2)}) copy-start(f32[8]{0:T(128)} %param.11) | copy-start | bytes 100
  4.8 5.1 %copy-start.4 = (f32[8]{0:T(128)S(1)}, f32[8]{0:T(128)}, u32[]{:S(2)}) copy-start(f32[8]{0:T(128)} %param.10) | copy-start | bytes 100
  4.8 5.1 %copy-start.5 = (f32[8]{0:T(128)S(1)}, f32[8]{0:T(128)}, u32[]{:S(2)}) copy-start(f32[8]{0:T(128)} %param.9) | copy-start | bytes 100
  4.8 9.6 %collective-permute-start.1 = (f32[272,128]{1,0:T(8,128)S(1)}, f32[272,128]{1,0:T(8,128)S(1)}, u32[]{:S(2)}, u32[]{:S(2)}) collective-permute-start(f32[272,128]{1,0:T(8,128)S(1)} %get-tuple-element.67), channel_id=1, source_target_pairs={{0,1},{1,2},{2,3},{3,0},{4,5},{5,6},{6,7},{7,4},{8,9},{9,10},{10,1... | collective-permute-start | bytes 417800 | tf_op jit(solution)/shard_map/ppermute | solution.py:576
  7.8 8.4 %collective-permute-start.2 = (f32[272,128]{1,0:T(8,128)S(1)}, f32[272,128]{1,0:T(8,128)S(1)}, u32[]{:S(2)}, u32[]{:S(2)}) collective-permute-start(f32[272,128]{1,0:T(8,128)S(1)} %get-tuple-element.68), channel_id=1, source_target_pairs={{1,0},{2,1},{3,2},{0,3},{5,4},{6,5},{7,6},{4,7},{9,8},{10,9},{11,1... | collective-permute-start | bytes 417800 | tf_op jit(solution)/shard_map/ppermute | solution.py:575
  18.0 5.5 %collective-permute-start.6 = (f32[312,128]{1,0:T(8,128)S(1)}, f32[312,128]{1,0:T(8,128)S(1)}, u32[]{:S(2)}, u32[]{:S(2)}) collective-permute-start(f32[312,128]{1,0:T(8,128)S(1)} %get-tuple-element.75.d), channel_id=1, source_target_pairs={{0,8},{4,12},{8,0},{12,4},{16,24},{20,28},{24,16},{28,20},{1,9},{5... | collective-permute-start | bytes 479240 | tf_op jit(solution)/shard_map/ppermute | solution.py:514
  21.5 7.0 %collective-permute-start.3 = (f32[312,128]{1,0:T(8,128)S(1)}, f32[312,128]{1,0:T(8,128)S(1)}, u32[]{:S(2)}, u32[]{:S(2)}) collective-permute-start(f32[312,128]{1,0:T(8,128)S(1)} %get-tuple-element.74.d), channel_id=1, source_target_pairs={{0,16},{4,20},{8,24},{12,28},{16,0},{20,4},{24,8},{28,12},{1,17},{... | collective-permute-start | bytes 479240 | tf_op jit(solution)/shard_map/ppermute | solution.py:514
  23.7 6.5 %collective-permute-start.7 = (f32[312,128]{1,0:T(8,128)S(1)}, f32[312,128]{1,0:T(8,128)S(1)}, u32[]{:S(2)}, u32[]{:S(2)}) collective-permute-start(f32[312,128]{1,0:T(8,128)S(1)} %get-tuple-element.93), channel_id=1, source_target_pairs={{0,16},{4,20},{8,24},{12,28},{16,0},{20,4},{24,8},{28,12},{1,17},{... | collective-permute-start | bytes 479240 | tf_op jit(solution)/shard_map/ppermute | solution.py:514
  28.6 5.7 %collective-permute-start.4 = (f32[312,128]{1,0:T(8,128)S(1)}, f32[312,128]{1,0:T(8,128)S(1)}, u32[]{:S(2)}, u32[]{:S(2)}) collective-permute-start(f32[312,128]{1,0:T(8,128)S(1)} %get-tuple-element.79), channel_id=1, source_target_pairs={{0,8},{4,12},{8,0},{12,4},{16,24},{20,28},{24,16},{28,20},{1,9},{5... | collective-permute-start | bytes 479240 | tf_op jit(solution)/shard_map/ppermute | solution.py:514
  32.6 5.0 %collective-permute-start.11 = (f32[256,128]{1,0:T(8,128)S(1)}, f32[256,128]{1,0:T(8,128)S(1)}, u32[]{:S(2)}, u32[]{:S(2)}) collective-permute-start(f32[256,128]{1,0:T(8,128)S(1)} %get-tuple-element.100.d), channel_id=1, source_target_pairs={{0,8},{4,12},{8,0},{12,4},{16,24},{20,28},{24,16},{28,20},{1,9},{5... | collective-permute-start | bytes 393224 | tf_op jit(solution)/shard_map/ppermute | solution.py:514
  37.8 5.0 %collective-permute-start.12 = (f32[256,128]{1,0:T(8,128)S(1)}, f32[256,128]{1,0:T(8,128)S(1)}, u32[]{:S(2)}, u32[]{:S(2)}) collective-permute-start(f32[256,128]{1,0:T(8,128)S(1)} %get-tuple-element.111), channel_id=1, source_target_pairs={{0,16},{4,20},{8,24},{12,28},{16,0},{20,4},{24,8},{28,12},{1,17},{... | collective-permute-start | bytes 393224 | tf_op jit(solution)/shard_map/ppermute | solution.py:514
  39.4 5.0 %collective-permute-start.5 = (f32[256,128]{1,0:T(8,128)S(1)}, f32[256,128]{1,0:T(8,128)S(1)}, u32[]{:S(2)}, u32[]{:S(2)}) collective-permute-start(f32[256,128]{1,0:T(8,128)S(1)} %get-tuple-element.89.d), channel_id=1, source_target_pairs={{0,16},{4,20},{8,24},{12,28},{16,0},{20,4},{24,8},{28,12},{1,17},{... | collective-permute-start | bytes 393224 | tf_op jit(solution)/shard_map/ppermute | solution.py:514
  39.9 5.3 %collective-permute-start.9 = (f32[256,128]{1,0:T(8,128)S(1)}, f32[256,128]{1,0:T(8,128)S(1)}, u32[]{:S(2)}, u32[]{:S(2)}) collective-permute-start(f32[256,128]{1,0:T(8,128)S(1)} %get-tuple-element.106), channel_id=1, source_target_pairs={{0,4},{4,0},{8,12},{12,8},{16,20},{20,16},{24,28},{28,24},{1,5},{5... | collective-permute-start | bytes 393224 | tf_op jit(solution)/shard_map/ppermute | solution.py:600
  39.9 5.3 %collective-permute-start.10 = (f32[256,128]{1,0:T(8,128)S(1)}, f32[256,128]{1,0:T(8,128)S(1)}, u32[]{:S(2)}, u32[]{:S(2)}) collective-permute-start(f32[256,128]{1,0:T(8,128)S(1)} %get-tuple-element.108), channel_id=1, source_target_pairs={{0,4},{4,0},{8,12},{12,8},{16,20},{20,16},{24,28},{28,24},{1,5},{5... | collective-permute-start | bytes 393224 | tf_op jit(solution)/shard_map/ppermute | solution.py:600
  42.9 3.1 %collective-permute-start.13 = (f32[256,128]{1,0:T(8,128)S(1)}, f32[256,128]{1,0:T(8,128)S(1)}, u32[]{:S(2)}, u32[]{:S(2)}) collective-permute-start(f32[256,128]{1,0:T(8,128)S(1)} %get-tuple-element.114), channel_id=1, source_target_pairs={{0,4},{4,0},{8,12},{12,8},{16,20},{20,16},{24,28},{28,24},{1,5},{5... | collective-permute-start | bytes 393224 | tf_op jit(solution)/shard_map/ppermute | solution.py:614
  44.4 5.0 %collective-permute-start.8 = (f32[256,128]{1,0:T(8,128)S(1)}, f32[256,128]{1,0:T(8,128)S(1)}, u32[]{:S(2)}, u32[]{:S(2)}) collective-permute-start(f32[256,128]{1,0:T(8,128)S(1)} %get-tuple-element.103), channel_id=1, source_target_pairs={{0,8},{4,12},{8,0},{12,4},{16,24},{20,28},{24,16},{28,20},{1,9},{5... | collective-permute-start | bytes 393224 | tf_op jit(solution)/shard_map/ppermute | solution.py:514
  49.5 1.4 %collective-permute-start.14 = (f32[256,128]{1,0:T(8,128)S(1)}, f32[256,128]{1,0:T(8,128)S(1)}, u32[]{:S(2)}, u32[]{:S(2)}) collective-permute-start(f32[256,128]{1,0:T(8,128)S(1)} %get-tuple-element.117), channel_id=1, source_target_pairs={{0,4},{4,0},{8,12},{12,8},{16,20},{20,16},{24,28},{28,24},{1,5},{5... | collective-permute-start | bytes 393224 | tf_op jit(solution)/shard_map/ppermute | solution.py:614
